TPU v7x, 32 devices: a whole 2x2x4 slice. The times are simulated.
32 devices in a mesh: rows: 16 (over z, y, core), cols: 2 (over x).
Axes of the slice: x: 2, y: 2, z: 4, core: 2. Of those that a mesh axis runs over, the one named last changes fastest.
Arguments:
- phi_start: float32 [256, 192, 384], P('rows', 'cols'), may hold values from -12 to 12
- source: float32 [256, 192, 384], P('rows', 'cols'), may hold values from -18 to 18
- owner_voxel: int32 [24576], P(('rows', 'cols')), may hold values from 0 to 589823, as said below
- column_slot: int32 [24576], replicated, may hold values from 0 to 24575, each once
- layer_matrix: float32 [1536, 24576], P('rows', 'cols'), may hold values from -0.0390625 to 0.0390625
Outputs:
- potential: float32 [256, 192, 384], P('rows', 'cols')
- boundary_phi: float32 [1536], P(('rows', 'cols'))
Inputs may be any that keep to these rules, and one draw needn't show every extreme that they name: `owner_voxel`: offsets index the 16 x 96 x 384 block of the device that owns the slot, in row-major order.
All inputs are finite; a program needn't handle non-finite values.
Results may differ from a plain program's by a relative error of at most 0.00011.
Values sent between devices are 32-bit elements; how exact they have to be, the bound alone decides.
No kernel may reach another device: no remote copies, remote signals or barrier semaphores. Data moves between devices by JAX's collectives and lax.ppermute only.
A program may use at most 128 MiB of HBM per device.

v0:
```python
import jax
import jax.numpy as jnp
from jax import lax
from jax.sharding import PartitionSpec as P

ITERS = 4


def with_halo(value, sides, width):
    for axis, dim in sides:
        size, length = (lax.axis_size(axis), value.shape[dim])
        up = [(i, (i + 1) % size) for i in range(size - 1)]
        down = [(j, i) for i, j in up]
        last = lax.slice_in_dim(value, length - width, length, axis=dim)
        first = lax.slice_in_dim(value, 0, width, axis=dim)
        before = lax.ppermute(last, axis, up)
        after = lax.ppermute(first, axis, down)
        value = jnp.concatenate([before, value, after], axis=dim)
    return value


def neighbour_sum(padded):
    padded = jnp.pad(padded, ((0, 0), (0, 0), (1, 1)))
    neighbours = padded[2:, 1:-1, 1:-1] + padded[:-2, 1:-1, 1:-1]
    neighbours = neighbours + padded[1:-1, 2:, 1:-1] + padded[1:-1, :-2, 1:-1]
    neighbours = neighbours + padded[1:-1, 1:-1, 2:] + padded[1:-1, 1:-1, :-2]
    return neighbours


def local(phi_start, source, owner_voxel, column_slot, layer_matrix):
    potential = phi_start
    for sweep_index in range(ITERS):
        padded = with_halo(potential, (("rows", 0), ("cols", 1)), 1)
        potential = (source + neighbour_sum(padded)) / 6.0
    node_values = potential.reshape(-1)[owner_voxel]
    col_count = lax.axis_size("cols")
    col_index = lax.axis_index("cols")
    node_total = column_slot.shape[0]
    block_len = node_total // col_count
    block_slots = lax.dynamic_slice_in_dim(column_slot, col_index * block_len, block_len, 0)
    gathered = lax.all_gather(node_values, ("rows", "cols"), axis=0, tiled=True)
    trace_block = gathered[block_slots]
    boundary_phi = lax.psum_scatter(
        jnp.dot(
            layer_matrix,
            trace_block,
            precision=lax.Precision.HIGHEST,
            preferred_element_type=jnp.float32,
        ),
        "cols",
        scatter_dimension=0,
        tiled=True,
    )
    return (potential, boundary_phi)


def solution(mesh):
    return jax.shard_map(
        local,
        mesh=mesh,
        in_specs=(
            P("rows", "cols", None),
            P("rows", "cols", None),
            P(("rows", "cols")),
            P(),
            P("rows", "cols"),
        ),
        out_specs=(P("rows", "cols", None), P(("rows", "cols"))),
        check_vma=False,
    )
```

profile of v0, /device:TPU:0, one launch (start us, length us, event | category | flops | bytes accessed | tf_op | source)
XLA Modules:
  0.0 251.6 jit_solution(13802172284914870467)
XLA Ops:
  1.6 2.4 collective-permute-start.1
  5.3 1.8 constant_dynamic-update-slice_fusion.1
  7.2 2.2 collective-permute-done
  10.8 4.8 %collective-permute-start.3 = (f32[18,1,384]{2,1,0:T(1,128)S(1)}, f32[18,1,384]{2,1,0:T(1,128)S(1)}, u32[]{:S(2)}, u32[]{:S(2)}) collective-permute-start(f32[18,1,384]{2,1,0:T(1,128)S(1)} %get-tuple-element.8), channel_id=1, source_target_pairs={{0,1},{2,3},{4,5},{6,7},{8,9},{10,11},{12,13},{14,15},{16,17},{18,... | collective-permute-start | bytes 82952 | tf_op jit(solution)/shard_map/ppermute | solution.py:16
  15.6 1.5 collective-permute-done.3
  18.5 3.4 %fusion.17 = f32[16,96,384]{2,1,0:T(8,128)S(1)} fusion(f32[16,96,384]{2,1,0:T(8,128)S(1)} %copy-done.2, f32[18,98,386]{2,1,0:T(8,128)S(1)} %select_maximum_fusion.12, f32[18,96,384]{2,1,0:T(8,128)S(1)} %constant_dynamic-update-slice_fusion, f32[18,1,384]{2,1,0:T(1,128)S(1)} %collective-permute-done.3, f32[18,1,384]{2,1,0:T(1,128)S(1)} %collective-permute-done.2, ...), kind=kLoop, calls=%fused_computation.66 | loop fusion | flops 6488064 | bytes 14800896 | tf_op jit(solution)/shard_map/div | solution.py:34
  23.3 5.1 %collective-permute-start.5 = (f32[1,96,384]{2,1,0:T(8,128)S(1)}, f32[1,96,384]{2,1,0:T(8,128)S(1)}, u32[]{:S(2)}, u32[]{:S(2)}) collective-permute-start(f32[1,96,384]{2,1,0:T(8,128)S(1)} %get-tuple-element.14), channel_id=1, source_target_pairs={{0,2},{2,4},{4,6},{6,8},{8,10},{10,12},{12,14},{14,16},{16,18},{18... | collective-permute-start | bytes 442376 | tf_op jit(solution)/shard_map/ppermute | solution.py:16
  30.7 4.5 %collective-permute-start.7 = (f32[18,1,384]{2,1,0:T(1,128)S(1)}, f32[18,1,384]{2,1,0:T(1,128)S(1)}, u32[]{:S(2)}, u32[]{:S(2)}) collective-permute-start(f32[18,1,384]{2,1,0:T(1,128)S(1)} %get-tuple-element.6), channel_id=1, source_target_pairs={{0,1},{2,3},{4,5},{6,7},{8,9},{10,11},{12,13},{14,15},{16,17},{18,... | collective-permute-start | bytes 82952 | tf_op jit(solution)/shard_map/ppermute | solution.py:16
  36.8 3.3 %select_maximum_fusion.8 = f32[18,98,386]{2,1,0:T(8,128)S(1)} fusion(f32[18,1,384]{2,1,0:T(1,128)S(1)} %collective-permute-done.6, f32[18,1,384]{2,1,0:T(1,128)S(1)} %collective-permute-done.7, f32[1,96,384]{2,1,0:T(8,128)S(1)} %collective-permute-done.4, f32[16,96,384]{2,1,0:T(8,128)S(1)} %fusion.17, f32[1,96,384]{2,1,0:T(8,128)S(1)} %collective-permute-done.5), kind=kLoop, calls=%fused_computation.12 | loop fusion | flops 8170848 | bytes 5433120 | tf_op jit(solution)/shard_map/concatenate | solution.py:18
  40.1 4.2 %fusion.12 = f32[16,96,384]{2,1,0:T(8,128)S(1)} fusion(f32[16,96,384]{2,1,0:T(8,128)S(1)} %copy-done.2, f32[18,98,386]{2,1,0:T(8,128)S(1)} %select_maximum_fusion.8, f32[18,1,384]{2,1,0:T(1,128)S(1)} %collective-permute-done.7, f32[1,96,384]{2,1,0:T(8,128)S(1)} %collective-permute-done.4, f32[16,96,384]{2,1,0:T(8,128)S(1)} %fusion.17, ...), kind=kLoop, calls=%fused_computation.51 | loop fusion | flops 8847360 | bytes 12146688 | tf_op jit(solution)/shard_map/div | solution.py:34
  45.7 5.8 %collective-permute-start.9 = (f32[1,96,384]{2,1,0:T(8,128)S(1)}, f32[1,96,384]{2,1,0:T(8,128)S(1)}, u32[]{:S(2)}, u32[]{:S(2)}) collective-permute-start(f32[1,96,384]{2,1,0:T(8,128)S(1)} %get-tuple-element.12), channel_id=1, source_target_pairs={{0,2},{2,4},{4,6},{6,8},{8,10},{10,12},{12,14},{14,16},{16,18},{18... | collective-permute-start | bytes 442376 | tf_op jit(solution)/shard_map/ppermute | solution.py:16
  53.8 4.5 %collective-permute-start.11 = (f32[18,1,384]{2,1,0:T(1,128)S(1)}, f32[18,1,384]{2,1,0:T(1,128)S(1)}, u32[]{:S(2)}, u32[]{:S(2)}) collective-permute-start(f32[18,1,384]{2,1,0:T(1,128)S(1)} %get-tuple-element.4), channel_id=1, source_target_pairs={{0,1},{2,3},{4,5},{6,7},{8,9},{10,11},{12,13},{14,15},{16,17},{18,... | collective-permute-start | bytes 82952 | tf_op jit(solution)/shard_map/ppermute | solution.py:16
  59.8 3.3 %select_maximum_fusion.4 = f32[18,98,386]{2,1,0:T(8,128)S(1)} fusion(f32[18,1,384]{2,1,0:T(1,128)S(1)} %collective-permute-done.10, f32[18,1,384]{2,1,0:T(1,128)S(1)} %collective-permute-done.11, f32[1,96,384]{2,1,0:T(8,128)S(1)} %collective-permute-done.8, f32[16,96,384]{2,1,0:T(8,128)S(1)} %fusion.12, f32[1,96,384]{2,1,0:T(8,128)S(1)} %collective-permute-done.9), kind=kLoop, calls=%fused_computation.8 | loop fusion | flops 8170848 | bytes 5433120 | tf_op jit(solution)/shard_map/concatenate | solution.py:18
  63.2 4.2 %fusion.7 = f32[16,96,384]{2,1,0:T(8,128)S(1)} fusion(f32[16,96,384]{2,1,0:T(8,128)S(1)} %copy-done.3, f32[18,98,386]{2,1,0:T(8,128)S(1)} %select_maximum_fusion.4, f32[18,1,384]{2,1,0:T(1,128)S(1)} %collective-permute-done.11, f32[1,96,384]{2,1,0:T(8,128)S(1)} %collective-permute-done.8, f32[16,96,384]{2,1,0:T(8,128)S(1)} %fusion.12, ...), kind=kLoop, calls=%fused_computation.36 | loop fusion | flops 8847360 | bytes 12146688 | tf_op jit(solution)/shard_map/div | solution.py:34
  68.9 7.0 %collective-permute-start.13 = (f32[1,96,384]{2,1,0:T(8,128)S(1)}, f32[1,96,384]{2,1,0:T(8,128)S(1)}, u32[]{:S(2)}, u32[]{:S(2)}) collective-permute-start(f32[1,96,384]{2,1,0:T(8,128)S(1)} %get-tuple-element.10), channel_id=1, source_target_pairs={{0,2},{2,4},{4,6},{6,8},{8,10},{10,12},{12,14},{14,16},{16,18},{18... | collective-permute-start | bytes 442376 | tf_op jit(solution)/shard_map/ppermute | solution.py:16
  78.2 4.5 %collective-permute-start.15 = (f32[18,1,384]{2,1,0:T(1,128)S(1)}, f32[18,1,384]{2,1,0:T(1,128)S(1)}, u32[]{:S(2)}, u32[]{:S(2)}) collective-permute-start(f32[18,1,384]{2,1,0:T(1,128)S(1)} %get-tuple-element.2), channel_id=1, source_target_pairs={{0,1},{2,3},{4,5},{6,7},{8,9},{10,11},{12,13},{14,15},{16,17},{18,... | collective-permute-start | bytes 82952 | tf_op jit(solution)/shard_map/ppermute | solution.py:16
  84.3 4.8 %select_maximum_fusion = f32[18,98,386]{2,1,0:T(8,128)S(1)} fusion(f32[18,1,384]{2,1,0:T(1,128)S(1)} %collective-permute-done.14, f32[18,1,384]{2,1,0:T(1,128)S(1)} %collective-permute-done.15, f32[1,96,384]{2,1,0:T(8,128)S(1)} %collective-permute-done.12, f32[16,96,384]{2,1,0:T(8,128)} %copy-done, f32[1,96,384]{2,1,0:T(8,128)S(1)} %collective-permute-done.13), kind=kLoop, calls=%fused_computation.4 | loop fusion | flops 8170848 | bytes 5433120 | tf_op jit(solution)/shard_map/concatenate | solution.py:18
  89.1 5.2 %fusion.2 = f32[16,96,384]{2,1,0:T(8,128)} fusion(f32[16,96,384]{2,1,0:T(8,128)S(1)} %copy-done.4, f32[18,98,386]{2,1,0:T(8,128)S(1)} %select_maximum_fusion, f32[18,1,384]{2,1,0:T(1,128)S(1)} %collective-permute-done.15, f32[1,96,384]{2,1,0:T(8,128)S(1)} %collective-permute-done.12, f32[16,96,384]{2,1,0:T(8,128)S(1)} %copy-done.1, ...), kind=kLoop, calls=%fused_computation.21 | loop fusion | flops 8847360 | bytes 12146688 | tf_op jit(solution)/shard_map/div | solution.py:34
  94.3 2.3 reshape.7
  96.6 4.5 %gather_fusion = f32[768]{0:T(1024)S(1)} fusion(f32[589824]{0:T(1024)S(1)} %reshape.7, s32[1024]{0:T(1024)S(1)} %pad_clamp_fusion), kind=kCustom, calls=%fused_computation | custom fusion | bytes 9216 | tf_op jit(solution)/shard_map/gather | solution.py:35
  101.1 71.4 %all-gather.1 = f32[32,1,768]{2,1,0:T(1,128)S(1)} all-gather(f32[1,1,768]{2,1,0:T(1,128)S(1)} %reshape.27), channel_id=2, replica_groups=mesh['rows'=16,'cols'=2] {'rows','cols'}, dimensions={0}, use_global_device_ids=true | all-gather | bytes 101376 | tf_op jit(solution)/shard_map/all_gather | solution.py:41
  172.5 68.0 %gather_fusion.1 = f32[12288]{0:T(1024)S(1)} fusion(f32[24576]{0:T(1024)S(1)} %bitcast.7, s32[12288]{0:T(1024)S(1)} %fusion.21), kind=kCustom, calls=%fused_computation.1 | custom fusion | bytes 147456 | tf_op jit(solution)/shard_map/gather | solution.py:42
  240.5 5.5 %convolution_bitcast_fusion = f32[96]{0:T(128)S(1)} fusion(f32[12288,1]{0,1:T(1,128)S(1)} %bitcast.8, f32[96,12288]{1,0:T(8,128)} %param.9), kind=kOutput, calls=%fused_computation.75 | convolution fusion | flops 14155776 | bytes 4768128 | tf_op jit(solution)/shard_map/dot_general | solution.py:44
  246.0 4.9 %all-reduce.4 = f32[96]{0:T(128)S(1)} all-reduce(f32[96]{0:T(128)S(1)} %convolution_bitcast_fusion), channel_id=3, replica_groups=mesh['rows'=16,'cols'=2] {'cols'}, use_global_device_ids=true, to_apply=%region_0.1.clone | all-reduce | flops 96 | bytes 768
  (57 shorter events, 20.5 us)
Async XLA Ops:
  1.6 3.7 %collective-permute-start.1 = (f32[1,96,384]{2,1,0:T(8,128)S(1)}, f32[1,96,384]{2,1,0:T(8,128)S(1)}, u32[]{:S(2)}, u32[]{:S(2)}) collective-permute-start(f32[1,96,384]{2,1,0:T(8,128)S(1)} %get-tuple-element.17), channel_id=1, source_target_pairs={{0,2},{2,4},{4,6},{6,8},{8,10},{10,12},{12,14},{14,16},{16,18},{18... | collective-permute-start | bytes 442376 | tf_op jit(solution)/shard_map/ppermute | solution.py:16
  4.0 5.4 %collective-permute-start = (f32[1,96,384]{2,1,0:T(8,128)S(1)}, f32[1,96,384]{2,1,0:T(8,128)S(1)}, u32[]{:S(2)}, u32[]{:S(2)}) collective-permute-start(f32[1,96,384]{2,1,0:T(8,128)S(1)} %get-tuple-element.16), channel_id=1, source_target_pairs={{2,0},{4,2},{6,4},{8,6},{10,8},{12,10},{14,12},{16,14},{18,16},{20... | collective-permute-start | bytes 442376 | tf_op jit(solution)/shard_map/ppermute | solution.py:17
  9.5 6.1 %collective-permute-start.2 = (f32[18,1,384]{2,1,0:T(1,128)S(1)}, f32[18,1,384]{2,1,0:T(1,128)S(1)}, u32[]{:S(2)}, u32[]{:S(2)}) collective-permute-start(f32[18,1,384]{2,1,0:T(1,128)S(1)} %get-tuple-element.9), channel_id=1, source_target_pairs={{1,0},{3,2},{5,4},{7,6},{9,8},{11,10},{13,12},{15,14},{17,16},{19,... | collective-permute-start | bytes 82952 | tf_op jit(solution)/shard_map/ppermute | solution.py:17
  10.8 7.8 %copy-start.2 = (f32[16,96,384]{2,1,0:T(8,128)S(1)}, f32[16,96,384]{2,1,0:T(8,128)}, u32[]{:S(2)}) copy-start(f32[16,96,384]{2,1,0:T(8,128)} %param.6) | copy-start | bytes 7077892
  10.8 7.8 %copy-start.5 = (f32[16,96,384]{2,1,0:T(8,128)S(1)}, f32[16,96,384]{2,1,0:T(8,128)}, u32[]{:S(2)}) copy-start(f32[16,96,384]{2,1,0:T(8,128)} %param.5) | copy-start | bytes 7077892
  10.8 6.3 %collective-permute-start.3 = (f32[18,1,384]{2,1,0:T(1,128)S(1)}, f32[18,1,384]{2,1,0:T(1,128)S(1)}, u32[]{:S(2)}, u32[]{:S(2)}) collective-permute-start(f32[18,1,384]{2,1,0:T(1,128)S(1)} %get-tuple-element.8), channel_id=1, source_target_pairs={{0,1},{2,3},{4,5},{6,7},{8,9},{10,11},{12,13},{14,15},{16,17},{18,... | collective-permute-start | bytes 82952 | tf_op jit(solution)/shard_map/ppermute | solution.py:16
  22.0 6.4 %collective-permute-start.4 = (f32[1,96,384]{2,1,0:T(8,128)S(1)}, f32[1,96,384]{2,1,0:T(8,128)S(1)}, u32[]{:S(2)}, u32[]{:S(2)}) collective-permute-start(f32[1,96,384]{2,1,0:T(8,128)S(1)} %get-tuple-element.15), channel_id=1, source_target_pairs={{2,0},{4,2},{6,4},{8,6},{10,8},{12,10},{14,12},{16,14},{18,16},{20... | collective-permute-start | bytes 442376 | tf_op jit(solution)/shard_map/ppermute | solution.py:17
  23.3 6.1 %collective-permute-start.5 = (f32[1,96,384]{2,1,0:T(8,128)S(1)}, f32[1,96,384]{2,1,0:T(8,128)S(1)}, u32[]{:S(2)}, u32[]{:S(2)}) collective-permute-start(f32[1,96,384]{2,1,0:T(8,128)S(1)} %get-tuple-element.14), channel_id=1, source_target_pairs={{0,2},{2,4},{4,6},{6,8},{8,10},{10,12},{12,14},{14,16},{16,18},{18... | collective-permute-start | bytes 442376 | tf_op jit(solution)/shard_map/ppermute | solution.py:16
  29.4 5.9 %collective-permute-start.6 = (f32[18,1,384]{2,1,0:T(1,128)S(1)}, f32[18,1,384]{2,1,0:T(1,128)S(1)}, u32[]{:S(2)}, u32[]{:S(2)}) collective-permute-start(f32[18,1,384]{2,1,0:T(1,128)S(1)} %get-tuple-element.7), channel_id=1, source_target_pairs={{1,0},{3,2},{5,4},{7,6},{9,8},{11,10},{13,12},{15,14},{17,16},{19,... | collective-permute-start | bytes 82952 | tf_op jit(solution)/shard_map/ppermute | solution.py:17
  30.7 6.1 %collective-permute-start.7 = (f32[18,1,384]{2,1,0:T(1,128)S(1)}, f32[18,1,384]{2,1,0:T(1,128)S(1)}, u32[]{:S(2)}, u32[]{:S(2)}) collective-permute-start(f32[18,1,384]{2,1,0:T(1,128)S(1)} %get-tuple-element.6), channel_id=1, source_target_pairs={{0,1},{2,3},{4,5},{6,7},{8,9},{10,11},{12,13},{14,15},{16,17},{18,... | collective-permute-start | bytes 82952 | tf_op jit(solution)/shard_map/ppermute | solution.py:16
  44.3 14.0 %copy-start.6 = (s32[24576]{0:T(1024)S(1)}, s32[24576]{0:T(1024)}, u32[]{:S(2)}) copy-start(s32[24576]{0:T(1024)} %param.8) | copy-start | bytes 294916
  44.4 7.1 %collective-permute-start.8 = (f32[1,96,384]{2,1,0:T(8,128)S(1)}, f32[1,96,384]{2,1,0:T(8,128)S(1)}, u32[]{:S(2)}, u32[]{:S(2)}) collective-permute-start(f32[1,96,384]{2,1,0:T(8,128)S(1)} %get-tuple-element.13), channel_id=1, source_target_pairs={{2,0},{4,2},{6,4},{8,6},{10,8},{12,10},{14,12},{16,14},{18,16},{20... | collective-permute-start | bytes 442376 | tf_op jit(solution)/shard_map/ppermute | solution.py:17
  45.7 6.7 %collective-permute-start.9 = (f32[1,96,384]{2,1,0:T(8,128)S(1)}, f32[1,96,384]{2,1,0:T(8,128)S(1)}, u32[]{:S(2)}, u32[]{:S(2)}) collective-permute-start(f32[1,96,384]{2,1,0:T(8,128)S(1)} %get-tuple-element.12), channel_id=1, source_target_pairs={{0,2},{2,4},{4,6},{6,8},{8,10},{10,12},{12,14},{14,16},{16,18},{18... | collective-permute-start | bytes 442376 | tf_op jit(solution)/shard_map/ppermute | solution.py:16
  52.5 5.9 %collective-permute-start.10 = (f32[18,1,384]{2,1,0:T(1,128)S(1)}, f32[18,1,384]{2,1,0:T(1,128)S(1)}, u32[]{:S(2)}, u32[]{:S(2)}) collective-permute-start(f32[18,1,384]{2,1,0:T(1,128)S(1)} %get-tuple-element.5), channel_id=1, source_target_pairs={{1,0},{3,2},{5,4},{7,6},{9,8},{11,10},{13,12},{15,14},{17,16},{19,... | collective-permute-start | bytes 82952 | tf_op jit(solution)/shard_map/ppermute | solution.py:17
  53.8 6.1 %collective-permute-start.11 = (f32[18,1,384]{2,1,0:T(1,128)S(1)}, f32[18,1,384]{2,1,0:T(1,128)S(1)}, u32[]{:S(2)}, u32[]{:S(2)}) collective-permute-start(f32[18,1,384]{2,1,0:T(1,128)S(1)} %get-tuple-element.4), channel_id=1, source_target_pairs={{0,1},{2,3},{4,5},{6,7},{8,9},{10,11},{12,13},{14,15},{16,17},{18,... | collective-permute-start | bytes 82952 | tf_op jit(solution)/shard_map/ppermute | solution.py:16
  63.2 12.7 %copy-start.7 = (s32[768]{0:T(1024)S(1)}, s32[768]{0:T(1024)}, u32[]{:S(2)}) copy-start(s32[768]{0:T(1024)} %param.7) | copy-start | bytes 9220
  67.4 9.5 %copy-start = (f32[16,96,384]{2,1,0:T(8,128)}, f32[16,96,384]{2,1,0:T(8,128)S(1)}, u32[]{:S(2)}) copy-start(f32[16,96,384]{2,1,0:T(8,128)S(1)} %fusion.7) | copy-start | bytes 7077892
  67.4 15.4 %copy-start.8 = (u32[32]{0:T(128)S(1)}, u32[32]{0:T(128)}, u32[]{:S(2)}) copy-start(u32[32]{0:T(128)} %constant.33) | copy-start | bytes 388
  67.4 8.5 %collective-permute-start.12 = (f32[1,96,384]{2,1,0:T(8,128)S(1)}, f32[1,96,384]{2,1,0:T(8,128)S(1)}, u32[]{:S(2)}, u32[]{:S(2)}) collective-permute-start(f32[1,96,384]{2,1,0:T(8,128)S(1)} %get-tuple-element.11), channel_id=1, source_target_pairs={{2,0},{4,2},{6,4},{8,6},{10,8},{12,10},{14,12},{16,14},{18,16},{20... | collective-permute-start | bytes 442376 | tf_op jit(solution)/shard_map/ppermute | solution.py:17
  68.9 8.0 %collective-permute-start.13 = (f32[1,96,384]{2,1,0:T(8,128)S(1)}, f32[1,96,384]{2,1,0:T(8,128)S(1)}, u32[]{:S(2)}, u32[]{:S(2)}) collective-permute-start(f32[1,96,384]{2,1,0:T(8,128)S(1)} %get-tuple-element.10), channel_id=1, source_target_pairs={{0,2},{2,4},{4,6},{6,8},{8,10},{10,12},{12,14},{14,16},{16,18},{18... | collective-permute-start | bytes 442376 | tf_op jit(solution)/shard_map/ppermute | solution.py:16
  76.9 7.1 %collective-permute-start.14 = (f32[18,1,384]{2,1,0:T(1,128)S(1)}, f32[18,1,384]{2,1,0:T(1,128)S(1)}, u32[]{:S(2)}, u32[]{:S(2)}) collective-permute-start(f32[18,1,384]{2,1,0:T(1,128)S(1)} %get-tuple-element.3), channel_id=1, source_target_pairs={{1,0},{3,2},{5,4},{7,6},{9,8},{11,10},{13,12},{15,14},{17,16},{19,... | collective-permute-start | bytes 82952 | tf_op jit(solution)/shard_map/ppermute | solution.py:17
  78.2 6.1 %collective-permute-start.15 = (f32[18,1,384]{2,1,0:T(1,128)S(1)}, f32[18,1,384]{2,1,0:T(1,128)S(1)}, u32[]{:S(2)}, u32[]{:S(2)}) collective-permute-start(f32[18,1,384]{2,1,0:T(1,128)S(1)} %get-tuple-element.2), channel_id=1, source_target_pairs={{0,1},{2,3},{4,5},{6,7},{8,9},{10,11},{12,13},{14,15},{16,17},{18,... | collective-permute-start | bytes 82952 | tf_op jit(solution)/shard_map/ppermute | solution.py:16
  84.0 5.0 %copy-start.1 = (f32[16,96,384]{2,1,0:T(8,128)S(1)}, f32[16,96,384]{2,1,0:T(8,128)}, u32[]{:S(2)}) copy-start(f32[16,96,384]{2,1,0:T(8,128)} %copy-done) | copy-start | bytes 7077892
  84.1 5.0 %copy-start.4 = (f32[16,96,384]{2,1,0:T(8,128)S(1)}, f32[16,96,384]{2,1,0:T(8,128)}, u32[]{:S(2)}) copy-start(f32[16,96,384]{2,1,0:T(8,128)} %param.6) | copy-start | bytes 7077892
  (1 other events, 4.8 us)
where the time goes:
time: 252 us
  local copies, waits for them, and re-layouts  79 us (31%)
  blocking collectives  76.3 us (30%)
  starting transfers between devices  49.2 us (20%)
  other arithmetic  29.9 us (12%)
  waiting for transfers between devices  9.86 us (4%)
  matrix products  5.54 us (2%)
    all_gather x1, blocking collectives, local(): gathered = lax.all_gather(node_values, ('rows', 'cols'), axis=0, tiled=True)  71.4 us
    gather x1, local copies, waits for them, and re-layouts, local(): trace_block = gathered[block_slots]  68 us
    ppermute x8, starting transfers between devices, with_halo(): before = lax.ppermute(last, axis, up)  38.7 us
    div x4, other arithmetic, local(): potential = (source + neighbour_sum(padded)) / 6.0  17 us
    concatenate x7, other arithmetic, with_halo(): value = jnp.concatenate([before, value, after], axis=dim)  12.9 us
    ppermute x8, starting transfers between devices, with_halo(): after = lax.ppermute(first, axis, down)  10.5 us
    ppermute x8, waiting for transfers between devices, with_halo(): before = lax.ppermute(last, axis, up)  7.62 us
    dot_general x1, matrix products, local(): jnp.dot(layer_matrix, trace_block, precision=lax.Precision.HIGHEST, prefe...  5.54 us
  transfers between devices with their start and end apart: 16, of which 8 were waited for; matrix products, arithmetic and copies ran while one was open for 1% of the time, Pallas kernels for 0%

commit v1 on v0

--- a/solution.py
+++ b/solution.py
@@ -1,9 +1,90 @@
 import jax
 import jax.numpy as jnp
 from jax import lax
+from jax.experimental import pallas as pl
+from jax.experimental.pallas import tpu as pltpu
 from jax.sharding import PartitionSpec as P
 
-ITERS = 4
+LANES = 128
+BOTH = ("rows", "cols")
+
+
+def window_kernel(col_ref, table_ref, slot_ref, matrix_hbm, keep_ref, send_ref, matrix_ref, trace_ref, rows_ref, sem):
+    copy = pltpu.make_async_copy(matrix_hbm, matrix_ref, sem)
+    copy.start()
+    owners, width = table_ref.shape
+    parts = width // LANES
+    chunks = trace_ref.shape[0]
+    for q in range(parts):
+        rows_ref[q * owners:(q + 1) * owners, :] = table_ref[:, q * LANES:(q + 1) * LANES]
+    half = chunks
+    group = 12
+    first = col_ref[0] * half
+
+    def gather_group(g, carry):
+        base = pl.multiple_of(g * (group * 8), 8)
+        slots = [slot_ref[pl.ds(pl.multiple_of(first + base + 8 * v, 8), 8), :] for v in range(group)]
+        low = [s & (LANES - 1) for s in slots]
+        high = [s >> 7 for s in slots]
+
+        def owner_step(d, accs):
+            accs = list(accs)
+            for q in range(parts):
+                row = jnp.broadcast_to(rows_ref[pl.ds(q * owners + d, 1), :], (8, LANES))
+                number = d * parts + q
+                for v in range(group):
+                    picked = jnp.take_along_axis(row, low[v], axis=1)
+                    accs[v] = jnp.where(high[v] == number, picked, accs[v])
+            return tuple(accs)
+
+        zero = jnp.zeros((8, LANES), jnp.float32)
+        accs = lax.fori_loop(0, owners, owner_step, (zero,) * group)
+        for v in range(group):
+            trace_ref[pl.ds(pl.multiple_of(base + 8 * v, 8), 8), :] = accs[v]
+        return carry
+
+    lax.fori_loop(0, chunks // (8 * group), gather_group, 0)
+    copy.wait()
+    rows = matrix_ref.shape[0]
+    blocks = rows // 16
+    start = [pl.multiple_of(col_ref[0] * (rows // 2), 8), pl.multiple_of((1 - col_ref[0]) * (rows // 2), 8)]
+
+    def chunk_step(c, accs):
+        accs = list(accs)
+        for u in range(8):
+            at = pl.multiple_of((c * 8 + u) * LANES, LANES)
+            value = jnp.broadcast_to(trace_ref[pl.ds(c * 8 + u, 1), :], (8, LANES))
+            for side in range(2):
+                for b in range(blocks):
+                    tile = matrix_ref[pl.ds(start[side] + 8 * b, 8), pl.ds(at, LANES)]
+                    accs[side * blocks + b] = accs[side * blocks + b] + tile * value
+        return tuple(accs)
+
+    zero = jnp.zeros((8, LANES), jnp.float32)
+    accs = lax.fori_loop(0, chunks // 8, chunk_step, (zero,) * (2 * blocks))
+    for side, out in enumerate((keep_ref, send_ref)):
+        stack = jnp.concatenate(accs[side * blocks:(side + 1) * blocks] + (zero,) * (16 - blocks), axis=0)
+        out[...] = jnp.sum(stack.T, axis=0, keepdims=True)
+
+
+def window_product(col, table, slots, matrix):
+    rows, columns = matrix.shape
+    chunks = columns // LANES
+    out = jax.ShapeDtypeStruct((1, LANES), jnp.float32)
+    vmem = pl.BlockSpec(memory_space=pltpu.VMEM)
+    return pl.pallas_call(
+        window_kernel,
+        out_shape=(out, out),
+        in_specs=[pl.BlockSpec(memory_space=pltpu.SMEM), vmem, vmem, pl.BlockSpec(memory_space=pl.ANY)],
+        out_specs=(vmem, vmem),
+        scratch_shapes=[
+            pltpu.VMEM((rows, columns), jnp.float32),
+            pltpu.VMEM((chunks, LANES), jnp.float32),
+            pltpu.VMEM((table.size // LANES, LANES), jnp.float32),
+            pltpu.SemaphoreType.DMA,
+        ],
+        compiler_params=pltpu.CompilerParams(vmem_limit_bytes=48 << 20),
+    )(col, table, slots, matrix)
 
 
 def with_halo(value, sides, width):
@@ -27,31 +108,23 @@
     return neighbours
 
 
+ITERS = 4
+
+
 def local(phi_start, source, owner_voxel, column_slot, layer_matrix):
     potential = phi_start
     for sweep_index in range(ITERS):
         padded = with_halo(potential, (("rows", 0), ("cols", 1)), 1)
         potential = (source + neighbour_sum(padded)) / 6.0
     node_values = potential.reshape(-1)[owner_voxel]
-    col_count = lax.axis_size("cols")
-    col_index = lax.axis_index("cols")
-    node_total = column_slot.shape[0]
-    block_len = node_total // col_count
-    block_slots = lax.dynamic_slice_in_dim(column_slot, col_index * block_len, block_len, 0)
-    gathered = lax.all_gather(node_values, ("rows", "cols"), axis=0, tiled=True)
-    trace_block = gathered[block_slots]
-    boundary_phi = lax.psum_scatter(
-        jnp.dot(
-            layer_matrix,
-            trace_block,
-            precision=lax.Precision.HIGHEST,
-            preferred_element_type=jnp.float32,
-        ),
-        "cols",
-        scatter_dimension=0,
-        tiled=True,
-    )
-    return (potential, boundary_phi)
+    col = lax.axis_index("cols")
+    devices = lax.axis_size(BOTH)
+    table = lax.all_to_all(jnp.broadcast_to(node_values[None], (devices, node_values.shape[0])), BOTH, 0, 0)
+    slots = column_slot.reshape(-1, LANES)
+    keep, send = window_product(col.astype(jnp.int32)[None], table, slots, layer_matrix)
+    received = lax.ppermute(send, "cols", [(0, 1), (1, 0)])
+    half = layer_matrix.shape[0] // 2
+    return potential, (keep + received)[0, :half]
 
 
 def solution(mesh):

time: 252 us -> 139 us (0.55)
  blocking collectives: 76.3 us -> 0 us
  local copies, waits for them, and re-layouts: 79 us -> 13.4 us
  starting transfers between devices: 49.2 us -> 62.9 us
  waiting for transfers between devices: 9.86 us -> 22.5 us
  Pallas kernels: 0 us -> 10.1 us
  matrix products: 5.54 us -> 0 us
    all_gather x1 -> x0, blocking collectives: 71.4 us -> none  [local(): gathered = lax.all_gather(node_values, ('rows', 'cols'), axis=0, tiled=True)]
    gather x1 -> x0, local copies, waits for them, and re-layouts: 68 us -> none  [local(): trace_block = gathered[block_slots]]
    all_to_all x0 -> x1, starting transfers between devices: none -> 13.3 us  [local(): lax.all_to_all(jnp.broadcast_to(node_values[None], (devices, node_values....]
    pallas_call x0 -> x1, Pallas kernels: none -> 10.1 us  [window_product(): pl.pallas_call(window_kernel, out_shape=(out, out), in_specs=[pl.BlockSpe...]
    all_to_all x0 -> x1, waiting for transfers between devices: none -> 8.1 us  [local(): lax.all_to_all(jnp.broadcast_to(node_values[None], (devices, node_values....]
    dot_general x1 -> x0, matrix products: 5.54 us -> none  [local(): jnp.dot(layer_matrix, trace_block, precision=lax.Precision.HIGHEST, prefe...]
    unnamed x1 -> x0, blocking collectives: 4.94 us -> none
    ppermute x0 -> x1, waiting for transfers between devices: none -> 3.16 us  [local(): received = lax.ppermute(send, 'cols', [(0, 1), (1, 0)])]
  transfers between devices with their start and end apart: 16 -> 18, of which waited for: 8 -> 10; matrix products, arithmetic and copies ran while one was open for 1% -> 1% of each run, Pallas kernels for 0% -> 0%
where the time goes in v1:
time: 139 us; the launch traced here: 138 us
  starting transfers between devices  62.9 us (45%)
  other arithmetic  28.4 us (20%)
  waiting for transfers between devices  22.5 us (16%)
  local copies, waits for them, and re-layouts  13.4 us (10%)
  Pallas kernels  10.1 us (7%)
    ppermute x8, starting transfers between devices, with_halo(): before = lax.ppermute(last, axis, up)  38.8 us
    div x4, other arithmetic, local(): potential = (source + neighbour_sum(padded)) / 6.0  17 us
    all_to_all x1, starting transfers between devices, local(): lax.all_to_all(jnp.broadcast_to(node_values[None], (devices, node_values....  13.3 us
    concatenate x7, other arithmetic, with_halo(): value = jnp.concatenate([before, value, after], axis=dim)  11.4 us
    ppermute x8, starting transfers between devices, with_halo(): after = lax.ppermute(first, axis, down)  10.3 us
    pallas_call x1, Pallas kernels, window_product(): pl.pallas_call(window_kernel, out_shape=(out, out), in_specs=[pl.BlockSpe...  10.1 us
    ppermute x8, waiting for transfers between devices, with_halo(): before = lax.ppermute(last, axis, up)  8.96 us
    all_to_all x1, waiting for transfers between devices, local(): lax.all_to_all(jnp.broadcast_to(node_values[None], (devices, node_values....  8.1 us
  transfers between devices with their start and end apart: 18, of which 10 were waited for; matrix products, arithmetic and copies ran while one was open for 1% of the time, Pallas kernels for 0%

profile of v1, /device:TPU:0, one launch (start us, length us, event | category | flops | bytes accessed | tf_op | source)
XLA Modules:
  0.0 138.3 jit_solution(4719662832303936879)
XLA Ops:
  1.6 2.4 %collective-permute-start.1 = (f32[1,96,384]{2,1,0:T(8,128)S(1)}, f32[1,96,384]{2,1,0:T(8,128)S(1)}, u32[]{:S(2)}, u32[]{:S(2)}) collective-permute-start(f32[1,96,384]{2,1,0:T(8,128)S(1)} %get-tuple-element.21), channel_id=1, source_target_pairs={{0,2},{2,4},{4,6},{6,8},{8,10},{10,12},{12,14},{14,16},{16,18},{18... | collective-permute-start | bytes 442376 | tf_op jit(solution)/shard_map/ppermute | solution.py:97
  5.3 1.8 %constant_dynamic-update-slice_fusion.1 = f32[18,96,384]{2,1,0:T(8,128)S(1)} fusion(f32[18,96,384]{2,1,0:T(8,128)S(1)} %constant_dynamic-update-slice_fusion.2, f32[16,96,384]{2,1,0:T(8,128)} %param.5), kind=kLoop, calls=%fused_computation.86 | loop fusion | bytes 4718592
  7.2 2.2 %collective-permute-done = f32[1,96,384]{2,1,0:T(8,128)S(1)} collective-permute-done((f32[1,96,384]{2,1,0:T(8,128)S(1)}, f32[1,96,384]{2,1,0:T(8,128)S(1)}, u32[]{:S(2)}, u32[]{:S(2)}) %collective-permute-start) | collective-permute-done | bytes 147488 | tf_op jit(solution)/shard_map/ppermute | solution.py:98
  10.8 4.8 %collective-permute-start.3 = (f32[18,1,384]{2,1,0:T(1,128)S(1)}, f32[18,1,384]{2,1,0:T(1,128)S(1)}, u32[]{:S(2)}, u32[]{:S(2)}) collective-permute-start(f32[18,1,384]{2,1,0:T(1,128)S(1)} %get-tuple-element.12), channel_id=1, source_target_pairs={{0,1},{2,3},{4,5},{6,7},{8,9},{10,11},{12,13},{14,15},{16,17},{18,... | collective-permute-start | bytes 82952 | tf_op jit(solution)/shard_map/ppermute | solution.py:97
  18.5 3.4 %fusion.17 = f32[16,96,384]{2,1,0:T(8,128)S(1)} fusion(f32[16,96,384]{2,1,0:T(8,128)S(1)} %copy-done.2, f32[18,98,386]{2,1,0:T(8,128)S(1)} %select_maximum_fusion.12, f32[18,96,384]{2,1,0:T(8,128)S(1)} %constant_dynamic-update-slice_fusion, f32[18,1,384]{2,1,0:T(1,128)S(1)} %collective-permute-done.3, f32[18,1,384]{2,1,0:T(1,128)S(1)} %collective-permute-done.2, ...), kind=kLoop, calls=%fused_computation.65 | loop fusion | flops 6488064 | bytes 14800896 | tf_op jit(solution)/shard_map/div | solution.py:118
  23.3 5.1 %collective-permute-start.5 = (f32[1,96,384]{2,1,0:T(8,128)S(1)}, f32[1,96,384]{2,1,0:T(8,128)S(1)}, u32[]{:S(2)}, u32[]{:S(2)}) collective-permute-start(f32[1,96,384]{2,1,0:T(8,128)S(1)} %get-tuple-element.18), channel_id=1, source_target_pairs={{0,2},{2,4},{4,6},{6,8},{8,10},{10,12},{12,14},{14,16},{16,18},{18... | collective-permute-start | bytes 442376 | tf_op jit(solution)/shard_map/ppermute | solution.py:97
  30.7 4.5 %collective-permute-start.7 = (f32[18,1,384]{2,1,0:T(1,128)S(1)}, f32[18,1,384]{2,1,0:T(1,128)S(1)}, u32[]{:S(2)}, u32[]{:S(2)}) collective-permute-start(f32[18,1,384]{2,1,0:T(1,128)S(1)} %get-tuple-element.10), channel_id=1, source_target_pairs={{0,1},{2,3},{4,5},{6,7},{8,9},{10,11},{12,13},{14,15},{16,17},{18,... | collective-permute-start | bytes 82952 | tf_op jit(solution)/shard_map/ppermute | solution.py:97
  36.8 3.3 %select_maximum_fusion.8 = f32[18,98,386]{2,1,0:T(8,128)S(1)} fusion(f32[18,1,384]{2,1,0:T(1,128)S(1)} %collective-permute-done.6, f32[18,1,384]{2,1,0:T(1,128)S(1)} %collective-permute-done.7, f32[1,96,384]{2,1,0:T(8,128)S(1)} %collective-permute-done.4, f32[16,96,384]{2,1,0:T(8,128)S(1)} %fusion.17, f32[1,96,384]{2,1,0:T(8,128)S(1)} %collective-permute-done.5), kind=kLoop, calls=%fused_computation.11 | loop fusion | flops 8170848 | bytes 5433120 | tf_op jit(solution)/shard_map/concatenate | solution.py:99
  40.1 4.2 %fusion.12 = f32[16,96,384]{2,1,0:T(8,128)S(1)} fusion(f32[16,96,384]{2,1,0:T(8,128)S(1)} %copy-done.2, f32[18,98,386]{2,1,0:T(8,128)S(1)} %select_maximum_fusion.8, f32[18,1,384]{2,1,0:T(1,128)S(1)} %collective-permute-done.7, f32[1,96,384]{2,1,0:T(8,128)S(1)} %collective-permute-done.4, f32[16,96,384]{2,1,0:T(8,128)S(1)} %fusion.17, ...), kind=kLoop, calls=%fused_computation.50 | loop fusion | flops 8847360 | bytes 12146688 | tf_op jit(solution)/shard_map/div | solution.py:118
  45.7 5.8 %collective-permute-start.9 = (f32[1,96,384]{2,1,0:T(8,128)S(1)}, f32[1,96,384]{2,1,0:T(8,128)S(1)}, u32[]{:S(2)}, u32[]{:S(2)}) collective-permute-start(f32[1,96,384]{2,1,0:T(8,128)S(1)} %get-tuple-element.16), channel_id=1, source_target_pairs={{0,2},{2,4},{4,6},{6,8},{8,10},{10,12},{12,14},{14,16},{16,18},{18... | collective-permute-start | bytes 442376 | tf_op jit(solution)/shard_map/ppermute | solution.py:97
  53.7 4.5 %collective-permute-start.11 = (f32[18,1,384]{2,1,0:T(1,128)S(1)}, f32[18,1,384]{2,1,0:T(1,128)S(1)}, u32[]{:S(2)}, u32[]{:S(2)}) collective-permute-start(f32[18,1,384]{2,1,0:T(1,128)S(1)} %get-tuple-element.8), channel_id=1, source_target_pairs={{0,1},{2,3},{4,5},{6,7},{8,9},{10,11},{12,13},{14,15},{16,17},{18,... | collective-permute-start | bytes 82952 | tf_op jit(solution)/shard_map/ppermute | solution.py:97
  59.8 3.3 %select_maximum_fusion.4 = f32[18,98,386]{2,1,0:T(8,128)S(1)} fusion(f32[18,1,384]{2,1,0:T(1,128)S(1)} %collective-permute-done.10, f32[18,1,384]{2,1,0:T(1,128)S(1)} %collective-permute-done.11, f32[1,96,384]{2,1,0:T(8,128)S(1)} %collective-permute-done.8, f32[16,96,384]{2,1,0:T(8,128)S(1)} %fusion.12, f32[1,96,384]{2,1,0:T(8,128)S(1)} %collective-permute-done.9), kind=kLoop, calls=%fused_computation.7 | loop fusion | flops 8170848 | bytes 5433120 | tf_op jit(solution)/shard_map/concatenate | solution.py:99
  63.2 4.2 %fusion.7 = f32[16,96,384]{2,1,0:T(8,128)S(1)} fusion(f32[16,96,384]{2,1,0:T(8,128)S(1)} %copy-done.2, f32[18,98,386]{2,1,0:T(8,128)S(1)} %select_maximum_fusion.4, f32[18,1,384]{2,1,0:T(1,128)S(1)} %collective-permute-done.11, f32[1,96,384]{2,1,0:T(8,128)S(1)} %collective-permute-done.8, f32[16,96,384]{2,1,0:T(8,128)S(1)} %fusion.12, ...), kind=kLoop, calls=%fused_computation.35 | loop fusion | flops 8847360 | bytes 12146688 | tf_op jit(solution)/shard_map/div | solution.py:118
  68.7 7.2 %collective-permute-start.13 = (f32[1,96,384]{2,1,0:T(8,128)S(1)}, f32[1,96,384]{2,1,0:T(8,128)S(1)}, u32[]{:S(2)}, u32[]{:S(2)}) collective-permute-start(f32[1,96,384]{2,1,0:T(8,128)S(1)} %get-tuple-element.14), channel_id=1, source_target_pairs={{0,2},{2,4},{4,6},{6,8},{8,10},{10,12},{12,14},{14,16},{16,18},{18... | collective-permute-start | bytes 442376 | tf_op jit(solution)/shard_map/ppermute | solution.py:97
  78.2 4.5 %collective-permute-start.15 = (f32[18,1,384]{2,1,0:T(1,128)S(1)}, f32[18,1,384]{2,1,0:T(1,128)S(1)}, u32[]{:S(2)}, u32[]{:S(2)}) collective-permute-start(f32[18,1,384]{2,1,0:T(1,128)S(1)} %get-tuple-element.6), channel_id=1, source_target_pairs={{0,1},{2,3},{4,5},{6,7},{8,9},{10,11},{12,13},{14,15},{16,17},{18,... | collective-permute-start | bytes 82952 | tf_op jit(solution)/shard_map/ppermute | solution.py:97
  84.3 3.3 %select_maximum_fusion = f32[18,98,386]{2,1,0:T(8,128)S(1)} fusion(f32[18,1,384]{2,1,0:T(1,128)S(1)} %collective-permute-done.14, f32[18,1,384]{2,1,0:T(1,128)S(1)} %collective-permute-done.15, f32[1,96,384]{2,1,0:T(8,128)S(1)} %collective-permute-done.12, f32[16,96,384]{2,1,0:T(8,128)S(1)} %fusion.7, f32[1,96,384]{2,1,0:T(8,128)S(1)} %collective-permute-done.13), kind=kLoop, calls=%fused_computation.3 | loop fusion | flops 8170848 | bytes 5433120 | tf_op jit(solution)/shard_map/concatenate | solution.py:99
  87.6 5.2 %fusion.2 = f32[16,96,384]{2,1,0:T(8,128)} fusion(f32[16,96,384]{2,1,0:T(8,128)S(1)} %copy-done.2, f32[18,98,386]{2,1,0:T(8,128)S(1)} %select_maximum_fusion, f32[18,1,384]{2,1,0:T(1,128)S(1)} %collective-permute-done.15, f32[1,96,384]{2,1,0:T(8,128)S(1)} %collective-permute-done.12, f32[16,96,384]{2,1,0:T(8,128)S(1)} %fusion.7, ...), kind=kLoop, calls=%fused_computation.20 | loop fusion | flops 8847360 | bytes 12146688 | tf_op jit(solution)/shard_map/div | solution.py:118
  92.8 2.3 %reshape.16 = f32[589824]{0:T(1024)S(1)} reshape(f32[16,96,384]{2,1,0:T(8,128)} %fusion.2) | data formatting | bytes 4718592 | tf_op jit(solution)/shard_map/reshape | solution.py:119
  95.2 4.5 %gather_fusion = f32[768]{0:T(1024)S(1)} fusion(f32[589824]{0:T(1024)S(1)} %reshape.16, s32[1024]{0:T(1024)S(1)} %pad_clamp_fusion), kind=kCustom, calls=%fused_computation | custom fusion | bytes 9216 | tf_op jit(solution)/shard_map/gather | solution.py:119
  100.3 13.3 %all-to-all-start = ((f32[32,1,768]{2,1,0:T(1,128)}), f32[32,1,768]{2,1,0:T(1,128)S(1)}, u32[]{:S(2)}, u32[]{:S(2)}) async-start(f32[32,1,768]{2,1,0:T(1,128)} %broadcast_in_dim.14), calls=%async_computation | async-start | bytes 196608 | tf_op jit(solution)/shard_map/all_to_all | solution.py:122
  113.6 8.1 %all-to-all-done = f32[32,1,768]{2,1,0:T(1,128)S(1)} async-done(((f32[32,1,768]{2,1,0:T(1,128)}), f32[32,1,768]{2,1,0:T(1,128)S(1)}, u32[]{:S(2)}, u32[]{:S(2)}) %all-to-all-start) | async-done | bytes 98336 | tf_op jit(solution)/shard_map/all_to_all | solution.py:122
  121.8 2.3 %copy-done = f32[96,12288]{1,0:T(8,128)S(1)} copy-done((f32[96,12288]{1,0:T(8,128)S(1)}, f32[96,12288]{1,0:T(8,128)}, u32[]{:S(2)}) %copy-start) | copy-done | bytes 4718616
  124.1 10.1 %shard_map.68 = (f32[1,128]{1,0:T(1,128)S(1)}, f32[1,128]{1,0:T(1,128)S(1)}) custom-call(s32[1]{0:T(128)} %bitcast.col_ref, f32[32,768]{1,0:T(8,128)S(1)} %bitcast.7, s32[192,128]{1,0:T(8,128)S(1)} %bitcast.8, f32[96,12288]{1,0:T(8,128)S(1)} %copy-done), custom_call_target="tpu_custom_call" | custom-call | tf_op jit(solution)/shard_map/pallas_call | solution.py:75
  134.6 3.2 %collective-permute-done.16 = f32[1,128]{1,0:T(1,128)S(1)} collective-permute-done((f32[1,128]{1,0:T(1,128)S(1)}, f32[1,128]{1,0:T(1,128)S(1)}, u32[]{:S(2)}, u32[]{:S(2)}) %collective-permute-start.16) | collective-permute-done | bytes 544 | tf_op jit(solution)/shard_map/ppermute | solution.py:125
  (50 shorter events, 23.6 us)
Async XLA Ops:
  1.6 3.7 %collective-permute-start.1 = (f32[1,96,384]{2,1,0:T(8,128)S(1)}, f32[1,96,384]{2,1,0:T(8,128)S(1)}, u32[]{:S(2)}, u32[]{:S(2)}) collective-permute-start(f32[1,96,384]{2,1,0:T(8,128)S(1)} %get-tuple-element.21), channel_id=1, source_target_pairs={{0,2},{2,4},{4,6},{6,8},{8,10},{10,12},{12,14},{14,16},{16,18},{18... | collective-permute-start | bytes 442376 | tf_op jit(solution)/shard_map/ppermute | solution.py:97
  4.0 5.4 %collective-permute-start = (f32[1,96,384]{2,1,0:T(8,128)S(1)}, f32[1,96,384]{2,1,0:T(8,128)S(1)}, u32[]{:S(2)}, u32[]{:S(2)}) collective-permute-start(f32[1,96,384]{2,1,0:T(8,128)S(1)} %get-tuple-element.20), channel_id=1, source_target_pairs={{2,0},{4,2},{6,4},{8,6},{10,8},{12,10},{14,12},{16,14},{18,16},{20... | collective-permute-start | bytes 442376 | tf_op jit(solution)/shard_map/ppermute | solution.py:98
  9.5 6.1 %collective-permute-start.2 = (f32[18,1,384]{2,1,0:T(1,128)S(1)}, f32[18,1,384]{2,1,0:T(1,128)S(1)}, u32[]{:S(2)}, u32[]{:S(2)}) collective-permute-start(f32[18,1,384]{2,1,0:T(1,128)S(1)} %get-tuple-element.13), channel_id=1, source_target_pairs={{1,0},{3,2},{5,4},{7,6},{9,8},{11,10},{13,12},{15,14},{17,16},{19,... | collective-permute-start | bytes 82952 | tf_op jit(solution)/shard_map/ppermute | solution.py:98
  10.8 7.8 %copy-start.2 = (f32[16,96,384]{2,1,0:T(8,128)S(1)}, f32[16,96,384]{2,1,0:T(8,128)}, u32[]{:S(2)}) copy-start(f32[16,96,384]{2,1,0:T(8,128)} %param.6) | copy-start | bytes 7077892
  10.8 7.8 %copy-start.3 = (f32[16,96,384]{2,1,0:T(8,128)S(1)}, f32[16,96,384]{2,1,0:T(8,128)}, u32[]{:S(2)}) copy-start(f32[16,96,384]{2,1,0:T(8,128)} %param.5) | copy-start | bytes 7077892
  10.8 6.3 %collective-permute-start.3 = (f32[18,1,384]{2,1,0:T(1,128)S(1)}, f32[18,1,384]{2,1,0:T(1,128)S(1)}, u32[]{:S(2)}, u32[]{:S(2)}) collective-permute-start(f32[18,1,384]{2,1,0:T(1,128)S(1)} %get-tuple-element.12), channel_id=1, source_target_pairs={{0,1},{2,3},{4,5},{6,7},{8,9},{10,11},{12,13},{14,15},{16,17},{18,... | collective-permute-start | bytes 82952 | tf_op jit(solution)/shard_map/ppermute | solution.py:97
  22.0 6.4 %collective-permute-start.4 = (f32[1,96,384]{2,1,0:T(8,128)S(1)}, f32[1,96,384]{2,1,0:T(8,128)S(1)}, u32[]{:S(2)}, u32[]{:S(2)}) collective-permute-start(f32[1,96,384]{2,1,0:T(8,128)S(1)} %get-tuple-element.19), channel_id=1, source_target_pairs={{2,0},{4,2},{6,4},{8,6},{10,8},{12,10},{14,12},{16,14},{18,16},{20... | collective-permute-start | bytes 442376 | tf_op jit(solution)/shard_map/ppermute | solution.py:98
  23.3 6.1 %collective-permute-start.5 = (f32[1,96,384]{2,1,0:T(8,128)S(1)}, f32[1,96,384]{2,1,0:T(8,128)S(1)}, u32[]{:S(2)}, u32[]{:S(2)}) collective-permute-start(f32[1,96,384]{2,1,0:T(8,128)S(1)} %get-tuple-element.18), channel_id=1, source_target_pairs={{0,2},{2,4},{4,6},{6,8},{8,10},{10,12},{12,14},{14,16},{16,18},{18... | collective-permute-start | bytes 442376 | tf_op jit(solution)/shard_map/ppermute | solution.py:97
  29.4 5.9 %collective-permute-start.6 = (f32[18,1,384]{2,1,0:T(1,128)S(1)}, f32[18,1,384]{2,1,0:T(1,128)S(1)}, u32[]{:S(2)}, u32[]{:S(2)}) collective-permute-start(f32[18,1,384]{2,1,0:T(1,128)S(1)} %get-tuple-element.11), channel_id=1, source_target_pairs={{1,0},{3,2},{5,4},{7,6},{9,8},{11,10},{13,12},{15,14},{17,16},{19,... | collective-permute-start | bytes 82952 | tf_op jit(solution)/shard_map/ppermute | solution.py:98
  30.7 6.1 %collective-permute-start.7 = (f32[18,1,384]{2,1,0:T(1,128)S(1)}, f32[18,1,384]{2,1,0:T(1,128)S(1)}, u32[]{:S(2)}, u32[]{:S(2)}) collective-permute-start(f32[18,1,384]{2,1,0:T(1,128)S(1)} %get-tuple-element.10), channel_id=1, source_target_pairs={{0,1},{2,3},{4,5},{6,7},{8,9},{10,11},{12,13},{14,15},{16,17},{18,... | collective-permute-start | bytes 82952 | tf_op jit(solution)/shard_map/ppermute | solution.py:97
  44.4 7.1 %collective-permute-start.8 = (f32[1,96,384]{2,1,0:T(8,128)S(1)}, f32[1,96,384]{2,1,0:T(8,128)S(1)}, u32[]{:S(2)}, u32[]{:S(2)}) collective-permute-start(f32[1,96,384]{2,1,0:T(8,128)S(1)} %get-tuple-element.17), channel_id=1, source_target_pairs={{2,0},{4,2},{6,4},{8,6},{10,8},{12,10},{14,12},{16,14},{18,16},{20... | collective-permute-start | bytes 442376 | tf_op jit(solution)/shard_map/ppermute | solution.py:98
  45.7 6.7 %collective-permute-start.9 = (f32[1,96,384]{2,1,0:T(8,128)S(1)}, f32[1,96,384]{2,1,0:T(8,128)S(1)}, u32[]{:S(2)}, u32[]{:S(2)}) collective-permute-start(f32[1,96,384]{2,1,0:T(8,128)S(1)} %get-tuple-element.16), channel_id=1, source_target_pairs={{0,2},{2,4},{4,6},{6,8},{8,10},{10,12},{12,14},{14,16},{16,18},{18... | collective-permute-start | bytes 442376 | tf_op jit(solution)/shard_map/ppermute | solution.py:97
  52.4 5.9 %collective-permute-start.10 = (f32[18,1,384]{2,1,0:T(1,128)S(1)}, f32[18,1,384]{2,1,0:T(1,128)S(1)}, u32[]{:S(2)}, u32[]{:S(2)}) collective-permute-start(f32[18,1,384]{2,1,0:T(1,128)S(1)} %get-tuple-element.9), channel_id=1, source_target_pairs={{1,0},{3,2},{5,4},{7,6},{9,8},{11,10},{13,12},{15,14},{17,16},{19,... | collective-permute-start | bytes 82952 | tf_op jit(solution)/shard_map/ppermute | solution.py:98
  53.7 6.1 %collective-permute-start.11 = (f32[18,1,384]{2,1,0:T(1,128)S(1)}, f32[18,1,384]{2,1,0:T(1,128)S(1)}, u32[]{:S(2)}, u32[]{:S(2)}) collective-permute-start(f32[18,1,384]{2,1,0:T(1,128)S(1)} %get-tuple-element.8), channel_id=1, source_target_pairs={{0,1},{2,3},{4,5},{6,7},{8,9},{10,11},{12,13},{14,15},{16,17},{18,... | collective-permute-start | bytes 82952 | tf_op jit(solution)/shard_map/ppermute | solution.py:97
  63.2 12.7 %copy-start.4 = (s32[768]{0:T(1024)S(1)}, s32[768]{0:T(1024)}, u32[]{:S(2)}) copy-start(s32[768]{0:T(1024)} %param.7) | copy-start | bytes 9220
  67.4 8.5 %collective-permute-start.12 = (f32[1,96,384]{2,1,0:T(8,128)S(1)}, f32[1,96,384]{2,1,0:T(8,128)S(1)}, u32[]{:S(2)}, u32[]{:S(2)}) collective-permute-start(f32[1,96,384]{2,1,0:T(8,128)S(1)} %get-tuple-element.15), channel_id=1, source_target_pairs={{2,0},{4,2},{6,4},{8,6},{10,8},{12,10},{14,12},{16,14},{18,16},{20... | collective-permute-start | bytes 442376 | tf_op jit(solution)/shard_map/ppermute | solution.py:98
  68.7 8.2 %collective-permute-start.13 = (f32[1,96,384]{2,1,0:T(8,128)S(1)}, f32[1,96,384]{2,1,0:T(8,128)S(1)}, u32[]{:S(2)}, u32[]{:S(2)}) collective-permute-start(f32[1,96,384]{2,1,0:T(8,128)S(1)} %get-tuple-element.14), channel_id=1, source_target_pairs={{0,2},{2,4},{4,6},{6,8},{8,10},{10,12},{12,14},{14,16},{16,18},{18... | collective-permute-start | bytes 442376 | tf_op jit(solution)/shard_map/ppermute | solution.py:97
  76.9 5.9 %collective-permute-start.14 = (f32[18,1,384]{2,1,0:T(1,128)S(1)}, f32[18,1,384]{2,1,0:T(1,128)S(1)}, u32[]{:S(2)}, u32[]{:S(2)}) collective-permute-start(f32[18,1,384]{2,1,0:T(1,128)S(1)} %get-tuple-element.7), channel_id=1, source_target_pairs={{1,0},{3,2},{5,4},{7,6},{9,8},{11,10},{13,12},{15,14},{17,16},{19,... | collective-permute-start | bytes 82952 | tf_op jit(solution)/shard_map/ppermute | solution.py:98
  78.2 6.1 %collective-permute-start.15 = (f32[18,1,384]{2,1,0:T(1,128)S(1)}, f32[18,1,384]{2,1,0:T(1,128)S(1)}, u32[]{:S(2)}, u32[]{:S(2)}) collective-permute-start(f32[18,1,384]{2,1,0:T(1,128)S(1)} %get-tuple-element.6), channel_id=1, source_target_pairs={{0,1},{2,3},{4,5},{6,7},{8,9},{10,11},{12,13},{14,15},{16,17},{18,... | collective-permute-start | bytes 82952 | tf_op jit(solution)/shard_map/ppermute | solution.py:97
  95.1 26.6 %copy-start.1 = (s32[24576]{0:T(1024)S(1)}, s32[24576]{0:T(1024)}, u32[]{:S(2)}) copy-start(s32[24576]{0:T(1024)} %param.8) | copy-start | bytes 294916
  100.3 21.4 %all-to-all-start = ((f32[32,1,768]{2,1,0:T(1,128)}), f32[32,1,768]{2,1,0:T(1,128)S(1)}, u32[]{:S(2)}, u32[]{:S(2)}) async-start(f32[32,1,768]{2,1,0:T(1,128)} %broadcast_in_dim.14), calls=%async_computation | async-start | bytes 196608 | tf_op jit(solution)/shard_map/all_to_all | solution.py:122
  121.8 2.3 %copy-start = (f32[96,12288]{1,0:T(8,128)S(1)}, f32[96,12288]{1,0:T(8,128)}, u32[]{:S(2)}) copy-start(f32[96,12288]{1,0:T(8,128)} %matrix_hbm.1) | copy-start | bytes 14155780
  134.2 3.6 %collective-permute-start.16 = (f32[1,128]{1,0:T(1,128)S(1)}, f32[1,128]{1,0:T(1,128)S(1)}, u32[]{:S(2)}, u32[]{:S(2)}) collective-permute-start(f32[1,128]{1,0:T(1,128)S(1)} %get-tuple-element.5), channel_id=1, source_target_pairs={{0,1},{1,0},{2,3},{3,2},{4,5},{5,4},{6,7},{7,6},{8,9},{9,8},{10,11... | collective-permute-start | bytes 1544 | tf_op jit(solution)/shard_map/ppermute | solution.py:125

commit v2 on v1

v2 whole, which is shorter than its diff:
```python
import functools

import jax
import jax.numpy as jnp
from jax import lax
from jax.experimental import pallas as pl
from jax.experimental.pallas import tpu as pltpu
from jax.sharding import PartitionSpec as P

ITERS = 4
LANES = 128
SUB = 8
SIXTH = 1.0 / 6.0
BOTH = ("rows", "cols")
VMEM = pl.BlockSpec(memory_space=pltpu.VMEM)
SMEM = pl.BlockSpec(memory_space=pltpu.SMEM)
ANY = pl.BlockSpec(memory_space=pl.ANY)


def lanes_of(shape=(SUB, LANES)):
    return lax.broadcasted_iota(jnp.int32, shape, 1)


def subs_of(shape=(SUB, LANES)):
    return lax.broadcasted_iota(jnp.int32, shape, 0)


def in_layer(tiles):
    blocks, chunks = len(tiles), len(tiles[0])
    lane, sub = lanes_of(), subs_of()
    zero = jnp.zeros((SUB, LANES), jnp.float32)
    before = [[pltpu.roll(t, 1, 1) for t in row] for row in tiles]
    after = [[pltpu.roll(t, LANES - 1, 1) for t in row] for row in tiles]
    above = [[pltpu.roll(t, 1, 0) for t in row] for row in tiles]
    below = [[pltpu.roll(t, SUB - 1, 0) for t in row] for row in tiles]
    out = []
    for b in range(blocks):
        row = []
        for c in range(chunks):
            west = jnp.where(lane == 0, before[b][c - 1] if c else zero, before[b][c])
            east = jnp.where(lane == LANES - 1, after[b][c + 1] if c + 1 < chunks else zero, after[b][c])
            north = jnp.where(sub == 0, above[b - 1][c] if b else zero, above[b][c])
            south = jnp.where(sub == SUB - 1, below[b + 1][c] if b + 1 < blocks else zero, below[b][c])
            row.append((west + east) + (north + south))
        out.append(row)
    return out


def load(ref, at, blocks, chunks):
    return [[ref[pl.ds(at + SUB * b, SUB), c * LANES:(c + 1) * LANES] for c in range(chunks)] for b in range(blocks)]


def store(ref, at, tiles):
    for b, row in enumerate(tiles):
        for c, tile in enumerate(row):
            ref[pl.ds(at + SUB * b, SUB), c * LANES:(c + 1) * LANES] = tile


def total(*terms):
    terms = [t for t in terms if t is not None]
    out = []
    for b in range(len(terms[0])):
        row = []
        for c in range(len(terms[0][0])):
            value = terms[0][b][c]
            for t in terms[1:]:
                value = value + t[b][c]
            row.append(value * SIXTH)
        out.append(row)
    return out


def spread(tile, i):
    return jnp.broadcast_to(tile[i:i + 1, :], (SUB, LANES))


def stack(rows):
    sub = subs_of()
    out = []
    for c in range(len(rows[0])):
        value = rows[0][c]
        for i in range(1, len(rows)):
            value = jnp.where(sub == i, rows[i][c], value)
        out.append(value)
    return out


def near_row(right, first, last, m):
    return [jnp.where(right, spread(f, m), spread(t, SUB - 1 - m)) for f, t in zip(first, last)]


def face_kernel(info, phi, src, pack_a, pack_b, pack_y, diag_a, diag_b, p0, s0, ps, edge0, edge_s, edge, sem):
    cz, cy, nx = phi.shape
    blocks, chunks = cy // SUB, nx // LANES
    odd, col = info[0], info[1]
    right = (col == 1)
    copies = []
    for i in range(2):
        low = odd if i == 0 else 1 - odd
        for j in range(4):
            z = jnp.where(low == 1, j, cz - 1 - j)
            copies.append(pltpu.make_async_copy(phi.at[z], p0.at[i, j], sem.at[i, j]))
            if j < 3:
                copies.append(pltpu.make_async_copy(src.at[z], s0.at[i, j], sem.at[i, 4 + j]))
    at = pl.multiple_of(jnp.where(right, 0, cy - SUB), SUB)
    edges = [
        pltpu.make_async_copy(phi.at[:, pl.ds(at, SUB), :], edge0, sem.at[0, 7]),
        pltpu.make_async_copy(src.at[:, pl.ds(at, SUB), :], edge_s, sem.at[1, 7]),
    ]
    for c in copies + edges:
        c.start()
    for c in copies:
        c.wait()
    for i, (pack, diag) in enumerate(((pack_a, diag_a), (pack_b, diag_b))):
        layer0 = [load(p0.at[i, j], 0, blocks, chunks) for j in range(4)]
        layer_s = [load(s0.at[i, j], 0, blocks, chunks) for j in range(3)]
        store(pack, 0, layer0[0])
        layer1 = []
        for j in range(3):
            layer1.append(total(layer_s[j], in_layer(layer0[j]), layer0[j + 1], layer0[j - 1] if j else None))
            if j:
                store(ps.at[i, j - 1], 0, layer1[j])
            else:
                store(pack, cy, layer1[j])
        layer1 = [load(pack, cy, blocks, chunks)] + [load(ps.at[i, j], 0, blocks, chunks) for j in range(2)]
        layer2 = []
        for j in range(2):
            layer2.append(total(layer_s[j], in_layer(layer1[j]), layer1[j + 1], layer1[j - 1] if j else None))
            if j:
                store(ps.at[i, 2], 0, layer2[j])
            else:
                store(pack, 2 * cy, layer2[j])
        layer2 = [load(pack, 2 * cy, blocks, chunks), load(ps.at[i, 2], 0, blocks, chunks)]
        store(pack, 3 * cy, total(layer_s[0], in_layer(layer2[0]), layer2[1]))
        near = lambda layer, m: near_row(right, layer[0], layer[-1], m)
        store(pack, 4 * cy, [near(layer0[1], 0)])
        store(pack_y, 4 * cz, [stack([near(layer0[0], 1)] * 2)]) if i == 0 else None
        if i == 1:
            kept = load(pack_y, 4 * cz, 1, chunks)[0]
            store(pack_y, 4 * cz, [stack([kept, near(layer0[0], 1)])])
        first = [near(layer0[0], 0), near(layer0[1], 0), near(layer0[2], 0), near(layer1[0], 0), near(layer1[1], 0),
                 near(layer2[0], 0), near(layer0[0], 1), near(layer0[0], 2)]
        store(diag, 0, [stack(first)])
        store(diag, SUB, [near(layer1[0], 1)])
    for c in edges:
        c.wait()

    def planes(k, tiles):
        for half in range(cz // SUB):
            rows = [near_row(right, tiles[half * SUB + z], tiles[half * SUB + z], 0) for z in range(SUB)]
            store(pack_y, k * cz + half * SUB, [stack(rows)])

    now = [[edge0[z, :, c * LANES:(c + 1) * LANES] for c in range(chunks)] for z in range(cz)]
    planes(0, now)
    for k in range(1, 4):
        then = []
        for z in range(cz):
            source = [[edge_s[z, :, c * LANES:(c + 1) * LANES] for c in range(chunks)]]
            parts = [source, in_layer([now[z]])]
            if z:
                parts.append([now[z - 1]])
            if z + 1 < cz:
                parts.append([now[z + 1]])
            tiles = total(*parts)
            then.append(tiles[0])
            for c in range(chunks):
                edge[k % 2, z, :, c * LANES:(c + 1) * LANES] = tiles[0][c]
        now = [[edge[k % 2, z, :, c * LANES:(c + 1) * LANES] for c in range(chunks)] for z in range(cz)]
        planes(k, now)


def faces(info, phi, src):
    cz, cy, nx = phi.shape
    f32 = lambda *shape: jax.ShapeDtypeStruct(shape, jnp.float32)
    return pl.pallas_call(
        face_kernel,
        out_shape=(f32(4 * cy + SUB, nx), f32(4 * cy + SUB, nx), f32(4 * cz + SUB, nx), f32(2 * SUB, nx), f32(2 * SUB, nx)),
        in_specs=[SMEM, ANY, ANY],
        out_specs=(VMEM,) * 5,
        scratch_shapes=[
            pltpu.VMEM((2, 4, cy, nx), jnp.float32),
            pltpu.VMEM((2, 3, cy, nx), jnp.float32),
            pltpu.VMEM((2, 3, cy, nx), jnp.float32),
            pltpu.VMEM((cz, SUB, nx), jnp.float32),
            pltpu.VMEM((cz, SUB, nx), jnp.float32),
            pltpu.VMEM((2, cz, SUB, nx), jnp.float32),
            pltpu.SemaphoreType.DMA((2, 8)),
        ],
        compiler_params=pltpu.CompilerParams(vmem_limit_bytes=24 << 20),
        name="faces",
    )(info, phi, src)


def alone_kernel(phi, src, out, buf, sources, sem):
    cz, cy, nx = phi.shape
    blocks, chunks = cy // SUB, nx // LANES
    copies = [
        pltpu.make_async_copy(phi, buf.at[0, 1:cz + 1], sem.at[0]),
        pltpu.make_async_copy(src, sources, sem.at[1]),
    ]
    for c in copies:
        c.start()
    zero = [[jnp.zeros((SUB, LANES), jnp.float32)] * chunks] * blocks
    for i in range(2):
        for z in (0, cz + 1):
            store(buf.at[i, z], 0, zero)
    for c in copies:
        c.wait()

    for k in range(ITERS):
        last = k == ITERS - 1

        def layer(z, carry, k=k, last=last):
            at = k % 2
            value = total(
                load(sources.at[z], 0, blocks, chunks),
                in_layer(load(buf.at[at, z + 1], 0, blocks, chunks)),
                load(buf.at[at, z], 0, blocks, chunks),
                load(buf.at[at, z + 2], 0, blocks, chunks),
            )
            if last:
                for c in range(chunks):
                    for b in range(blocks):
                        out[c, pl.ds(pl.multiple_of(z * cy, SUB) + SUB * b, SUB), :] = value[b][c]
            else:
                store(buf.at[1 - at, z + 1], 0, value)
            return carry

        lax.fori_loop(0, cz, layer, 0)


def alone(phi, src):
    cz, cy, nx = phi.shape
    return pl.pallas_call(
        alone_kernel,
        out_shape=jax.ShapeDtypeStruct((nx // LANES, cz * cy, LANES), jnp.float32),
        in_specs=[ANY, ANY],
        out_specs=VMEM,
        scratch_shapes=[
            pltpu.VMEM((2, cz + 2, cy, nx), jnp.float32),
            pltpu.VMEM((cz, cy, nx), jnp.float32),
            pltpu.SemaphoreType.DMA((2,)),
        ],
        compiler_params=pltpu.CompilerParams(vmem_limit_bytes=24 << 20),
        cost_estimate=pl.CostEstimate(flops=10 * ITERS * phi.size, bytes_accessed=12 * phi.size, transcendentals=0),
        name="alone",
    )(phi, src)


def respond(blocks, chunks, outer, inner, mask, scratch, finish):
    slot = iter(range(scratch.shape[0]))

    def keep(tiles):
        ref = scratch.at[next(slot)]
        store(ref, 0, mask(tiles))
        return lambda: load(ref, 0, blocks, chunks)

    o0, i0 = keep(total(outer(0))), keep(total(inner(0)))
    o0_2 = keep(total(outer(1), in_layer(o0()), i0()))
    i0_2 = keep(total(inner(1), in_layer(i0()), o0()))
    o1_2, i1_2 = keep(total(o0())), keep(total(i0()))
    o0_3 = keep(total(outer(2), in_layer(o0_2()), o1_2(), i0_2()))
    i0_3 = keep(total(inner(2), in_layer(i0_2()), o0_2(), i1_2()))
    i1_3 = keep(total(in_layer(i1_2()), i0_2()))
    i2_3 = keep(total(i1_2()))
    finish(0, total(inner(3), in_layer(i0_3()), o0_3(), i1_3()))
    finish(1, total(in_layer(i1_3()), i0_3(), i2_3()))
    finish(2, total(in_layer(i2_3()), i1_3()))
    finish(3, total(i2_3()))


SLOTS = 10


def join_kernel(
    info, row_of, lane_of, block, own_a, own_b, own_y, got_a, got_b, got_y, got_da, got_db,
    potential, values, pot, layers, columns, picked, sem,
):
    chunks, cells, _ = pot.shape
    cy = (own_a.shape[0] - SUB) // 4
    cz = cells // cy
    blocks = cy // SUB
    odd, right = info[0], info[1] == 1
    has = (info[2].astype(jnp.float32), info[3].astype(jnp.float32))
    fetch = pltpu.make_async_copy(block, pot, sem.at[0])
    fetch.start()
    sub = subs_of()
    zero = [jnp.zeros((SUB, LANES), jnp.float32)] * chunks
    at_low = jnp.where(right, 1.0, 0.0)
    at_high = 1.0 - at_low

    def tile_row(ref, at):
        return load(ref, at, 1, chunks)[0]

    def row(ref, at, i):
        return [spread(t, i) for t in tile_row(ref, at)]

    def scale(tiles, factor):
        return [t * factor for t in tiles]

    def flank(rows, low):
        if not rows:
            return zero
        out = zero
        for m, value in enumerate(rows):
            out = [jnp.where(sub == (SUB - 1 - m if low else m), v, o) for v, o in zip(value, out)]
        return out

    def near(ref, at, m):
        return near_row(right, tile_row(ref, at), tile_row(ref, at + cy - SUB), m)

    def diag(ref, k, j=0, m=0):
        place = {(0, 0, 0): 0, (0, 1, 0): 1, (0, 2, 0): 2, (1, 0, 0): 3, (1, 1, 0): 4, (2, 0, 0): 5, (0, 0, 1): 6,
                 (0, 0, 2): 7, (1, 0, 1): 8}[(k, j, m)]
        return row(ref, place // SUB * SUB, place % SUB)

    for i, (own, got, got_d) in enumerate(((own_a, got_a, got_da), (own_b, got_b, got_db))):
        low_side = odd if i == 0 else 1 - odd

        def layer_start(j, low_side=low_side):
            return pl.multiple_of(jnp.where(low_side == 1, j, cz - 1 - j) * cy, SUB)

        def column_row(ref, k, low_side=low_side):
            return [jnp.where(low_side == 1, a, b) for a, b in zip(row(ref, k * cz, 0), row(ref, k * cz + cz - SUB, SUB - 1))]

        def driven(plane, rows, i=i):
            middle = [scale(t, has[i]) for t in plane]
            return ([scale(flank(rows, True), has[i] * at_low)] + middle + [scale(flank(rows, False), has[i] * at_high)])

        def inner(k, got=got, got_d=got_d, driven=driven):
            rows = [diag(got_d, k, m=m) for m in range(3 - k)]
            return driven(load(got, k * cy, blocks, chunks), rows)

        def outer(k, own=own, driven=driven, column_row=column_row, i=i):
            rows = [column_row(got_y, k)] if k < 2 else []
            if k == 0:
                rows.append(row(got_y, 4 * cz, i))
            return driven(load(own, k * cy, blocks, chunks), rows)

        def mask(tiles):
            return [scale(tiles[0], at_low)] + tiles[1:-1] + [scale(tiles[-1], at_high)]

        def finish(j, tiles, i=i, layer_start=layer_start):
            if i == 0 and j == 0:
                fetch.wait()
            start = layer_start(j)
            for b in range(blocks):
                for c in range(chunks):
                    where = (c, pl.ds(start + SUB * b, SUB), slice(None))
                    pot[where] = pot[where] + tiles[b + 1][c]

        respond(blocks + 2, chunks, outer, inner, mask, layers, finish)

    low_has = jnp.where(odd == 1, has[0], has[1])
    high_has = jnp.where(odd == 1, has[1], has[0])

    def either(a, b):
        return [jnp.where(odd == 1, x, y) for x, y in zip(a, b)], [jnp.where(odd == 1, y, x) for x, y in zip(a, b)]

    def along(plane, pairs):
        low = scale(flank([p[0] for p in pairs], True), low_has)
        high = scale(flank([p[1] for p in pairs], False), high_has)
        return [low] + plane + [high]

    def inner_y(k):
        pairs = [either(diag(got_da, k, j=j), diag(got_db, k, j=j)) for j in range(3 - k)]
        return along(load(got_y, k * cz, cz // SUB, chunks), pairs)

    def outer_y(k):
        pairs = [either(near(got_a, k * cy, 0), near(got_b, k * cy, 0))] if k < 2 else []
        if k == 0:
            pairs.append(either(row(got_a, 4 * cy, 0), row(got_b, 4 * cy, 0)))
        return along(load(own_y, k * cz, cz // SUB, chunks), pairs)

    def mask_y(tiles):
        return [scale(tiles[0], low_has)] + tiles[1:-1] + [scale(tiles[-1], high_has)]

    ends = []

    def finish_y(j, tiles):
        ends.append(tiles[1:-1])

    respond(cz // SUB + 2, chunks, outer_y, inner_y, mask_y, columns, finish_y)
    edge = pl.multiple_of(jnp.where(right, 0, cy - SUB), SUB)
    for z in range(cz):
        for c in range(chunks):
            change = jnp.zeros((SUB, LANES), jnp.float32)
            for m in range(4):
                place = jnp.where(right, m, SUB - 1 - m)
                change = jnp.where(sub == place, spread(ends[m][z // SUB][c], z % SUB), change)
            where = (c, pl.ds(z * cy + edge, SUB), slice(None))
            pot[where] = pot[where] + change

    leave = [
        pltpu.make_async_copy(pot.at[c], potential.at[:, pl.ds(c * LANES, LANES)], sem.at[1 + c]) for c in range(chunks)
    ]
    for c in leave:
        c.start()

    flat = pot.reshape(chunks * cells, LANES)
    wide = picked.shape[0]

    def pick(g, carry):
        for u in range(16):
            i = g * 16 + u
            picked[pl.ds(i, 1), :] = flat[pl.ds(row_of[i], 1), :]
        return carry

    lax.fori_loop(0, wide // 16, pick, 0)
    deep = lax.broadcasted_iota(jnp.int32, (LANES, LANES), 0)
    for q in range(wide // LANES):
        turned = picked[q * LANES:(q + 1) * LANES, :].T
        chosen = jnp.where(deep == lane_of[q:q + 1, :], turned, 0.0)
        line = jnp.sum(chosen, axis=0, keepdims=True)
        values[:, :, q * LANES:(q + 1) * LANES] = jnp.broadcast_to(line[None], (values.shape[0], 1, LANES))
    for c in leave:
        c.wait()


def join(info, row_of, lane_of, block, own, got, devices):
    chunks, cells, _ = block.shape
    cy = (own[0].shape[0] - SUB) // 4
    cz = cells // cy
    nodes = row_of.shape[0]
    nx = chunks * LANES
    return pl.pallas_call(
        join_kernel,
        out_shape=(
            jax.ShapeDtypeStruct((cells, nx), jnp.float32),
            jax.ShapeDtypeStruct((devices, 1, nodes), jnp.float32),
        ),
        in_specs=[SMEM, SMEM, VMEM, ANY] + [VMEM] * 8,
        out_specs=(ANY, VMEM),
        scratch_shapes=[
            pltpu.VMEM((chunks, cells, LANES), jnp.float32),
            pltpu.VMEM((SLOTS, cy + 2 * SUB, nx), jnp.float32),
            pltpu.VMEM((SLOTS, cz + 2 * SUB, nx), jnp.float32),
            pltpu.VMEM((nodes, LANES), jnp.float32),
            pltpu.SemaphoreType.DMA((1 + chunks,)),
        ],
        compiler_params=pltpu.CompilerParams(vmem_limit_bytes=24 << 20),
        name="join",
    )(info, row_of, lane_of, block, *own[:3], *got)


def window_kernel(col_ref, table_ref, slot_ref, matrix_hbm, keep_ref, send_ref, matrix_ref, trace_ref, sem):
    copy = pltpu.make_async_copy(matrix_hbm, matrix_ref, sem)
    copy.start()
    owners, _, width = table_ref.shape
    parts = width // LANES
    chunks = trace_ref.shape[0]
    group = 12
    first = col_ref[0] * chunks

    def gather_group(g, carry):
        base = pl.multiple_of(g * (group * SUB), SUB)
        slots = [slot_ref[pl.ds(pl.multiple_of(first + base + SUB * v, SUB), SUB), :] for v in range(group)]
        low = [s & (LANES - 1) for s in slots]
        high = [s >> 7 for s in slots]

        def owner_step(d, accs):
            accs = list(accs)
            for q in range(parts):
                row = jnp.broadcast_to(table_ref[d, :, q * LANES:(q + 1) * LANES], (SUB, LANES))
                number = d * parts + q
                for v in range(group):
                    picked = jnp.take_along_axis(row, low[v], axis=1)
                    accs[v] = jnp.where(high[v] == number, picked, accs[v])
            return tuple(accs)

        zero = jnp.zeros((SUB, LANES), jnp.float32)
        accs = lax.fori_loop(0, owners, owner_step, (zero,) * group)
        for v in range(group):
            trace_ref[pl.ds(pl.multiple_of(base + SUB * v, SUB), SUB), :] = accs[v]
        return carry

    lax.fori_loop(0, chunks // (SUB * group), gather_group, 0)
    copy.wait()
    rows = matrix_ref.shape[0]
    blocks = rows // 16
    start = [pl.multiple_of(col_ref[0] * (rows // 2), SUB), pl.multiple_of((1 - col_ref[0]) * (rows // 2), SUB)]

    def chunk_step(c, accs):
        accs = list(accs)
        for u in range(SUB):
            at = pl.multiple_of((c * SUB + u) * LANES, LANES)
            value = jnp.broadcast_to(trace_ref[pl.ds(c * SUB + u, 1), :], (SUB, LANES))
            for side in range(2):
                for b in range(blocks):
                    tile = matrix_ref[pl.ds(start[side] + SUB * b, SUB), pl.ds(at, LANES)]
                    accs[side * blocks + b] = accs[side * blocks + b] + tile * value
        return tuple(accs)

    zero = jnp.zeros((SUB, LANES), jnp.float32)
    accs = lax.fori_loop(0, chunks // SUB, chunk_step, (zero,) * (2 * blocks))
    for side, out in enumerate((keep_ref, send_ref)):
        tall = jnp.concatenate(accs[side * blocks:(side + 1) * blocks] + (zero,) * (16 - blocks), axis=0)
        out[...] = jnp.sum(tall.T, axis=0, keepdims=True)


def window_product(col, table, slots, matrix):
    rows, columns = matrix.shape
    chunks = columns // LANES
    out = jax.ShapeDtypeStruct((1, LANES), jnp.float32)
    return pl.pallas_call(
        window_kernel,
        out_shape=(out, out),
        in_specs=[SMEM, VMEM, VMEM, pl.BlockSpec(memory_space=pltpu.HBM)],
        out_specs=(VMEM, VMEM),
        scratch_shapes=[
            pltpu.VMEM((rows, columns), jnp.float32),
            pltpu.VMEM((chunks, LANES), jnp.float32),
            pltpu.SemaphoreType.DMA,
        ],
        compiler_params=pltpu.CompilerParams(vmem_limit_bytes=48 << 20),
        name="window",
    )(col, table, slots, matrix)


def routes(n):
    def across(r):
        other = r + 1 if r % 2 else r - 1
        return other if 0 <= other < n else None

    near = [(r, r ^ 1) for r in range(n)]
    far, near_diag, far_diag = [], [], []
    for r in range(n):
        for c in range(2):
            other = across(r)
            far.append((r * 2 + c, r * 2 + 1 - c if other is None else other * 2 + c))
            near_diag.append((r * 2 + c, (r ^ 1) * 2 + 1 - c))
            far_diag.append((r * 2 + c, (r if other is None else other) * 2 + 1 - c))
    return near, far, near_diag, far_diag


def local(phi_start, source, owner_voxel, column_slot, layer_matrix):
    n = lax.axis_size("rows")
    assert lax.axis_size("cols") == 2 and n % 2 == 0
    devices = 2 * n
    cz, cy, nx = phi_start.shape
    r = lax.axis_index("rows").astype(jnp.int32)
    col = lax.axis_index("cols").astype(jnp.int32)
    odd = r % 2
    far_row = jnp.where(odd == 1, r < n - 1, r > 0).astype(jnp.int32)
    info = jnp.stack([odd, col, jnp.ones_like(odd), far_row])
    near, far, near_diag, far_diag = routes(n)
    swap = [(0, 1), (1, 0)]

    pack_a, pack_b, pack_y, diag_a, diag_b = faces(info, phi_start, source)
    got_b = lax.ppermute(pack_b, BOTH, far)
    got_db = lax.ppermute(diag_b, BOTH, far_diag)
    got_y = lax.ppermute(pack_y, "cols", swap)
    got_da = lax.ppermute(diag_a, BOTH, near_diag)
    got_a = lax.ppermute(pack_a, "rows", near)
    block = alone(phi_start, source)
    x = owner_voxel % nx
    row_of = (x // LANES) * (cz * cy) + owner_voxel // nx
    lane_of = (x % LANES).reshape(-1, LANES)
    potential, values = join(
        info, row_of, lane_of, block, (pack_a, pack_b, pack_y), (got_a, got_b, got_y, got_da, got_db), devices
    )
    table = lax.all_to_all(values, BOTH, 0, 0, tiled=True)
    slots = column_slot.reshape(-1, LANES)
    keep, send = window_product(col[None], table, slots, layer_matrix)
    received = lax.ppermute(send, "cols", swap)
    half = layer_matrix.shape[0] // 2
    return potential.reshape(cz, cy, nx), (keep + received)[0, :half]


def solution(mesh):
    return jax.shard_map(
        local,
        mesh=mesh,
        in_specs=(
            P("rows", "cols", None),
            P("rows", "cols", None),
            P(("rows", "cols")),
            P(),
            P("rows", "cols"),
        ),
        out_specs=(P("rows", "cols", None), P(("rows", "cols"))),
        check_vma=False,
    )
```

time: 139 us -> 59 us (0.42)
  starting transfers between devices: 62.9 us -> 6.79 us
  other arithmetic: 28.4 us -> 0.1 us
  Pallas kernels: 10.1 us -> 30.7 us
  waiting for transfers between devices: 22.5 us -> 3.17 us
  blocking collectives: 0 us -> 13.4 us
  local copies, waits for them, and re-layouts: 13.4 us -> 3.87 us
    ppermute x17 -> x6, starting transfers between devices: 49.6 us -> 6.79 us  [the longest x1 2.56 us: local(): got_b = lax.ppermute(pack_b, BOTH, far)]
    pallas_call x1 -> x4, Pallas kernels: 10.1 us -> 30.7 us  [the longest x1 11 us: alone(): pl.pallas_call(alone_kernel, out_shape=jax.ShapeDtypeStruct((nx // LANES,...]
    div x4 -> x0, other arithmetic: 17 us -> none  [local(): potential = (source + neighbour_sum(padded)) / 6.0]
    all_to_all x0 -> x1, blocking collectives: none -> 13.4 us  [local(): table = lax.all_to_all(values, BOTH, 0, 0, tiled=True)]
    all_to_all x1 -> x0, starting transfers between devices: 13.3 us -> none  [local(): lax.all_to_all(jnp.broadcast_to(node_values[None], (devices, node_values....]
    concatenate x7 -> x0, other arithmetic: 11.4 us -> none  [with_halo(): value = jnp.concatenate([before, value, after], axis=dim)]
    ppermute x17 -> x6, waiting for transfers between devices: 14.3 us -> 3.17 us  [the longest x1 3.16 us: local(): received = lax.ppermute(send, 'cols', swap)]
    all_to_all x1 -> x0, waiting for transfers between devices: 8.1 us -> none  [local(): lax.all_to_all(jnp.broadcast_to(node_values[None], (devices, node_values....]
  transfers between devices with their start and end apart: 18 -> 6, of which waited for: 10 -> 1; matrix products, arithmetic and copies ran while one was open for 1% -> 0% of each run, Pallas kernels for 0% -> 19%
where the time goes in v2:
time: 59 us; the launch traced here: 58.8 us
  Pallas kernels  30.7 us (52%)
  blocking collectives  13.4 us (23%)
  starting transfers between devices  6.79 us (12%)
  local copies, waits for them, and re-layouts  3.87 us (7%)
  waiting for transfers between devices  3.17 us (5%)
  between operations  0.76 us (1%)
    all_to_all x1, blocking collectives, local(): table = lax.all_to_all(values, BOTH, 0, 0, tiled=True)  13.4 us
    pallas_call x1, Pallas kernels, alone(): pl.pallas_call(alone_kernel, out_shape=jax.ShapeDtypeStruct((nx // LANES,...  11 us
    pallas_call x1, Pallas kernels, window_product(): pl.pallas_call(window_kernel, out_shape=(out, out), in_specs=[SMEM, VMEM,...  10.1 us
    pallas_call x1, Pallas kernels, faces(): pl.pallas_call(face_kernel, out_shape=(f32(4 * cy + SUB, nx), f32(4 * cy...  5.09 us
    pallas_call x1, Pallas kernels, join(): pl.pallas_call(join_kernel, out_shape=(jax.ShapeDtypeStruct((cells, nx),...  4.51 us
    unnamed x12, local copies, waits for them, and re-layouts  3.35 us
    ppermute x1, waiting for transfers between devices, local(): received = lax.ppermute(send, 'cols', swap)  3.16 us
    ppermute x1, starting transfers between devices, local(): got_b = lax.ppermute(pack_b, BOTH, far)  2.56 us
  transfers between devices with their start and end apart: 6, of which 1 were waited for; matrix products, arithmetic and copies ran while one was open for 0% of the time, Pallas kernels for 19%

profile of v2, /device:TPU:0, one launch (start us, length us, event | category | flops | bytes accessed | tf_op | source)
XLA Modules:
  0.0 58.8 jit_solution(1497109212577940687)
XLA Ops:
  0.6 0.1 pad_add_fusion.info
  0.7 1.7 %copy-done = f32[16,96,384]{2,1,0:T(8,128)S(1)} copy-done((f32[16,96,384]{2,1,0:T(8,128)S(1)}, f32[16,96,384]{2,1,0:T(8,128)}, u32[]{:S(2)}) %copy-start) | copy-done | bytes 2359320
  2.4 1.7 %copy-done.1 = f32[16,96,384]{2,1,0:T(8,128)S(1)} copy-done((f32[16,96,384]{2,1,0:T(8,128)S(1)}, f32[16,96,384]{2,1,0:T(8,128)}, u32[]{:S(2)}) %copy-start.1) | copy-done | bytes 2359320
  4.1 5.1 %faces.1 = (f32[392,384]{1,0:T(8,128)S(1)}, f32[392,384]{1,0:T(8,128)S(1)}, f32[72,384]{1,0:T(8,128)S(1)}, f32[16,384]{1,0:T(8,128)S(1)}, f32[16,384]{1,0:T(8,128)S(1)}) custom-call(s32[4]{0:T(128)S(1)} %pad_add_fusion.info, f32[16,96,384]{2,1,0:T(8,128)S(1)} %copy-done, f32[16,96,384]{2,1,0:T(8,128)S(1)} %copy-done.1), custom_call_target="tpu_custom_call" | custom-call | tf_op jit(solution)/shard_map/faces/pallas_call | solution.py:175
  9.2 0.5 collective-permute-start
  9.7 2.6 %collective-permute-start.1 = (f32[392,384]{1,0:T(8,128)S(1)}, f32[392,384]{1,0:T(8,128)S(1)}, u32[]{:S(2)}, u32[]{:S(2)}) collective-permute-start(f32[392,384]{1,0:T(8,128)S(1)} %get-tuple-element.12.own_b), channel_id=1, source_target_pairs={{0,1},{1,0},{2,4},{3,5},{4,2},{5,3},{6,8},{7,9},{8,6},{9,7},{10,12... | collective-permute-start | bytes 1806344 | tf_op jit(solution)/shard_map/ppermute | solution.py:550
  12.2 1.2 %collective-permute-start.3 = (f32[16,384]{1,0:T(8,128)S(1)}, f32[16,384]{1,0:T(8,128)S(1)}, u32[]{:S(2)}, u32[]{:S(2)}) collective-permute-start(f32[16,384]{1,0:T(8,128)S(1)} %get-tuple-element.14), channel_id=1, source_target_pairs={{0,3},{1,2},{2,1},{3,0},{4,7},{5,6},{6,5},{7,4},{8,11},{9,10},{10,... | collective-permute-start | bytes 73736 | tf_op jit(solution)/shard_map/ppermute | solution.py:553
  13.5 0.5 collective-permute-start.4
  14.0 1.5 %collective-permute-start.2 = (f32[72,384]{1,0:T(8,128)S(1)}, f32[72,384]{1,0:T(8,128)S(1)}, u32[]{:S(2)}, u32[]{:S(2)}) collective-permute-start(f32[72,384]{1,0:T(8,128)S(1)} %get-tuple-element.13.own_y), channel_id=1, source_target_pairs={{0,1},{1,0},{2,3},{3,2},{4,5},{5,4},{6,7},{7,6},{8,9},{9,8},{10,11... | collective-permute-start | bytes 331784 | tf_op jit(solution)/shard_map/ppermute | solution.py:552
  15.5 0.0 copy-done.3
  15.5 0.0 slice-start.1
  15.6 11.0 %alone.1.block = f32[3,1536,128]{2,1,0:T(8,128)S(1)} custom-call(f32[16,96,384]{2,1,0:T(8,128)S(1)} %copy-done, f32[16,96,384]{2,1,0:T(8,128)S(1)} %copy-done.1), custom_call_target="tpu_custom_call" | custom-call | flops 23592960 | bytes 7077888 | tf_op jit(solution)/shard_map/alone/pallas_call | solution.py:234
  26.6 0.0 collective-permute-done.3.got_da
  26.6 0.0 collective-permute-done.4.got_db
  26.6 0.0 collective-permute-done.2.got_y
  26.6 0.0 collective-permute-done.got_a
  26.6 0.0 collective-permute-done.1.got_b
  26.6 0.0 copy-start.2
  26.6 4.5 %join.1 = (f32[1536,384]{1,0:T(8,128)}, f32[32,1,768]{2,1,0:T(1,128)S(1)}) custom-call(s32[4]{0:T(128)S(1)} %pad_add_fusion.info, s32[768]{0:T(1024)S(1)} %get-tuple-element.21.row_of, s32[6,128]{1,0:T(8,128)S(1)} %get-tuple-element.20.lane_of, f32[3,1536,128]{2,1,0:T(8,128)S(1)} %alone.1.block, f32[392,384]{1,0:T(8,128)S(1)} %get-tuple-element.11.own_a, ...), custom_call_target="tpu_custom_call" | custom-call | tf_op jit(solution)/shard_map/join/pallas_call | solution.py:426
  31.1 13.4 %all_to_all.5.table_ref = f32[32,1,768]{2,1,0:T(1,128)S(1)} all-to-all(f32[32,1,768]{2,1,0:T(1,128)S(1)} %get-tuple-element.17), channel_id=1, replica_groups=mesh['rows'=16,'cols'=2] {'rows','cols'}, dimensions={0} | all-to-all | bytes 196608 | tf_op jit(solution)/shard_map/all_to_all | solution.py:562
  44.6 10.1 %window.1 = (f32[1,128]{1,0:T(1,128)S(1)}, f32[1,128]{1,0:T(1,128)S(1)}) custom-call(s32[1]{0:T(128)} %bitcast.1.col_ref, f32[32,1,768]{2,1,0:T(1,128)S(1)} %all_to_all.5.table_ref, s32[192,128]{1,0:T(8,128)S(1)} %bitcast.11, f32[96,12288]{1,0:T(8,128)S(1)} %bitcast.10), custom_call_target="tpu_custom_call" | custom-call | tf_op jit(solution)/shard_map/window/pallas_call | solution.py:505
  54.6 0.4 collective-permute-start.5
  55.1 3.2 %collective-permute-done.5 = f32[1,128]{1,0:T(1,128)S(1)} collective-permute-done((f32[1,128]{1,0:T(1,128)S(1)}, f32[1,128]{1,0:T(1,128)S(1)}, u32[]{:S(2)}, u32[]{:S(2)}) %collective-permute-start.5) | collective-permute-done | bytes 544 | tf_op jit(solution)/shard_map/ppermute | solution.py:565
  58.2 0.5 slice_bitcast_fusion
  (10 shorter events, 0.0 us)
Async XLA Ops:
  0.7 1.7 %copy-start = (f32[16,96,384]{2,1,0:T(8,128)S(1)}, f32[16,96,384]{2,1,0:T(8,128)}, u32[]{:S(2)}) copy-start(f32[16,96,384]{2,1,0:T(8,128)} %phi.3) | copy-start | bytes 7077892
  2.4 1.7 %copy-start.1 = (f32[16,96,384]{2,1,0:T(8,128)S(1)}, f32[16,96,384]{2,1,0:T(8,128)}, u32[]{:S(2)}) copy-start(f32[16,96,384]{2,1,0:T(8,128)} %src.3) | copy-start | bytes 7077892
  4.1 11.5 %copy-start.3 = (s32[768]{0:T(1024)S(1)}, s32[768]{0:T(1024)}, u32[]{:S(2)}) copy-start(s32[768]{0:T(1024)} %param.7) | copy-start | bytes 9220
  4.1 40.5 %slice-start = ((s8[4718592]{0:T(1024)(128)(4,1)}), s8[4194304]{0:T(1024)(128)(4,1)S(1)}, s32[]{:S(2)}) async-start(s8[4718592]{0:T(1024)(128)(4,1)} %bitcast.9), calls=%async_computation.1 | async-start | bytes 8388608
  9.2 17.4 %collective-permute-start = (f32[392,384]{1,0:T(8,128)S(1)}, f32[392,384]{1,0:T(8,128)S(1)}, u32[]{:S(2)}, u32[]{:S(2)}) collective-permute-start(f32[392,384]{1,0:T(8,128)S(1)} %get-tuple-element.11.own_a), channel_id=1, source_target_pairs={{0,2},{2,0},{4,6},{6,4},{8,10},{10,8},{12,14},{14,12},{16,18},{18,... | collective-permute-start | bytes 1806344 | tf_op jit(solution)/shard_map/ppermute | solution.py:554
  9.7 16.9 %collective-permute-start.1 = (f32[392,384]{1,0:T(8,128)S(1)}, f32[392,384]{1,0:T(8,128)S(1)}, u32[]{:S(2)}, u32[]{:S(2)}) collective-permute-start(f32[392,384]{1,0:T(8,128)S(1)} %get-tuple-element.12.own_b), channel_id=1, source_target_pairs={{0,1},{1,0},{2,4},{3,5},{4,2},{5,3},{6,8},{7,9},{8,6},{9,7},{10,12... | collective-permute-start | bytes 1806344 | tf_op jit(solution)/shard_map/ppermute | solution.py:550
  12.2 14.3 %collective-permute-start.3 = (f32[16,384]{1,0:T(8,128)S(1)}, f32[16,384]{1,0:T(8,128)S(1)}, u32[]{:S(2)}, u32[]{:S(2)}) collective-permute-start(f32[16,384]{1,0:T(8,128)S(1)} %get-tuple-element.14), channel_id=1, source_target_pairs={{0,3},{1,2},{2,1},{3,0},{4,7},{5,6},{6,5},{7,4},{8,11},{9,10},{10,... | collective-permute-start | bytes 73736 | tf_op jit(solution)/shard_map/ppermute | solution.py:553
  13.5 13.1 %collective-permute-start.4 = (f32[16,384]{1,0:T(8,128)S(1)}, f32[16,384]{1,0:T(8,128)S(1)}, u32[]{:S(2)}, u32[]{:S(2)}) collective-permute-start(f32[16,384]{1,0:T(8,128)S(1)} %get-tuple-element.15), channel_id=1, source_target_pairs={{0,1},{1,0},{2,5},{3,4},{4,3},{5,2},{6,9},{7,8},{8,7},{9,6},{10,13... | collective-permute-start | bytes 73736 | tf_op jit(solution)/shard_map/ppermute | solution.py:551
  14.0 12.5 %collective-permute-start.2 = (f32[72,384]{1,0:T(8,128)S(1)}, f32[72,384]{1,0:T(8,128)S(1)}, u32[]{:S(2)}, u32[]{:S(2)}) collective-permute-start(f32[72,384]{1,0:T(8,128)S(1)} %get-tuple-element.13.own_y), channel_id=1, source_target_pairs={{0,1},{1,0},{2,3},{3,2},{4,5},{5,4},{6,7},{7,6},{8,9},{9,8},{10,11... | collective-permute-start | bytes 331784 | tf_op jit(solution)/shard_map/ppermute | solution.py:552
  15.5 29.0 %slice-start.1 = ((s8[4718592]{0:T(1024)(128)(4,1)}), s8[524288]{0:T(1024)(128)(4,1)S(1)}, s32[]{:S(2)}) async-start(s8[4718592]{0:T(1024)(128)(4,1)} %bitcast.9), calls=%async_computation.2 | async-start | bytes 1048576
  26.6 17.9 %copy-start.2 = (s32[24576]{0:T(1024)S(1)}, s32[24576]{0:T(1024)}, u32[]{:S(2)}) copy-start(s32[24576]{0:T(1024)} %param.8) | copy-start | bytes 294916
  54.6 3.6 %collective-permute-start.5 = (f32[1,128]{1,0:T(1,128)S(1)}, f32[1,128]{1,0:T(1,128)S(1)}, u32[]{:S(2)}, u32[]{:S(2)}) collective-permute-start(f32[1,128]{1,0:T(1,128)S(1)} %get-tuple-element.19), channel_id=1, source_target_pairs={{0,1},{1,0},{2,3},{3,2},{4,5},{5,4},{6,7},{7,6},{8,9},{9,8},{10,11... | collective-permute-start | bytes 1544 | tf_op jit(solution)/shard_map/ppermute | solution.py:565

commit v3 on v0

v3 whole, which is shorter than its diff:
```python
import functools

import jax
import jax.numpy as jnp
from jax import lax
from jax.experimental import pallas as pl
from jax.experimental.pallas import tpu as pltpu
from jax.sharding import PartitionSpec as P

ITERS = 4
LANES = 128
SUB = 8
SIXTH = 1.0 / 6.0
FIRST_LIMIT = 58 << 20
BOTH = ("rows", "cols")
VMEM = pl.BlockSpec(memory_space=pltpu.VMEM)
SMEM = pl.BlockSpec(memory_space=pltpu.SMEM)
ANY = pl.BlockSpec(memory_space=pl.ANY)


def lanes_of(shape=(SUB, LANES)):
    return lax.broadcasted_iota(jnp.int32, shape, 1)


def subs_of(shape=(SUB, LANES)):
    return lax.broadcasted_iota(jnp.int32, shape, 0)


PAD = SUB


def around(ref, slot, rows):
    chunks = ref.shape[1]
    lane = lanes_of()
    zero = jnp.zeros((SUB, LANES), jnp.float32)
    out = []
    for b in range(rows // SUB):
        at = PAD + SUB * b
        here = [ref[slot, c, pl.ds(at, SUB), :] for c in range(chunks)]
        before = [pltpu.roll(t, 1, 1) for t in here]
        after = [pltpu.roll(t, LANES - 1, 1) for t in here]
        row = []
        for c in range(chunks):
            west = jnp.where(lane == 0, before[c - 1] if c else zero, before[c])
            east = jnp.where(lane == LANES - 1, after[c + 1] if c + 1 < chunks else zero, after[c])
            row.append((west + east) + (ref[slot, c, pl.ds(at - 1, SUB), :] + ref[slot, c, pl.ds(at + 1, SUB), :]))
        out.append(row)
    return out


def layer_of(ref, slot, rows):
    return [[ref[slot, c, pl.ds(PAD + SUB * b, SUB), :] for c in range(ref.shape[1])] for b in range(rows // SUB)]


def keep_layer(ref, slot, tiles):
    for b, row in enumerate(tiles):
        for c, tile in enumerate(row):
            ref[slot, c, pl.ds(PAD + SUB * b, SUB), :] = tile


def clear_pads(ref, slot, rows):
    zero = jnp.zeros((SUB, LANES), jnp.float32)
    for c in range(ref.shape[1]):
        ref[slot, c, 0:PAD, :] = zero
        ref[slot, c, PAD + rows:2 * PAD + rows, :] = zero


def load(ref, at, blocks):
    return [[ref[c, pl.ds(at + SUB * b, SUB), :] for c in range(ref.shape[0])] for b in range(blocks)]


def store(ref, at, tiles):
    for b, row in enumerate(tiles):
        for c, tile in enumerate(row):
            ref[c, pl.ds(at + SUB * b, SUB), :] = tile


def total(*terms):
    terms = [t for t in terms if t is not None]
    out = []
    for b in range(len(terms[0])):
        row = []
        for c in range(len(terms[0][0])):
            value = terms[0][b][c]
            for t in terms[1:]:
                value = value + t[b][c]
            row.append(value * SIXTH)
        out.append(row)
    return out


def spread(tile, i):
    return jnp.broadcast_to(tile[i:i + 1, :], (SUB, LANES))


def stack(rows):
    sub = subs_of()
    out = []
    for c in range(len(rows[0])):
        value = rows[0][c]
        for i in range(1, len(rows)):
            value = jnp.where(sub == i, rows[i][c], value)
        out.append(value)
    return out


def near_row(right, first, last, m):
    return [jnp.where(right, spread(f, m), spread(t, SUB - 1 - m)) for f, t in zip(first, last)]


def solve_face(first, source, work, pack, rows):
    blocks = rows // SUB
    start = [layer_of(*first(j), rows) for j in range(4)]
    store(pack, 0, start[0])
    for j in range(3):
        keep_layer(work, j, total(source(j), around(*first(j), rows), start[j + 1], start[j - 1] if j else None))
    one = [layer_of(work, j, rows) for j in range(3)]
    store(pack, rows, one[0])
    for j in range(2):
        keep_layer(work, 3 + j, total(source(j), around(work, j, rows), one[j + 1], one[j - 1] if j else None))
    two = [layer_of(work, 3 + j, rows) for j in range(2)]
    store(pack, 2 * rows, two[0])
    store(pack, 3 * rows, total(source(0), around(work, 3, rows), two[1]))


def fetch_face(phi, src, low, raw, sem):
    last = phi.shape[0] - 1
    copies = []
    for j in range(4):
        z = jnp.where(low == 1, j, last - j)
        copies.append(pltpu.make_async_copy(phi.at[z], raw.at[0, j], sem.at[0, j]))
        if j < 3:
            copies.append(pltpu.make_async_copy(src.at[z], raw.at[1, j], sem.at[1, j]))
    return copies


def tiles_of(ref):
    rows, wide = ref.shape
    return [[ref[SUB * b:SUB * b + SUB, c * LANES:(c + 1) * LANES] for c in range(wide // LANES)] for b in range(rows // SUB)]


def send_face(right, source, p0, work, pack, diag, cy):
    chunks = p0.shape[1]
    solve_face(lambda j: (p0, j), source, work, pack, cy)

    def near(ref, slot, m):
        edges = [[ref[slot, c, pl.ds(at, SUB), :] for c in range(chunks)] for at in (PAD, PAD + cy - SUB)]
        return near_row(right, *edges, m)

    store(pack, 4 * cy, [near(p0, 1, 0)])
    store(diag, 0, [stack([
        near(p0, 0, 0), near(p0, 1, 0), near(p0, 2, 0), near(work, 0, 0), near(work, 1, 0),
        near(work, 3, 0), near(p0, 0, 1), near(p0, 0, 2),
    ])])
    store(diag, SUB, [near(work, 0, 1)])


def far_face_kernel(phi, src, pack, diag, raw, p0, work, sem):
    cy = phi.shape[1]
    odd, col, _ = whereabouts()
    copies = fetch_face(phi, src, 1 - odd, raw, sem)
    for c in copies:
        c.start()
    for i in range(4):
        clear_pads(p0, i, cy)
    for i in range(5):
        clear_pads(work, i, cy)
    for c in copies:
        c.wait()
    for j in range(4):
        keep_layer(p0, j, tiles_of(raw.at[0, j]))
    send_face(col == 1, lambda j: tiles_of(raw.at[1, j]), p0, work, pack, diag, cy)


def f32(*shape):
    return jax.ShapeDtypeStruct(shape, jnp.float32)


def face_scratch(chunks, cy):
    tall = cy + 2 * PAD
    return [
        pltpu.VMEM((2, 4, cy, chunks * LANES), jnp.float32),
        pltpu.VMEM((4, chunks, tall, LANES), jnp.float32),
        pltpu.VMEM((5, chunks, tall, LANES), jnp.float32),
    ]


def whereabouts():
    n, r = lax.axis_size("rows"), lax.axis_index("rows").astype(jnp.int32)
    odd = lax.rem(r, 2)
    return odd, lax.axis_index("cols").astype(jnp.int32), jnp.where(odd == 1, r < n - 1, r > 0).astype(jnp.int32)


def far_face(phi, src):
    cz, cy, nx = phi.shape
    chunks = nx // LANES
    return pl.pallas_call(
        far_face_kernel,
        out_shape=(f32(chunks, 4 * cy + SUB, LANES), f32(chunks, 2 * SUB, LANES)),
        in_specs=[ANY, ANY],
        out_specs=(VMEM, VMEM),
        scratch_shapes=face_scratch(chunks, cy) + [pltpu.SemaphoreType.DMA((2, 4))],
        compiler_params=pltpu.CompilerParams(vmem_limit_bytes=FIRST_LIMIT),
        name="far_face",
    )(phi, src)


def near_face_kernel(after, phi, src, pack, pack_y, diag, p0, work, edge, edge_p, edge_w):
    cz, cy, nx = phi.shape
    chunks = nx // LANES
    odd, col, _ = whereabouts()
    right = col == 1
    for i in range(4):
        clear_pads(p0, i, cy)
        clear_pads(edge_p, i, cz)
    for i in range(5):
        clear_pads(work, i, cy)
        clear_pads(edge_w, i, cz)

    def layer(j):
        return jnp.where(odd == 1, j, cz - 1 - j)

    for j in range(4):
        keep_layer(p0, j, tiles_of(phi.at[layer(j)]))
    send_face(right, lambda j: tiles_of(src.at[layer(j)]), p0, work, pack, diag, cy)
    at = pl.multiple_of(jnp.where(right, 0, cy - SUB), SUB)
    for i, whole in enumerate((phi, src)):
        for z in range(cz):
            for c in range(chunks):
                edge[i, c, z * SUB:(z + 1) * SUB, :] = whole[z, pl.ds(at, SUB), c * LANES:(c + 1) * LANES]
    flat = edge.reshape(2 * chunks * cz * SUB, LANES)

    def plane(i, c, m):
        row = jnp.where(right, m, SUB - 1 - m)
        return flat[pl.ds((i * chunks + c) * cz * SUB + row, cz, stride=SUB), :]

    for m in range(4):
        for c in range(chunks):
            edge_p[m, c, PAD:PAD + cz, :] = plane(0, c, m)

    def source(m):
        whole = [plane(1, c, m) for c in range(chunks)]
        return [[w[SUB * b:SUB * b + SUB, :] for w in whole] for b in range(cz // SUB)]

    solve_face(lambda j: (edge_p, j), source, edge_w, pack_y, cz)
    ends = [[edge_p[1, c, pl.ds(PAD + i, 1), :] for c in range(chunks)] for i in (0, cz - 1)]
    ends = [[jnp.broadcast_to(t, (SUB, LANES)) for t in row] for row in ends]
    own = [[jnp.where(odd == 1, a, b) for a, b in zip(*ends)], [jnp.where(odd == 1, b, a) for a, b in zip(*ends)]]
    store(pack_y, 4 * cz, [stack(own)])


def near_face(after, phi, src):
    cz, cy, nx = phi.shape
    chunks = nx // LANES
    tall = cz + 2 * PAD
    return pl.pallas_call(
        near_face_kernel,
        out_shape=(f32(chunks, 4 * cy + SUB, LANES), f32(chunks, 4 * cz + SUB, LANES), f32(chunks, 2 * SUB, LANES)),
        in_specs=[ANY, VMEM, VMEM],
        out_specs=(VMEM,) * 3,
        scratch_shapes=face_scratch(chunks, cy)[1:] + [
            pltpu.VMEM((2, chunks, cz * SUB, LANES), jnp.float32),
            pltpu.VMEM((4, chunks, tall, LANES), jnp.float32),
            pltpu.VMEM((5, chunks, tall, LANES), jnp.float32),
        ],
        compiler_params=pltpu.CompilerParams(vmem_limit_bytes=24 << 20),
        name="near_face",
    )(after, phi, src)


def alone_kernel(phi, src, matrix, out, matrix_out, buf_a, buf_b, sem):
    cz, cy, nx = phi.shape
    blocks, chunks = cy // SUB, nx // LANES
    pieces = 4
    deep = matrix.shape[0] // pieces
    copies = [
        pltpu.make_async_copy(matrix.at[i * deep:(i + 1) * deep], matrix_out.at[i * deep:(i + 1) * deep], sem.at[i])
        for i in range(pieces)
    ]
    for c in copies:
        c.start()
    zero = [[jnp.zeros((SUB, LANES), jnp.float32)] * chunks] * blocks
    for ref in (buf_a, buf_b):
        for z in (0, cz + 1):
            keep_layer(ref, z, zero)

    def begin(z, carry):
        for ref in (buf_a, buf_b):
            clear_pads(ref, z + 1, cy)
        keep_layer(buf_a, z + 1, tiles_of(phi.at[z]))
        return carry

    lax.fori_loop(0, cz, begin, 0)
    for k in range(ITERS):
        here, there = (buf_a, buf_b) if k % 2 == 0 else (buf_b, buf_a)

        def layer(z, carry, here=here, there=there, last=k == ITERS - 1):
            value = total(tiles_of(src.at[z]), around(here, z + 1, cy), layer_of(here, z, cy), layer_of(here, z + 2, cy))
            if last:
                for c in range(chunks):
                    for b in range(blocks):
                        out[c, pl.ds(pl.multiple_of(z * cy, SUB) + SUB * b, SUB), :] = value[b][c]
            else:
                keep_layer(there, z + 1, value)
            return carry

        lax.fori_loop(0, cz, layer, 0)
    for c in copies:
        c.wait()


def alone(phi, src, matrix):
    cz, cy, nx = phi.shape
    chunks = nx // LANES
    return pl.pallas_call(
        alone_kernel,
        out_shape=(f32(chunks, cz * cy, LANES), f32(*matrix.shape)),
        in_specs=[VMEM, VMEM, ANY],
        out_specs=(VMEM, VMEM),
        scratch_shapes=[
            pltpu.VMEM((cz + 2, chunks, cy + 2 * PAD, LANES), jnp.float32),
            pltpu.VMEM((cz + 2, chunks, cy + 2 * PAD, LANES), jnp.float32),
            pltpu.SemaphoreType.DMA((4,)),
        ],
        compiler_params=pltpu.CompilerParams(vmem_limit_bytes=40 << 20),
        cost_estimate=pl.CostEstimate(flops=10 * ITERS * phi.size, bytes_accessed=12 * phi.size, transcendentals=0),
        name="alone",
    )(phi, src, matrix)


def respond(rows, outer, inner, mask, work, finish):
    for slot in range(SLOTS):
        clear_pads(work, slot, rows)
    o0, i0, o0_2, i0_2, o1_2, i1_2, o0_3, i0_3, i1_3, i2_3 = range(SLOTS)

    def keep(slot, *terms):
        keep_layer(work, slot, mask(total(*terms)))

    def at(slot):
        return layer_of(work, slot, rows)

    def near(slot):
        return around(work, slot, rows)

    keep(o0, outer(0))
    keep(i0, inner(0))
    keep(o0_2, outer(1), near(o0), at(i0))
    keep(i0_2, inner(1), near(i0), at(o0))
    keep(o1_2, at(o0))
    keep(i1_2, at(i0))
    keep(o0_3, outer(2), near(o0_2), at(o1_2), at(i0_2))
    keep(i0_3, inner(2), near(i0_2), at(o0_2), at(i1_2))
    keep(i1_3, near(i1_2), at(i0_2))
    keep(i2_3, at(i1_2))
    finish(0, total(inner(3), near(i0_3), at(o0_3), at(i1_3)))
    finish(1, total(near(i1_3), at(i0_3), at(i2_3)))
    finish(2, total(near(i2_3), at(i1_3)))
    finish(3, total(at(i2_3)))


SLOTS = 10


class Corner:
    def __init__(self, chunks):
        self.odd, col, has_far = whereabouts()
        self.right = col == 1
        self.has = (1.0, has_far.astype(jnp.float32))
        self.zero = [jnp.zeros((SUB, LANES), jnp.float32)] * chunks
        self.at_low = jnp.where(self.right, 1.0, 0.0)
        self.at_high = 1.0 - self.at_low

    def row(self, ref, at, i):
        return [spread(t, i) for t in load(ref, at, 1)[0]]

    def scale(self, tiles, factor):
        return [t * factor for t in tiles]

    def flank(self, rows, low):
        out, sub = self.zero, subs_of()
        for m, value in enumerate(rows):
            out = [jnp.where(sub == (SUB - 1 - m if low else m), v, o) for v, o in zip(value, out)]
        return out

    def near(self, ref, at, cy, m):
        return near_row(self.right, load(ref, at, 1)[0], load(ref, at + cy - SUB, 1)[0], m)

    def diag(self, ref, k, j=0, m=0):
        place = {(0, 0, 0): 0, (0, 1, 0): 1, (0, 2, 0): 2, (1, 0, 0): 3, (1, 1, 0): 4, (2, 0, 0): 5, (0, 0, 1): 6,
                 (0, 0, 2): 7, (1, 0, 1): 8}[(k, j, m)]
        return self.row(ref, place // SUB * SUB, place % SUB)

    def low_side(self, i):
        return self.odd if i == 0 else 1 - self.odd

    def interface(self, i, own, got, got_d, got_y, cz, cy, work, finish):
        low, blocks = self.low_side(i) == 1, cy // SUB

        def end_row(k):
            return [jnp.where(low, a, b) for a, b in zip(self.row(got_y, k * cz, 0), self.row(got_y, k * cz + cz - SUB, SUB - 1))]

        def driven(plane, rows):
            middle = [self.scale(t, self.has[i]) for t in plane]
            return ([self.scale(self.flank(rows, True), self.has[i] * self.at_low)] + middle
                    + [self.scale(self.flank(rows, False), self.has[i] * self.at_high)])

        def inner(k):
            return driven(load(got, k * cy, blocks), [self.diag(got_d, k, m=m) for m in range(3 - k)])

        def outer(k):
            rows = [end_row(k)] if k < 2 else []
            if k == 0:
                rows.append(self.row(got_y, 4 * cz, i))
            return driven(load(own, k * cy, blocks), rows)

        def mask(tiles):
            return [self.scale(tiles[0], self.at_low)] + tiles[1:-1] + [self.scale(tiles[-1], self.at_high)]

        respond(cy + 2 * SUB, outer, inner, mask, work, lambda j, tiles: finish(j, tiles[1:-1]))


def near_join_kernel(own, got, got_d, got_y, change, work):
    chunks = own.shape[0]
    cy = (own.shape[1] - SUB) // 4
    cz = (got_y.shape[1] - SUB) // 4
    Corner(chunks).interface(0, own, got, got_d, got_y, cz, cy, work, lambda j, tiles: store(change, j * cy, tiles))


def near_join(own, got, got_d, got_y):
    chunks, tall, _ = own.shape
    cy = (tall - SUB) // 4
    return pl.pallas_call(
        near_join_kernel,
        out_shape=f32(chunks, 4 * cy, LANES),
        in_specs=[VMEM] * 4,
        out_specs=VMEM,
        scratch_shapes=[pltpu.VMEM((SLOTS, chunks, cy + 2 * SUB + 2 * PAD, LANES), jnp.float32)],
        compiler_params=pltpu.CompilerParams(vmem_limit_bytes=24 << 20),
        name="near_join",
    )(own, got, got_d, got_y)


def join_kernel(
    row_of, lane_of, block, change, own_b, own_y, got_a, got_b, got_y, got_da, got_db,
    potential, values, pot, layers, columns, picked, sem,
):
    chunks, cells, _ = pot.shape
    cy = (own_b.shape[1] - SUB) // 4
    cz = cells // cy
    blocks = cy // SUB
    place = Corner(chunks)
    odd, right, has = place.odd, place.right, place.has
    fetch = pltpu.make_async_copy(block, pot, sem.at[0])
    fetch.start()
    sub = subs_of()

    def add_layer(i, j, tiles):
        start = pl.multiple_of(jnp.where(place.low_side(i) == 1, j, cz - 1 - j) * cy, SUB)
        for b in range(blocks):
            for c in range(chunks):
                where = (c, pl.ds(start + SUB * b, SUB), slice(None))
                pot[where] = pot[where] + tiles[b][c]

    def finish(j, tiles):
        if j == 0:
            fetch.wait()
            for old in range(4):
                add_layer(0, old, load(change, old * cy, blocks))
        add_layer(1, j, tiles)

    place.interface(1, own_b, got_b, got_db, got_y, cz, cy, layers, finish)

    low_has = jnp.where(odd == 1, has[0], has[1])
    high_has = jnp.where(odd == 1, has[1], has[0])

    def either(a, b):
        return [jnp.where(odd == 1, x, y) for x, y in zip(a, b)], [jnp.where(odd == 1, y, x) for x, y in zip(a, b)]

    def along(plane, pairs):
        low = place.scale(place.flank([p[0] for p in pairs], True), low_has)
        high = place.scale(place.flank([p[1] for p in pairs], False), high_has)
        return [low] + plane + [high]

    def inner_y(k):
        pairs = [either(place.diag(got_da, k, j=j), place.diag(got_db, k, j=j)) for j in range(3 - k)]
        return along(load(got_y, k * cz, cz // SUB), pairs)

    def outer_y(k):
        pairs = [either(place.near(got_a, k * cy, cy, 0), place.near(got_b, k * cy, cy, 0))] if k < 2 else []
        if k == 0:
            pairs.append(either(place.row(got_a, 4 * cy, 0), place.row(got_b, 4 * cy, 0)))
        return along(load(own_y, k * cz, cz // SUB), pairs)

    def mask_y(tiles):
        return [place.scale(tiles[0], low_has)] + tiles[1:-1] + [place.scale(tiles[-1], high_has)]

    flat = pot.reshape(chunks * cells, LANES)

    def finish_y(j, tiles):
        row = jnp.where(right, j, cy - 1 - j)
        for c in range(chunks):
            for half in range(cz // SUB):
                where = (pl.ds(c * cells + half * SUB * cy + row, SUB, stride=cy), slice(None))
                flat[where] = flat[where] + tiles[half + 1][c]

    respond(cz + 2 * SUB, outer_y, inner_y, mask_y, columns, finish_y)

    leave = [
        pltpu.make_async_copy(pot.at[c], potential.at[:, pl.ds(c * LANES, LANES)], sem.at[1 + c]) for c in range(chunks)
    ]
    for c in leave:
        c.start()

    wide = picked.shape[0]

    def pick(g, carry):
        for u in range(16):
            i = g * 16 + u
            picked[pl.ds(i, 1), :] = flat[pl.ds(row_of[i], 1), :]
        return carry

    lax.fori_loop(0, wide // 16, pick, 0)
    deep = lax.broadcasted_iota(jnp.int32, (LANES, LANES), 0)
    for q in range(wide // LANES):
        turned = picked[q * LANES:(q + 1) * LANES, :].T
        chosen = jnp.where(deep == lane_of[q:q + 1, :], turned, 0.0)
        line = jnp.sum(chosen, axis=0, keepdims=True)
        values[:, :, q * LANES:(q + 1) * LANES] = jnp.broadcast_to(line[None], (values.shape[0], 1, LANES))
    for c in leave:
        c.wait()


def join(row_of, lane_of, block, change, own, got, devices):
    chunks, cells, _ = block.shape
    cy = (own[0].shape[1] - SUB) // 4
    cz = cells // cy
    nodes = row_of.shape[0]
    nx = chunks * LANES
    return pl.pallas_call(
        join_kernel,
        out_shape=(f32(cells, nx), f32(devices, 1, nodes)),
        in_specs=[SMEM, VMEM, ANY] + [VMEM] * 8,
        out_specs=(ANY, VMEM),
        scratch_shapes=[
            pltpu.VMEM((chunks, cells, LANES), jnp.float32),
            pltpu.VMEM((SLOTS, chunks, cy + 2 * SUB + 2 * PAD, LANES), jnp.float32),
            pltpu.VMEM((SLOTS, chunks, cz + 2 * SUB + 2 * PAD, LANES), jnp.float32),
            pltpu.VMEM((nodes, LANES), jnp.float32),
            pltpu.SemaphoreType.DMA((1 + chunks,)),
        ],
        compiler_params=pltpu.CompilerParams(vmem_limit_bytes=24 << 20),
        name="join",
    )(row_of, lane_of, block, change, *own, *got)


def window_kernel(table_ref, slot_ref, matrix_ref, keep_ref, send_ref, rows_ref):
    rows, columns = matrix_ref.shape
    owners, _, width = table_ref.shape
    parts = width // LANES
    count = owners * parts
    for q in range(parts):
        rows_ref[pl.ds(q, owners, stride=parts), :] = table_ref[:, 0, q * LANES:(q + 1) * LANES]
    turned = rows_ref[...].T
    high_part = turned.astype(jnp.bfloat16)
    low_part = (turned - high_part.astype(jnp.float32)).astype(jnp.bfloat16)
    halves = jnp.concatenate([high_part, low_part], axis=0)
    number = lax.broadcasted_iota(jnp.int32, (count, LANES), 0)
    deep = lax.broadcasted_iota(jnp.int32, (LANES, LANES), 0)
    blocks = rows // 16
    chunks = columns // LANES
    each = WINDOW_CHUNKS
    col = lax.axis_index("cols").astype(jnp.int32)
    first = col * chunks
    start = [pl.multiple_of(side * (rows // 2), SUB) for side in (col, 1 - col)]

    def part(i, accs):
        accs = list(accs)
        slots = [slot_ref[pl.ds(first + i * each + u, 1), :] for u in range(each)]
        hot = jnp.concatenate(
            [jnp.where(number == jnp.broadcast_to(s >> 7, (count, LANES)), 1.0, 0.0).astype(jnp.bfloat16) for s in slots],
            axis=1,
        )
        found = jnp.dot(halves, hot, preferred_element_type=jnp.float32)
        for u in range(each):
            both = found[:LANES, u * LANES:(u + 1) * LANES] + found[LANES:, u * LANES:(u + 1) * LANES]
            lane = jnp.broadcast_to(slots[u] & (LANES - 1), (LANES, LANES))
            line = jnp.sum(jnp.where(deep == lane, both, 0.0), axis=0, keepdims=True)
            value = jnp.broadcast_to(line, (SUB, LANES))
            at = i * (each * LANES) + u * LANES
            at = at if isinstance(i, int) else pl.multiple_of(at, LANES)
            for side in range(2):
                for b in range(blocks):
                    tile = matrix_ref[pl.ds(start[side] + SUB * b, SUB), pl.ds(at, LANES)]
                    accs[side * blocks + b] = accs[side * blocks + b] + tile * value
        return tuple(accs)

    zero = jnp.zeros((SUB, LANES), jnp.float32)
    accs = (zero,) * (2 * blocks)
    if chunks // each <= 4:
        for i in range(chunks // each):
            accs = part(i, accs)
    else:
        accs = lax.fori_loop(0, chunks // each, part, accs)
    for side, out in enumerate((keep_ref, send_ref)):
        tall = jnp.concatenate(list(accs[side * blocks:(side + 1) * blocks]) + [zero] * (16 - blocks), axis=0)
        out[...] = jnp.sum(tall.T, axis=0, keepdims=True)


WINDOW_CHUNKS = 24


def window_product(table, slots, matrix):
    rows, columns = matrix.shape
    assert columns % (WINDOW_CHUNKS * LANES) == 0 and rows % 16 == 0 and rows <= 2 * LANES
    out = f32(1, LANES)
    return pl.pallas_call(
        window_kernel,
        out_shape=(out, out),
        in_specs=[VMEM, VMEM, VMEM],
        out_specs=(VMEM, VMEM),
        scratch_shapes=[pltpu.VMEM((table.size // LANES, LANES), jnp.float32)],
        compiler_params=pltpu.CompilerParams(vmem_limit_bytes=32 << 20),
        name="window",
    )(table, slots, matrix)


def routes(n):
    def across(r):
        other = r + 1 if r % 2 else r - 1
        return other if 0 <= other < n else None

    near = [(r, r ^ 1) for r in range(n)]
    far, near_diag, far_diag = [], [], []
    for r in range(n):
        for c in range(2):
            other = across(r)
            far.append((r * 2 + c, r * 2 + 1 - c if other is None else other * 2 + c))
            near_diag.append((r * 2 + c, (r ^ 1) * 2 + 1 - c))
            far_diag.append((r * 2 + c, (r if other is None else other) * 2 + 1 - c))
    return near, far, near_diag, far_diag


def local(phi_start, source, owner_voxel, column_slot, layer_matrix):
    n = lax.axis_size("rows")
    assert lax.axis_size("cols") == 2 and n % 2 == 0
    devices = 2 * n
    cz, cy, nx = phi_start.shape
    near, far, near_diag, far_diag = routes(n)
    swap = [(0, 1), (1, 0)]

    pack_b, diag_b = far_face(phi_start, source)
    got_b = lax.ppermute(pack_b, BOTH, far)
    pack_a, pack_y, diag_a = near_face(diag_b, phi_start, source)
    got_db = lax.ppermute(diag_b, BOTH, far_diag)
    got_y = lax.ppermute(pack_y, "cols", swap)
    got_da = lax.ppermute(diag_a, BOTH, near_diag)
    got_a = lax.ppermute(pack_a, "rows", near)
    block, matrix = alone(phi_start, source, layer_matrix)
    x = owner_voxel % nx
    row_of = (x // LANES) * (cz * cy) + owner_voxel // nx
    lane_of = (x % LANES).reshape(-1, LANES)
    change = near_join(pack_a, got_a, got_da, got_y)
    potential, values = join(
        row_of, lane_of, block, change, (pack_b, pack_y), (got_a, got_b, got_y, got_da, got_db), devices
    )
    table = lax.all_to_all(values, BOTH, 0, 0, tiled=True)
    slots = column_slot.reshape(-1, LANES)
    keep, send = window_product(table, slots, matrix)
    received = lax.ppermute(send, "cols", swap)
    half = layer_matrix.shape[0] // 2
    return potential.reshape(cz, cy, nx), (keep + received)[0, :half]


def solution(mesh):
    return jax.shard_map(
        local,
        mesh=mesh,
        in_specs=(
            P("rows", "cols", None),
            P("rows", "cols", None),
            P(("rows", "cols")),
            P(),
            P("rows", "cols"),
        ),
        out_specs=(P("rows", "cols", None), P(("rows", "cols"))),
        check_vma=False,
    )
```

time: 252 us -> 46.3 us (0.18)
  local copies, waits for them, and re-layouts: 79 us -> 0.54 us
  blocking collectives: 76.3 us -> 13.7 us
  starting transfers between devices: 49.2 us -> 6.76 us
  other arithmetic: 29.9 us -> 0.03 us
  Pallas kernels: 0 us -> 21.2 us
  waiting for transfers between devices: 9.86 us -> 3.18 us
  matrix products: 5.54 us -> 0 us
    gather x2 -> x0, local copies, waits for them, and re-layouts: 72.5 us -> none  [the longest x1 68 us: local(): trace_block = gathered[block_slots]]
    all_gather x1 -> x0, blocking collectives: 71.4 us -> none  [local(): gathered = lax.all_gather(node_values, ('rows', 'cols'), axis=0, tiled=True)]
    ppermute x16 -> x6, starting transfers between devices: 49.2 us -> 6.76 us  [the longest x1 2.73 us: local(): got_b = lax.ppermute(pack_b, BOTH, far)]
    pallas_call x0 -> x6, Pallas kernels: none -> 21.2 us  [the longest x1 10.1 us: alone(): pl.pallas_call(alone_kernel, out_shape=(f32(chunks, cz * cy, LANES), f32(...]
    div x4 -> x0, other arithmetic: 17 us -> none  [local(): potential = (source + neighbour_sum(padded)) / 6.0]
    all_to_all x0 -> x1, blocking collectives: none -> 13.7 us  [local(): table = lax.all_to_all(values, BOTH, 0, 0, tiled=True)]
    concatenate x7 -> x0, other arithmetic: 12.9 us -> none  [with_halo(): value = jnp.concatenate([before, value, after], axis=dim)]
    ppermute x16 -> x6, waiting for transfers between devices: 9.86 us -> 3.18 us  [the longest x1 3.16 us: local(): received = lax.ppermute(send, 'cols', swap)]
  transfers between devices with their start and end apart: 16 -> 6, of which waited for: 8 -> 1; matrix products, arithmetic and copies ran while one was open for 1% -> 0% of each run, Pallas kernels for 0% -> 23%
where the time goes in v3:
time: 46.3 us; the launch traced here: 46.1 us
  Pallas kernels  21.2 us (46%)
  blocking collectives  13.7 us (30%)
  starting transfers between devices  6.76 us (15%)
  waiting for transfers between devices  3.18 us (7%)
  between operations  0.77 us (2%)
  local copies, waits for them, and re-layouts  0.54 us (1%)
    all_to_all x1, blocking collectives, local(): table = lax.all_to_all(values, BOTH, 0, 0, tiled=True)  13.7 us
    pallas_call x1, Pallas kernels, alone(): pl.pallas_call(alone_kernel, out_shape=(f32(chunks, cz * cy, LANES), f32(...  10.1 us
    pallas_call x1, Pallas kernels, join(): pl.pallas_call(join_kernel, out_shape=(f32(cells, nx), f32(devices, 1, no...  3.55 us
    pallas_call x1, Pallas kernels, window_product(): pl.pallas_call(window_kernel, out_shape=(out, out), in_specs=[VMEM, VMEM,...  3.2 us
    ppermute x1, waiting for transfers between devices, local(): received = lax.ppermute(send, 'cols', swap)  3.16 us
    pallas_call x1, Pallas kernels, far_face(): pl.pallas_call(far_face_kernel, out_shape=(f32(chunks, 4 * cy + SUB, LANE...  2.89 us
    ppermute x1, starting transfers between devices, local(): got_b = lax.ppermute(pack_b, BOTH, far)  2.73 us
    ppermute x1, starting transfers between devices, local(): got_y = lax.ppermute(pack_y, 'cols', swap)  1.82 us
  transfers between devices with their start and end apart: 6, of which 1 were waited for; matrix products, arithmetic and copies ran while one was open for 0% of the time, Pallas kernels for 23%

profile of v3, /device:TPU:0, one launch (start us, length us, event | category | flops | bytes accessed | tf_op | source)
XLA Modules:
  0.0 46.1 jit_solution(4714249257468904121)
XLA Ops:
  0.6 2.9 %far_face.1 = (f32[3,392,128]{2,1,0:T(8,128)}, f32[3,16,128]{2,1,0:T(8,128)}) custom-call(f32[16,96,384]{2,1,0:T(8,128)} %phi.5, f32[16,96,384]{2,1,0:T(8,128)} %src.5), custom_call_target="tpu_custom_call" | custom-call | tf_op jit(solution)/shard_map/far_face/pallas_call | solution.py:197
  3.5 0.0 copy-done.1
  3.6 0.0 copy-start.2
  3.6 0.0 copy-start.4
  3.6 0.7 %near_face.1 = (f32[3,392,128]{2,1,0:T(8,128)S(1)}, f32[3,72,128]{2,1,0:T(8,128)S(1)}, f32[3,16,128]{2,1,0:T(8,128)S(1)}) custom-call(f32[3,16,128]{2,1,0:T(8,128)} %get-tuple-element.14.after, f32[16,96,384]{2,1,0:T(8,128)S(1)} %copy-done, f32[16,96,384]{2,1,0:T(8,128)S(1)} %copy-done.1), custom_call_target="tpu_custom_call" | custom-call | tf_op jit(solution)/shard_map/near_face/pallas_call | solution.py:256
  4.3 0.5 %collective-permute-start = (f32[3,392,128]{2,1,0:T(8,128)S(1)}, f32[3,392,128]{2,1,0:T(8,128)S(1)}, u32[]{:S(2)}, u32[]{:S(2)}) collective-permute-start(f32[3,392,128]{2,1,0:T(8,128)S(1)} %get-tuple-element.15.own), channel_id=1, source_target_pairs={{0,2},{2,0},{4,6},{6,4},{8,10},{10,8},{12,14},{14,12},{16,18},{18,... | collective-permute-start | bytes 1806344 | tf_op jit(solution)/shard_map/ppermute | solution.py:657
  4.8 2.7 %collective-permute-start.3 = (f32[3,392,128]{2,1,0:T(8,128)S(1)}, f32[3,392,128]{2,1,0:T(8,128)S(1)}, u32[]{:S(2)}, u32[]{:S(2)}) collective-permute-start(f32[3,392,128]{2,1,0:T(8,128)S(1)} %copy-done.2), channel_id=1, source_target_pairs={{0,1},{1,0},{2,4},{3,5},{4,2},{5,3},{6,8},{7,9},{8,6},{9,7},{10,12... | collective-permute-start | bytes 1806344 | tf_op jit(solution)/shard_map/ppermute | solution.py:652
  7.6 0.0 collective-permute-start.4
  7.6 1.2 %collective-permute-start.1 = (f32[3,16,128]{2,1,0:T(8,128)S(1)}, f32[3,16,128]{2,1,0:T(8,128)S(1)}, u32[]{:S(2)}, u32[]{:S(2)}) collective-permute-start(f32[3,16,128]{2,1,0:T(8,128)S(1)} %get-tuple-element.16), channel_id=1, source_target_pairs={{0,3},{1,2},{2,1},{3,0},{4,7},{5,6},{6,5},{7,4},{8,11},{9,10},{10,... | collective-permute-start | bytes 73736 | tf_op jit(solution)/shard_map/ppermute | solution.py:656
  8.8 1.8 %collective-permute-start.2 = (f32[3,72,128]{2,1,0:T(8,128)S(1)}, f32[3,72,128]{2,1,0:T(8,128)S(1)}, u32[]{:S(2)}, u32[]{:S(2)}) collective-permute-start(f32[3,72,128]{2,1,0:T(8,128)S(1)} %get-tuple-element.17.own_y), channel_id=1, source_target_pairs={{0,1},{1,0},{2,3},{3,2},{4,5},{5,4},{6,7},{7,6},{8,9},{9,8},{10,11... | collective-permute-start | bytes 331784 | tf_op jit(solution)/shard_map/ppermute | solution.py:655
  10.7 10.1 %alone.1 = (f32[3,1536,128]{2,1,0:T(8,128)S(1)}, f32[96,12288]{1,0:T(8,128)S(1)}) custom-call(f32[16,96,384]{2,1,0:T(8,128)S(1)} %copy-done, f32[16,96,384]{2,1,0:T(8,128)S(1)} %copy-done.1, f32[96,12288]{1,0:T(8,128)} %matrix.1), custom_call_target="tpu_custom_call" | custom-call | flops 23592960 | bytes 7077888 | tf_op jit(solution)/shard_map/alone/pallas_call | solution.py:315
  20.7 0.0 collective-permute-done.1.got_d.got_da
  20.7 0.0 collective-permute-done.2.got_y
  20.8 0.0 collective-permute-done.got.got_a
  20.8 0.8 %near_join.1.change = f32[3,384,128]{2,1,0:T(8,128)S(1)} custom-call(f32[3,392,128]{2,1,0:T(8,128)S(1)} %get-tuple-element.15.own, f32[3,392,128]{2,1,0:T(8,128)S(1)} %collective-permute-done.got.got_a, f32[3,16,128]{2,1,0:T(8,128)S(1)} %collective-permute-done.1.got_d.got_da, f32[3,72,128]{2,1,0:T(8,128)S(1)} %collective-permute-done.2.got_y), custom_call_target="tpu_custom_call" | custom-call | tf_op jit(solution)/shard_map/near_join/pallas_call | solution.py:432
  21.5 0.0 collective-permute-done.4.got_db
  21.5 0.0 collective-permute-done.3.got_b
  21.6 0.0 copy-start.3
  21.6 3.6 %join.1 = (f32[1536,384]{1,0:T(8,128)}, f32[32,1,768]{2,1,0:T(1,128)S(1)}) custom-call(s32[768]{0:T(1024)S(1)} %get-tuple-element.25.row_of, s32[6,128]{1,0:T(8,128)S(1)} %get-tuple-element.24.lane_of, f32[3,1536,128]{2,1,0:T(8,128)S(1)} %get-tuple-element.13.block, f32[3,384,128]{2,1,0:T(8,128)S(1)} %near_join.1.change, f32[3,392,128]{2,1,0:T(8,128)S(1)} %copy-done.2, ...), custom_call_target="tpu_custom_call" | custom-call | tf_op jit(solution)/shard_map/join/pallas_call | solution.py:539
  25.1 13.7 %all_to_all.5.table_ref = f32[32,1,768]{2,1,0:T(1,128)S(1)} all-to-all(f32[32,1,768]{2,1,0:T(1,128)S(1)} %get-tuple-element.20), channel_id=1, replica_groups=mesh['rows'=16,'cols'=2] {'rows','cols'}, dimensions={0} | all-to-all | bytes 196608 | tf_op jit(solution)/shard_map/all_to_all | solution.py:666
  38.8 3.2 %window.1 = (f32[1,128]{1,0:T(1,128)S(1)}, f32[1,128]{1,0:T(1,128)S(1)}) custom-call(f32[32,1,768]{2,1,0:T(1,128)S(1)} %all_to_all.5.table_ref, s32[192,128]{1,0:T(8,128)S(1)} %bitcast.6, f32[96,12288]{1,0:T(8,128)S(1)} %get-tuple-element.21.matrix_ref), custom_call_target="tpu_custom_call" | custom-call | tf_op jit(solution)/shard_map/window/pallas_call | solution.py:616
  42.0 0.4 collective-permute-start.5
  42.5 3.2 %collective-permute-done.5 = f32[1,128]{1,0:T(1,128)S(1)} collective-permute-done((f32[1,128]{1,0:T(1,128)S(1)}, f32[1,128]{1,0:T(1,128)S(1)}, u32[]{:S(2)}, u32[]{:S(2)}) %collective-permute-start.5) | collective-permute-done | bytes 544 | tf_op jit(solution)/shard_map/ppermute | solution.py:669
  45.6 0.5 %slice_bitcast_fusion = f32[48]{0:T(128)} fusion(f32[1,128]{1,0:T(1,128)S(1)} %add.21), kind=kLoop, calls=%fused_computation.16 | loop fusion | bytes 384 | tf_op jit(solution)/shard_map/squeeze | solution.py:671
  (8 shorter events, 0.0 us)
Async XLA Ops:
  0.6 2.9 %copy-start.1 = (f32[16,96,384]{2,1,0:T(8,128)S(1)}, f32[16,96,384]{2,1,0:T(8,128)}, u32[]{:S(2)}) copy-start(f32[16,96,384]{2,1,0:T(8,128)} %src.5) | copy-start | bytes 7077892
  0.6 2.9 %copy-start = (f32[16,96,384]{2,1,0:T(8,128)S(1)}, f32[16,96,384]{2,1,0:T(8,128)}, u32[]{:S(2)}) copy-start(f32[16,96,384]{2,1,0:T(8,128)} %phi.5) | copy-start | bytes 7077892
  3.6 1.3 %copy-start.2 = (f32[3,392,128]{2,1,0:T(8,128)S(1)}, f32[3,392,128]{2,1,0:T(8,128)}, u32[]{:S(2)}) copy-start(f32[3,392,128]{2,1,0:T(8,128)} %get-tuple-element.18.own_b) | copy-start | bytes 1806340
  3.6 7.1 %copy-start.4 = (s32[768]{0:T(1024)S(1)}, s32[768]{0:T(1024)}, u32[]{:S(2)}) copy-start(s32[768]{0:T(1024)} %param.7) | copy-start | bytes 9220
  4.3 16.4 %collective-permute-start = (f32[3,392,128]{2,1,0:T(8,128)S(1)}, f32[3,392,128]{2,1,0:T(8,128)S(1)}, u32[]{:S(2)}, u32[]{:S(2)}) collective-permute-start(f32[3,392,128]{2,1,0:T(8,128)S(1)} %get-tuple-element.15.own), channel_id=1, source_target_pairs={{0,2},{2,0},{4,6},{6,4},{8,10},{10,8},{12,14},{14,12},{16,18},{18,... | collective-permute-start | bytes 1806344 | tf_op jit(solution)/shard_map/ppermute | solution.py:657
  4.8 16.7 %collective-permute-start.3 = (f32[3,392,128]{2,1,0:T(8,128)S(1)}, f32[3,392,128]{2,1,0:T(8,128)S(1)}, u32[]{:S(2)}, u32[]{:S(2)}) collective-permute-start(f32[3,392,128]{2,1,0:T(8,128)S(1)} %copy-done.2), channel_id=1, source_target_pairs={{0,1},{1,0},{2,4},{3,5},{4,2},{5,3},{6,8},{7,9},{8,6},{9,7},{10,12... | collective-permute-start | bytes 1806344 | tf_op jit(solution)/shard_map/ppermute | solution.py:652
  7.6 14.0 %collective-permute-start.4 = (f32[3,16,128]{2,1,0:T(8,128)}, f32[3,16,128]{2,1,0:T(8,128)S(1)}, u32[]{:S(2)}, u32[]{:S(2)}) collective-permute-start(f32[3,16,128]{2,1,0:T(8,128)} %get-tuple-element.14.after), channel_id=1, source_target_pairs={{0,1},{1,0},{2,5},{3,4},{4,3},{5,2},{6,9},{7,8},{8,7},{9,6},{10,13... | collective-permute-start | bytes 73736 | tf_op jit(solution)/shard_map/ppermute | solution.py:654
  7.6 13.1 %collective-permute-start.1 = (f32[3,16,128]{2,1,0:T(8,128)S(1)}, f32[3,16,128]{2,1,0:T(8,128)S(1)}, u32[]{:S(2)}, u32[]{:S(2)}) collective-permute-start(f32[3,16,128]{2,1,0:T(8,128)S(1)} %get-tuple-element.16), channel_id=1, source_target_pairs={{0,3},{1,2},{2,1},{3,0},{4,7},{5,6},{6,5},{7,4},{8,11},{9,10},{10,... | collective-permute-start | bytes 73736 | tf_op jit(solution)/shard_map/ppermute | solution.py:656
  8.8 11.9 %collective-permute-start.2 = (f32[3,72,128]{2,1,0:T(8,128)S(1)}, f32[3,72,128]{2,1,0:T(8,128)S(1)}, u32[]{:S(2)}, u32[]{:S(2)}) collective-permute-start(f32[3,72,128]{2,1,0:T(8,128)S(1)} %get-tuple-element.17.own_y), channel_id=1, source_target_pairs={{0,1},{1,0},{2,3},{3,2},{4,5},{5,4},{6,7},{7,6},{8,9},{9,8},{10,11... | collective-permute-start | bytes 331784 | tf_op jit(solution)/shard_map/ppermute | solution.py:655
  21.6 17.3 %copy-start.3 = (s32[24576]{0:T(1024)S(1)}, s32[24576]{0:T(1024)}, u32[]{:S(2)}) copy-start(s32[24576]{0:T(1024)} %param.8) | copy-start | bytes 294916
  42.0 3.6 %collective-permute-start.5 = (f32[1,128]{1,0:T(1,128)S(1)}, f32[1,128]{1,0:T(1,128)S(1)}, u32[]{:S(2)}, u32[]{:S(2)}) collective-permute-start(f32[1,128]{1,0:T(1,128)S(1)} %get-tuple-element.23), channel_id=1, source_target_pairs={{0,1},{1,0},{2,3},{3,2},{4,5},{5,4},{6,7},{7,6},{8,9},{9,8},{10,11... | collective-permute-start | bytes 1544 | tf_op jit(solution)/shard_map/ppermute | solution.py:669

commit v4 on v3

--- a/solution.py
+++ b/solution.py
@@ -11,6 +11,7 @@
 LANES = 128
 SUB = 8
 SIXTH = 1.0 / 6.0
+LITTLE = pl.CostEstimate(flops=1, bytes_accessed=1, transcendentals=0)
 FIRST_LIMIT = 58 << 20
 BOTH = ("rows", "cols")
 VMEM = pl.BlockSpec(memory_space=pltpu.VMEM)
@@ -108,29 +109,28 @@
     return [jnp.where(right, spread(f, m), spread(t, SUB - 1 - m)) for f, t in zip(first, last)]
 
 
-def solve_face(first, source, work, pack, rows):
-    blocks = rows // SUB
-    start = [layer_of(*first(j), rows) for j in range(4)]
-    store(pack, 0, start[0])
+def solve_face(first, source, p0, work, put, rows):
+    first(0)
+    put(0, layer_of(p0, 0, rows))
     for j in range(3):
-        keep_layer(work, j, total(source(j), around(*first(j), rows), start[j + 1], start[j - 1] if j else None))
+        first(j + 1)
+        back = layer_of(p0, j - 1, rows) if j else None
+        keep_layer(work, j, total(source(j), around(p0, j, rows), layer_of(p0, j + 1, rows), back))
     one = [layer_of(work, j, rows) for j in range(3)]
-    store(pack, rows, one[0])
+    put(1, one[0])
     for j in range(2):
         keep_layer(work, 3 + j, total(source(j), around(work, j, rows), one[j + 1], one[j - 1] if j else None))
     two = [layer_of(work, 3 + j, rows) for j in range(2)]
-    store(pack, 2 * rows, two[0])
-    store(pack, 3 * rows, total(source(0), around(work, 3, rows), two[1]))
+    put(2, two[0])
+    put(3, total(source(0), around(work, 3, rows), two[1]))
 
 
 def fetch_face(phi, src, low, raw, sem):
     last = phi.shape[0] - 1
-    copies = []
-    for j in range(4):
+    copies = {}
+    for i, j in ((0, 0), (0, 1), (1, 0), (0, 2), (1, 1), (0, 3), (1, 2)):
         z = jnp.where(low == 1, j, last - j)
-        copies.append(pltpu.make_async_copy(phi.at[z], raw.at[0, j], sem.at[0, j]))
-        if j < 3:
-            copies.append(pltpu.make_async_copy(src.at[z], raw.at[1, j], sem.at[1, j]))
+        copies[i, j] = pltpu.make_async_copy((src if i else phi).at[z], raw.at[i, j], sem.at[i, j])
     return copies
 
 
@@ -139,15 +139,15 @@
     return [[ref[SUB * b:SUB * b + SUB, c * LANES:(c + 1) * LANES] for c in range(wide // LANES)] for b in range(rows // SUB)]
 
 
-def send_face(right, source, p0, work, pack, diag, cy):
+def send_face(right, first, source, p0, work, put, diag, cy):
     chunks = p0.shape[1]
-    solve_face(lambda j: (p0, j), source, work, pack, cy)
+    solve_face(first, source, p0, work, put, cy)
 
     def near(ref, slot, m):
         edges = [[ref[slot, c, pl.ds(at, SUB), :] for c in range(chunks)] for at in (PAD, PAD + cy - SUB)]
         return near_row(right, *edges, m)
 
-    store(pack, 4 * cy, [near(p0, 1, 0)])
+    put(4, [near(p0, 1, 0)])
     store(diag, 0, [stack([
         near(p0, 0, 0), near(p0, 1, 0), near(p0, 2, 0), near(work, 0, 0), near(work, 1, 0),
         near(work, 3, 0), near(p0, 0, 1), near(p0, 0, 2),
@@ -159,17 +159,23 @@
     cy = phi.shape[1]
     odd, col, _ = whereabouts()
     copies = fetch_face(phi, src, 1 - odd, raw, sem)
-    for c in copies:
+    for c in copies.values():
         c.start()
     for i in range(4):
         clear_pads(p0, i, cy)
     for i in range(5):
         clear_pads(work, i, cy)
-    for c in copies:
-        c.wait()
-    for j in range(4):
+    def first(j):
+        copies[0, j].wait()
         keep_layer(p0, j, tiles_of(raw.at[0, j]))
-    send_face(col == 1, lambda j: tiles_of(raw.at[1, j]), p0, work, pack, diag, cy)
+
+    def source(j, seen=set()):
+        if j not in seen:
+            seen.add(j)
+            copies[1, j].wait()
+        return tiles_of(raw.at[1, j])
+
+    send_face(col == 1, first, source, p0, work, lambda k, tiles: store(pack, k * cy, tiles), diag, cy)
 
 
 def f32(*shape):
@@ -220,9 +226,17 @@
     def layer(j):
         return jnp.where(odd == 1, j, cz - 1 - j)
 
-    for j in range(4):
+    def first(j):
         keep_layer(p0, j, tiles_of(phi.at[layer(j)]))
-    send_face(right, lambda j: tiles_of(src.at[layer(j)]), p0, work, pack, diag, cy)
+
+    def put(k, tiles):
+        if k < 4:
+            store(pack, k * cy, tiles)
+        else:
+            for c, tile in enumerate(tiles[0]):
+                pack[c, k * cy:k * cy + 1, :] = tile[:1, :]
+
+    send_face(right, first, lambda j: tiles_of(src.at[layer(j)]), p0, work, put, diag, cy)
     at = pl.multiple_of(jnp.where(right, 0, cy - SUB), SUB)
     for i, whole in enumerate((phi, src)):
         for z in range(cz):
@@ -234,7 +248,7 @@
         row = jnp.where(right, m, SUB - 1 - m)
         return flat[pl.ds((i * chunks + c) * cz * SUB + row, cz, stride=SUB), :]
 
-    for m in range(4):
+    def first_plane(m):
         for c in range(chunks):
             edge_p[m, c, PAD:PAD + cz, :] = plane(0, c, m)
 
@@ -242,7 +256,7 @@
         whole = [plane(1, c, m) for c in range(chunks)]
         return [[w[SUB * b:SUB * b + SUB, :] for w in whole] for b in range(cz // SUB)]
 
-    solve_face(lambda j: (edge_p, j), source, edge_w, pack_y, cz)
+    solve_face(first_plane, source, edge_p, edge_w, lambda k, tiles: store(pack_y, k * cz, tiles), cz)
     ends = [[edge_p[1, c, pl.ds(PAD + i, 1), :] for c in range(chunks)] for i in (0, cz - 1)]
     ends = [[jnp.broadcast_to(t, (SUB, LANES)) for t in row] for row in ends]
     own = [[jnp.where(odd == 1, a, b) for a, b in zip(*ends)], [jnp.where(odd == 1, b, a) for a, b in zip(*ends)]]
@@ -255,7 +269,9 @@
     tall = cz + 2 * PAD
     return pl.pallas_call(
         near_face_kernel,
-        out_shape=(f32(chunks, 4 * cy + SUB, LANES), f32(chunks, 4 * cz + SUB, LANES), f32(chunks, 2 * SUB, LANES)),
+        out_shape=(
+            f32(chunks, 4 * cy + 1, LANES), f32(chunks, 4 * cz + SUB, LANES), f32(chunks, 2 * SUB, LANES),
+        ),
         in_specs=[ANY, VMEM, VMEM],
         out_specs=(VMEM,) * 3,
         scratch_shapes=face_scratch(chunks, cy)[1:] + [
@@ -264,11 +280,12 @@
             pltpu.VMEM((5, chunks, tall, LANES), jnp.float32),
         ],
         compiler_params=pltpu.CompilerParams(vmem_limit_bytes=24 << 20),
+        cost_estimate=LITTLE,
         name="near_face",
     )(after, phi, src)
 
 
-def alone_kernel(phi, src, matrix, out, matrix_out, buf_a, buf_b, sem):
+def alone_kernel(phi, src, matrix, slots, out, matrix_out, hot, buf_a, buf_b, sem):
     cz, cy, nx = phi.shape
     blocks, chunks = cy // SUB, nx // LANES
     pieces = 4
@@ -304,28 +321,35 @@
                 keep_layer(there, z + 1, value)
             return carry
 
-        lax.fori_loop(0, cz, layer, 0)
+        lax.fori_loop(0, cz, layer, 0, unroll=True)
+    if hot.shape[0] == slots.shape[0]:
+        first = lax.axis_index("cols").astype(jnp.int32) * (hot.shape[1] // LANES)
+        number = lax.broadcasted_iota(jnp.int32, (hot.shape[0], LANES), 0)
+        for u in range(hot.shape[1] // LANES):
+            hot[:, u * LANES:(u + 1) * LANES] = one_hot(slots[pl.ds(first + u, 1), :], number)
     for c in copies:
         c.wait()
 
 
-def alone(phi, src, matrix):
+def alone(phi, src, matrix, slots):
     cz, cy, nx = phi.shape
     chunks = nx // LANES
+    count, columns = slots.shape[0], matrix.shape[1]
+    ahead = (count, columns) if count * columns <= 4 << 20 else (2 * SUB, LANES)
     return pl.pallas_call(
         alone_kernel,
-        out_shape=(f32(chunks, cz * cy, LANES), f32(*matrix.shape)),
-        in_specs=[VMEM, VMEM, ANY],
-        out_specs=(VMEM, VMEM),
+        out_shape=(f32(chunks, cz * cy, LANES), f32(*matrix.shape), jax.ShapeDtypeStruct(ahead, jnp.bfloat16)),
+        in_specs=[VMEM, VMEM, ANY, VMEM],
+        out_specs=(VMEM,) * 3,
         scratch_shapes=[
             pltpu.VMEM((cz + 2, chunks, cy + 2 * PAD, LANES), jnp.float32),
             pltpu.VMEM((cz + 2, chunks, cy + 2 * PAD, LANES), jnp.float32),
             pltpu.SemaphoreType.DMA((4,)),
         ],
-        compiler_params=pltpu.CompilerParams(vmem_limit_bytes=40 << 20),
-        cost_estimate=pl.CostEstimate(flops=10 * ITERS * phi.size, bytes_accessed=12 * phi.size, transcendentals=0),
+        compiler_params=pltpu.CompilerParams(vmem_limit_bytes=20 << 20),
+        cost_estimate=LITTLE,
         name="alone",
-    )(phi, src, matrix)
+    )(phi, src, matrix, slots)
 
 
 def respond(rows, outer, inner, mask, work, finish):
@@ -361,6 +385,11 @@
 SLOTS = 10
 
 
+def planes(refs, cy):
+    each = 4 // len(refs)
+    return lambda k: load(refs[k // each], k % each * cy, cy // SUB)
+
+
 class Corner:
     def __init__(self, chunks):
         self.odd, col, has_far = whereabouts()
@@ -393,6 +422,13 @@
     def low_side(self, i):
         return self.odd if i == 0 else 1 - self.odd
 
+    def add_layer(self, pot, i, j, cz, cy, tiles):
+        start = pl.multiple_of(jnp.where(self.low_side(i) == 1, j, cz - 1 - j) * cy, SUB)
+        for b, row in enumerate(tiles):
+            for c, tile in enumerate(row):
+                where = (c, pl.ds(start + SUB * b, SUB), slice(None))
+                pot[where] = pot[where] + tile
+
     def interface(self, i, own, got, got_d, got_y, cz, cy, work, finish):
         low, blocks = self.low_side(i) == 1, cy // SUB
 
@@ -405,13 +441,13 @@
                     + [self.scale(self.flank(rows, False), self.has[i] * self.at_high)])
 
         def inner(k):
-            return driven(load(got, k * cy, blocks), [self.diag(got_d, k, m=m) for m in range(3 - k)])
+            return driven(got(k), [self.diag(got_d, k, m=m) for m in range(3 - k)])
 
         def outer(k):
             rows = [end_row(k)] if k < 2 else []
             if k == 0:
                 rows.append(self.row(got_y, 4 * cz, i))
-            return driven(load(own, k * cy, blocks), rows)
+            return driven(own(k), rows)
 
         def mask(tiles):
             return [self.scale(tiles[0], self.at_low)] + tiles[1:-1] + [self.scale(tiles[-1], self.at_high)]
@@ -419,29 +455,39 @@
         respond(cy + 2 * SUB, outer, inner, mask, work, lambda j, tiles: finish(j, tiles[1:-1]))
 
 
-def near_join_kernel(own, got, got_d, got_y, change, work):
-    chunks = own.shape[0]
-    cy = (own.shape[1] - SUB) // 4
-    cz = (got_y.shape[1] - SUB) // 4
-    Corner(chunks).interface(0, own, got, got_d, got_y, cz, cy, work, lambda j, tiles: store(change, j * cy, tiles))
-
-
-def near_join(own, got, got_d, got_y):
+def near_join_kernel(own, got, got_d, got_y, block, out, work):
+    chunks, cells, _ = block.shape
+    cy = (own.shape[1] - 1) // 4
+    cz = cells // cy
+    place = Corner(chunks)
+    for z in range(cz):
+        store(out, z * cy, load(block, z * cy, cy // SUB))
+    place.interface(
+        0, planes((own,), cy), planes((got,), cy), got_d, got_y, cz, cy, work,
+        lambda j, tiles: place.add_layer(out, 0, j, cz, cy, tiles),
+    )
+
+
+def one_hot(slots, number):
+    return jnp.where(number == jnp.broadcast_to(slots >> 7, number.shape), 1.0, 0.0).astype(jnp.bfloat16)
+
+
+def near_join(own, got, got_d, got_y, block):
     chunks, tall, _ = own.shape
-    cy = (tall - SUB) // 4
+    cy = (tall - 1) // 4
     return pl.pallas_call(
         near_join_kernel,
-        out_shape=f32(chunks, 4 * cy, LANES),
-        in_specs=[VMEM] * 4,
+        out_shape=f32(*block.shape),
+        in_specs=[VMEM] * 5,
         out_specs=VMEM,
         scratch_shapes=[pltpu.VMEM((SLOTS, chunks, cy + 2 * SUB + 2 * PAD, LANES), jnp.float32)],
         compiler_params=pltpu.CompilerParams(vmem_limit_bytes=24 << 20),
         name="near_join",
-    )(own, got, got_d, got_y)
+    )(own, got, got_d, got_y, block)
 
 
 def join_kernel(
-    row_of, lane_of, block, change, own_b, own_y, got_a, got_b, got_y, got_da, got_db,
+    row_of, lane_of, block, own_b, own_y, got_a, got_b, got_y, got_da, got_db,
     potential, values, pot, layers, columns, picked, sem,
 ):
     chunks, cells, _ = pot.shape
@@ -450,25 +496,14 @@
     blocks = cy // SUB
     place = Corner(chunks)
     odd, right, has = place.odd, place.right, place.has
-    fetch = pltpu.make_async_copy(block, pot, sem.at[0])
-    fetch.start()
     sub = subs_of()
-
-    def add_layer(i, j, tiles):
-        start = pl.multiple_of(jnp.where(place.low_side(i) == 1, j, cz - 1 - j) * cy, SUB)
-        for b in range(blocks):
-            for c in range(chunks):
-                where = (c, pl.ds(start + SUB * b, SUB), slice(None))
-                pot[where] = pot[where] + tiles[b][c]
+    for z in range(cz):
+        store(pot, z * cy, load(block, z * cy, blocks))
 
     def finish(j, tiles):
-        if j == 0:
-            fetch.wait()
-            for old in range(4):
-                add_layer(0, old, load(change, old * cy, blocks))
-        add_layer(1, j, tiles)
-
-    place.interface(1, own_b, got_b, got_db, got_y, cz, cy, layers, finish)
+        place.add_layer(pot, 1, j, cz, cy, tiles)
+
+    place.interface(1, planes((own_b,), cy), planes((got_b,), cy), got_db, got_y, cz, cy, layers, finish)
 
     low_has = jnp.where(odd == 1, has[0], has[1])
     high_has = jnp.where(odd == 1, has[1], has[0])
@@ -488,7 +523,7 @@
     def outer_y(k):
         pairs = [either(place.near(got_a, k * cy, cy, 0), place.near(got_b, k * cy, cy, 0))] if k < 2 else []
         if k == 0:
-            pairs.append(either(place.row(got_a, 4 * cy, 0), place.row(got_b, 4 * cy, 0)))
+            pairs.append(either([jnp.broadcast_to(got_a[c, 4 * cy:4 * cy + 1, :], (SUB, LANES)) for c in range(chunks)], place.row(got_b, 4 * cy, 0)))
         return along(load(own_y, k * cz, cz // SUB), pairs)
 
     def mask_y(tiles):
@@ -506,7 +541,7 @@
     respond(cz + 2 * SUB, outer_y, inner_y, mask_y, columns, finish_y)
 
     leave = [
-        pltpu.make_async_copy(pot.at[c], potential.at[:, pl.ds(c * LANES, LANES)], sem.at[1 + c]) for c in range(chunks)
+        pltpu.make_async_copy(pot.at[c], potential.at[:, pl.ds(c * LANES, LANES)], sem.at[c]) for c in range(chunks)
     ]
     for c in leave:
         c.start()
@@ -530,30 +565,29 @@
         c.wait()
 
 
-def join(row_of, lane_of, block, change, own, got, devices):
+def join(row_of, lane_of, block, own, got, devices):
     chunks, cells, _ = block.shape
     cy = (own[0].shape[1] - SUB) // 4
     cz = cells // cy
     nodes = row_of.shape[0]
-    nx = chunks * LANES
     return pl.pallas_call(
         join_kernel,
-        out_shape=(f32(cells, nx), f32(devices, 1, nodes)),
-        in_specs=[SMEM, VMEM, ANY] + [VMEM] * 8,
+        out_shape=(f32(cells, chunks * LANES), f32(devices, 1, nodes)),
+        in_specs=[SMEM, VMEM, VMEM] + [VMEM] * 7,
         out_specs=(ANY, VMEM),
         scratch_shapes=[
             pltpu.VMEM((chunks, cells, LANES), jnp.float32),
             pltpu.VMEM((SLOTS, chunks, cy + 2 * SUB + 2 * PAD, LANES), jnp.float32),
             pltpu.VMEM((SLOTS, chunks, cz + 2 * SUB + 2 * PAD, LANES), jnp.float32),
             pltpu.VMEM((nodes, LANES), jnp.float32),
-            pltpu.SemaphoreType.DMA((1 + chunks,)),
+            pltpu.SemaphoreType.DMA((chunks,)),
         ],
         compiler_params=pltpu.CompilerParams(vmem_limit_bytes=24 << 20),
         name="join",
-    )(row_of, lane_of, block, change, *own, *got)
-
-
-def window_kernel(table_ref, slot_ref, matrix_ref, keep_ref, send_ref, rows_ref):
+    )(row_of, lane_of, block, *own, *got)
+
+
+def window_kernel(table_ref, slot_ref, matrix_ref, hot_ref, keep_ref, send_ref, rows_ref):
     rows, columns = matrix_ref.shape
     owners, _, width = table_ref.shape
     parts = width // LANES
@@ -576,10 +610,11 @@
     def part(i, accs):
         accs = list(accs)
         slots = [slot_ref[pl.ds(first + i * each + u, 1), :] for u in range(each)]
-        hot = jnp.concatenate(
-            [jnp.where(number == jnp.broadcast_to(s >> 7, (count, LANES)), 1.0, 0.0).astype(jnp.bfloat16) for s in slots],
-            axis=1,
-        )
+        at = i * (each * LANES)
+        if hot_ref.shape[0] == count:
+            hot = hot_ref[:, pl.ds(at if isinstance(i, int) else pl.multiple_of(at, LANES), each * LANES)]
+        else:
+            hot = jnp.concatenate([one_hot(s, number) for s in slots], axis=1)
         found = jnp.dot(halves, hot, preferred_element_type=jnp.float32)
         for u in range(each):
             both = found[:LANES, u * LANES:(u + 1) * LANES] + found[LANES:, u * LANES:(u + 1) * LANES]
@@ -609,19 +644,19 @@
 WINDOW_CHUNKS = 24
 
 
-def window_product(table, slots, matrix):
+def window_product(table, slots, matrix, hot):
     rows, columns = matrix.shape
     assert columns % (WINDOW_CHUNKS * LANES) == 0 and rows % 16 == 0 and rows <= 2 * LANES
     out = f32(1, LANES)
     return pl.pallas_call(
         window_kernel,
         out_shape=(out, out),
-        in_specs=[VMEM, VMEM, VMEM],
+        in_specs=[VMEM] * 4,
         out_specs=(VMEM, VMEM),
         scratch_shapes=[pltpu.VMEM((table.size // LANES, LANES), jnp.float32)],
         compiler_params=pltpu.CompilerParams(vmem_limit_bytes=32 << 20),
         name="window",
-    )(table, slots, matrix)
+    )(table, slots, matrix, hot)
 
 
 def routes(n):
@@ -655,17 +690,17 @@
     got_y = lax.ppermute(pack_y, "cols", swap)
     got_da = lax.ppermute(diag_a, BOTH, near_diag)
     got_a = lax.ppermute(pack_a, "rows", near)
-    block, matrix = alone(phi_start, source, layer_matrix)
+    slots = column_slot.reshape(-1, LANES)
+    block, matrix, hot = alone(phi_start, source, layer_matrix, slots)
     x = owner_voxel % nx
     row_of = (x // LANES) * (cz * cy) + owner_voxel // nx
     lane_of = (x % LANES).reshape(-1, LANES)
-    change = near_join(pack_a, got_a, got_da, got_y)
+    block = near_join(pack_a, got_a, got_da, got_y, block)
     potential, values = join(
-        row_of, lane_of, block, change, (pack_b, pack_y), (got_a, got_b, got_y, got_da, got_db), devices
+        row_of, lane_of, block, (pack_b, pack_y), (got_a, got_b, got_y, got_da, got_db), devices
     )
     table = lax.all_to_all(values, BOTH, 0, 0, tiled=True)
-    slots = column_slot.reshape(-1, LANES)
-    keep, send = window_product(table, slots, matrix)
+    keep, send = window_product(table, slots, matrix, hot)
     received = lax.ppermute(send, "cols", swap)
     half = layer_matrix.shape[0] // 2
     return potential.reshape(cz, cy, nx), (keep + received)[0, :half]

time: 46.3 us -> 44.2 us (0.955)
  Pallas kernels: 21.2 us -> 18.2 us
  local copies, waits for them, and re-layouts: 0.54 us -> 1.46 us
  starting transfers between devices: 6.76 us -> 7.56 us
  blocking collectives: 13.7 us -> 12.9 us
    pallas_call x1, Pallas kernels: 10.1 us -> 8.14 us  [alone(): pl.pallas_call(alone_kernel, out_shape=(f32(chunks, cz * cy, LANES), f32(...]
    ppermute x1, starting transfers between devices: 0.03 us -> 1.48 us  [local(): got_db = lax.ppermute(diag_b, BOTH, far_diag)]
    ppermute x1, starting transfers between devices: 1.82 us -> 0.54 us  [local(): got_y = lax.ppermute(pack_y, 'cols', swap)]
    pallas_call x4, Pallas kernels: 8.26 us -> 7.22 us  [the longest x1 3.45 us: join(): pl.pallas_call(join_kernel, out_shape=(f32(cells, chunks * LANES), f32(de...]
    unnamed x10 -> x14, local copies, waits for them, and re-layouts: 0.03 us -> 0.94 us
    all_to_all x1, blocking collectives: 13.7 us -> 12.9 us  [local(): table = lax.all_to_all(values, BOTH, 0, 0, tiled=True)]
    ppermute x1, starting transfers between devices: 1.21 us -> 1.88 us  [local(): got_da = lax.ppermute(diag_a, BOTH, near_diag)]
  transfers between devices with their start and end apart: 6 -> 6, of which waited for: 1 -> 1; matrix products, arithmetic and copies ran while one was open for 0% -> 0% of each run, Pallas kernels for 23% -> 22%
where the time goes in v4:
time: 44.2 us; the launch traced here: 44 us
  Pallas kernels  18.2 us (41%)
  blocking collectives  12.9 us (29%)
  starting transfers between devices  7.56 us (17%)
  waiting for transfers between devices  3.17 us (7%)
  local copies, waits for them, and re-layouts  1.46 us (3%)
  between operations  0.77 us (2%)
    all_to_all x1, blocking collectives, local(): table = lax.all_to_all(values, BOTH, 0, 0, tiled=True)  12.9 us
    pallas_call x1, Pallas kernels, alone(): pl.pallas_call(alone_kernel, out_shape=(f32(chunks, cz * cy, LANES), f32(...  8.14 us
    pallas_call x1, Pallas kernels, join(): pl.pallas_call(join_kernel, out_shape=(f32(cells, chunks * LANES), f32(de...  3.45 us
    ppermute x1, waiting for transfers between devices, local(): received = lax.ppermute(send, 'cols', swap)  3.16 us
    ppermute x1, starting transfers between devices, local(): got_b = lax.ppermute(pack_b, BOTH, far)  3 us
    pallas_call x1, Pallas kernels, far_face(): pl.pallas_call(far_face_kernel, out_shape=(f32(chunks, 4 * cy + SUB, LANE...  2.82 us
    pallas_call x1, Pallas kernels, window_product(): pl.pallas_call(window_kernel, out_shape=(out, out), in_specs=[VMEM] * 4,...  2.07 us
    ppermute x1, starting transfers between devices, local(): got_da = lax.ppermute(diag_a, BOTH, near_diag)  1.88 us
  transfers between devices with their start and end apart: 6, of which 1 were waited for; matrix products, arithmetic and copies ran while one was open for 0% of the time, Pallas kernels for 22%

profile of v4, /device:TPU:0, one launch (start us, length us, event | category | flops | bytes accessed | tf_op | source)
XLA Modules:
  0.0 44.0 jit_solution(15909922431701632655)
XLA Ops:
  0.6 2.8 %far_face.1 = (f32[3,392,128]{2,1,0:T(8,128)}, f32[3,16,128]{2,1,0:T(8,128)}) custom-call(f32[16,96,384]{2,1,0:T(8,128)} %phi.5, f32[16,96,384]{2,1,0:T(8,128)} %src.5), custom_call_target="tpu_custom_call" | custom-call | tf_op jit(solution)/shard_map/far_face/pallas_call | solution.py:203
  3.5 3.0 %collective-permute-start.3 = (f32[3,392,128]{2,1,0:T(8,128)}, f32[3,392,128]{2,1,0:T(8,128)S(1)}, u32[]{:S(2)}, u32[]{:S(2)}) collective-permute-start(f32[3,392,128]{2,1,0:T(8,128)} %get-tuple-element.19.own_b), channel_id=1, source_target_pairs={{0,1},{1,0},{2,4},{3,5},{4,2},{5,3},{6,8},{7,9},{8,6},{9,7},{10,12... | collective-permute-start | bytes 1806344 | tf_op jit(solution)/shard_map/ppermute | solution.py:687
  6.5 0.7 %near_face.1 = (f32[3,385,128]{2,1,0:T(8,128)S(1)}, f32[3,72,128]{2,1,0:T(8,128)S(1)}, f32[3,16,128]{2,1,0:T(8,128)S(1)}) custom-call(f32[3,16,128]{2,1,0:T(8,128)} %get-tuple-element.14.after, f32[16,96,384]{2,1,0:T(8,128)S(1)} %copy-done, f32[16,96,384]{2,1,0:T(8,128)S(1)} %copy-done.1), custom_call_target="tpu_custom_call" | custom-call | flops 1 | bytes 1 | tf_op jit(solution)/shard_map/near_face/pallas_call | solution.py:270
  7.2 0.2 collective-permute-start
  7.4 1.5 %collective-permute-start.4 = (f32[3,16,128]{2,1,0:T(8,128)}, f32[3,16,128]{2,1,0:T(8,128)S(1)}, u32[]{:S(2)}, u32[]{:S(2)}) collective-permute-start(f32[3,16,128]{2,1,0:T(8,128)} %get-tuple-element.14.after), channel_id=1, source_target_pairs={{0,1},{1,0},{2,5},{3,4},{4,3},{5,2},{6,9},{7,8},{8,7},{9,6},{10,13... | collective-permute-start | bytes 73736 | tf_op jit(solution)/shard_map/ppermute | solution.py:689
  8.9 0.5 %collective-permute-start.2 = (f32[3,72,128]{2,1,0:T(8,128)S(1)}, f32[3,72,128]{2,1,0:T(8,128)S(1)}, u32[]{:S(2)}, u32[]{:S(2)}) collective-permute-start(f32[3,72,128]{2,1,0:T(8,128)S(1)} %get-tuple-element.17.own_y), channel_id=1, source_target_pairs={{0,1},{1,0},{2,3},{3,2},{4,5},{5,4},{6,7},{7,6},{8,9},{9,8},{10,11... | collective-permute-start | bytes 331784 | tf_op jit(solution)/shard_map/ppermute | solution.py:690
  9.4 1.9 %collective-permute-start.1 = (f32[3,16,128]{2,1,0:T(8,128)S(1)}, f32[3,16,128]{2,1,0:T(8,128)S(1)}, u32[]{:S(2)}, u32[]{:S(2)}) collective-permute-start(f32[3,16,128]{2,1,0:T(8,128)S(1)} %get-tuple-element.16), channel_id=1, source_target_pairs={{0,3},{1,2},{2,1},{3,0},{4,7},{5,6},{6,5},{7,4},{8,11},{9,10},{10,... | collective-permute-start | bytes 73736 | tf_op jit(solution)/shard_map/ppermute | solution.py:691
  11.4 0.0 copy-start.4
  11.4 0.9 %copy-done.4 = s32[24576]{0:T(1024)S(1)} copy-done((s32[24576]{0:T(1024)S(1)}, s32[24576]{0:T(1024)}, u32[]{:S(2)}) %copy-start.4) | copy-done | bytes 98328
  12.3 8.1 %alone.1 = (f32[3,1536,128]{2,1,0:T(8,128)S(1)}, f32[96,12288]{1,0:T(8,128)S(1)}, bf16[192,12288]{1,0:T(8,128)(2,1)S(1)}) custom-call(f32[16,96,384]{2,1,0:T(8,128)S(1)} %copy-done, f32[16,96,384]{2,1,0:T(8,128)S(1)} %copy-done.1, f32[96,12288]{1,0:T(8,128)S(1)} %copy-done.2, s32[192,128]{1,0:T(8,128)S(1)} %bitcast.6), custom_call_target="tpu_custom_call" | custom-call | flops 1 | bytes 1 | tf_op jit(solution)/shard_map/alone/pallas_call | solution.py:339
  20.4 0.0 collective-permute-done.1.got_d.got_da
  20.4 0.0 collective-permute-done.2.got_y
  20.4 0.0 copy-start.3
  20.4 1.0 %near_join.1.block = f32[3,1536,128]{2,1,0:T(8,128)S(1)} custom-call(f32[3,385,128]{2,1,0:T(8,128)S(1)} %get-tuple-element.15.own, f32[3,385,128]{2,1,0:T(8,128)S(1)} %collective-permute-done.got.got_a, f32[3,16,128]{2,1,0:T(8,128)S(1)} %collective-permute-done.1.got_d.got_da, f32[3,72,128]{2,1,0:T(8,128)S(1)} %collective-permute-done.2.got_y, ...), custom_call_target="tpu_custom_call" | custom-call | tf_op jit(solution)/shard_map/near_join/pallas_call | solution.py:478
  21.4 0.0 copy-start.5
  21.5 0.0 collective-permute-done.4.got_db
  21.5 0.0 collective-permute-done.3.got_b
  21.5 0.0 copy-done.3
  21.5 3.4 %join.1 = (f32[1536,384]{1,0:T(8,128)}, f32[32,1,768]{2,1,0:T(1,128)S(1)}) custom-call(s32[768]{0:T(1024)S(1)} %get-tuple-element.27.row_of, s32[6,128]{1,0:T(8,128)S(1)} %get-tuple-element.26.lane_of, f32[3,1536,128]{2,1,0:T(8,128)S(1)} %near_join.1.block, f32[3,392,128]{2,1,0:T(8,128)S(1)} %copy-done.3, f32[3,72,128]{2,1,0:T(8,128)S(1)} %get-tuple-element.17.own_y, ...), custom_call_target="tpu_custom_call" | custom-call | tf_op jit(solution)/shard_map/join/pallas_call | solution.py:573
  25.0 12.9 %all_to_all.5.table_ref = f32[32,1,768]{2,1,0:T(1,128)S(1)} all-to-all(f32[32,1,768]{2,1,0:T(1,128)S(1)} %get-tuple-element.21), channel_id=1, replica_groups=mesh['rows'=16,'cols'=2] {'rows','cols'}, dimensions={0} | all-to-all | bytes 196608 | tf_op jit(solution)/shard_map/all_to_all | solution.py:702
  37.8 2.1 %window.1 = (f32[1,128]{1,0:T(1,128)S(1)}, f32[1,128]{1,0:T(1,128)S(1)}) custom-call(f32[32,1,768]{2,1,0:T(1,128)S(1)} %all_to_all.5.table_ref, s32[192,128]{1,0:T(8,128)S(1)} %bitcast.7, f32[96,12288]{1,0:T(8,128)S(1)} %get-tuple-element.22.matrix_ref, bf16[192,12288]{1,0:T(8,128)(2,1)S(1)} %get-tuple-element.23.hot_ref), custom_call_target="tpu_custom_call" | custom-call | tf_op jit(solution)/shard_map/window/pallas_call | solution.py:651
  39.9 0.4 %collective-permute-start.5 = (f32[1,128]{1,0:T(1,128)S(1)}, f32[1,128]{1,0:T(1,128)S(1)}, u32[]{:S(2)}, u32[]{:S(2)}) collective-permute-start(f32[1,128]{1,0:T(1,128)S(1)} %get-tuple-element.25), channel_id=1, source_target_pairs={{0,1},{1,0},{2,3},{3,2},{4,5},{5,4},{6,7},{7,6},{8,9},{9,8},{10,11... | collective-permute-start | bytes 1544 | tf_op jit(solution)/shard_map/ppermute | solution.py:704
  40.4 3.2 %collective-permute-done.5 = f32[1,128]{1,0:T(1,128)S(1)} collective-permute-done((f32[1,128]{1,0:T(1,128)S(1)}, f32[1,128]{1,0:T(1,128)S(1)}, u32[]{:S(2)}, u32[]{:S(2)}) %collective-permute-start.5) | collective-permute-done | bytes 544 | tf_op jit(solution)/shard_map/ppermute | solution.py:704
  43.5 0.5 %slice_bitcast_fusion = f32[48]{0:T(128)} fusion(f32[1,128]{1,0:T(1,128)S(1)} %add.21), kind=kLoop, calls=%fused_computation.16 | loop fusion | bytes 384 | tf_op jit(solution)/shard_map/squeeze | solution.py:706
  (12 shorter events, 0.0 us)
Async XLA Ops:
  0.6 5.9 %copy-start = (f32[16,96,384]{2,1,0:T(8,128)S(1)}, f32[16,96,384]{2,1,0:T(8,128)}, u32[]{:S(2)}) copy-start(f32[16,96,384]{2,1,0:T(8,128)} %phi.5) | copy-start | bytes 7077892
  0.6 5.8 %copy-start.1 = (f32[16,96,384]{2,1,0:T(8,128)S(1)}, f32[16,96,384]{2,1,0:T(8,128)}, u32[]{:S(2)}) copy-start(f32[16,96,384]{2,1,0:T(8,128)} %src.5) | copy-start | bytes 7077892
  3.5 18.0 %collective-permute-start.3 = (f32[3,392,128]{2,1,0:T(8,128)}, f32[3,392,128]{2,1,0:T(8,128)S(1)}, u32[]{:S(2)}, u32[]{:S(2)}) collective-permute-start(f32[3,392,128]{2,1,0:T(8,128)} %get-tuple-element.19.own_b), channel_id=1, source_target_pairs={{0,1},{1,0},{2,4},{3,5},{4,2},{5,3},{6,8},{7,9},{8,6},{9,7},{10,12... | collective-permute-start | bytes 1806344 | tf_op jit(solution)/shard_map/ppermute | solution.py:687
  6.5 4.8 %copy-start.6 = (s32[768]{0:T(1024)S(1)}, s32[768]{0:T(1024)}, u32[]{:S(2)}) copy-start(s32[768]{0:T(1024)} %param.7) | copy-start | bytes 9220
  6.5 4.9 %copy-start.2 = (f32[96,12288]{1,0:T(8,128)S(1)}, f32[96,12288]{1,0:T(8,128)}, u32[]{:S(2)}) copy-start(f32[96,12288]{1,0:T(8,128)} %matrix.1) | copy-start | bytes 14155780
  7.2 13.2 %collective-permute-start = (f32[3,385,128]{2,1,0:T(8,128)S(1)}, f32[3,385,128]{2,1,0:T(8,128)S(1)}, u32[]{:S(2)}, u32[]{:S(2)}) collective-permute-start(f32[3,385,128]{2,1,0:T(8,128)S(1)} %get-tuple-element.15.own), channel_id=1, source_target_pairs={{0,2},{2,0},{4,6},{6,4},{8,10},{10,8},{12,14},{14,12},{16,18},{18,... | collective-permute-start | bytes 1774088 | tf_op jit(solution)/shard_map/ppermute | solution.py:692
  7.4 14.0 %collective-permute-start.4 = (f32[3,16,128]{2,1,0:T(8,128)}, f32[3,16,128]{2,1,0:T(8,128)S(1)}, u32[]{:S(2)}, u32[]{:S(2)}) collective-permute-start(f32[3,16,128]{2,1,0:T(8,128)} %get-tuple-element.14.after), channel_id=1, source_target_pairs={{0,1},{1,0},{2,5},{3,4},{4,3},{5,2},{6,9},{7,8},{8,7},{9,6},{10,13... | collective-permute-start | bytes 73736 | tf_op jit(solution)/shard_map/ppermute | solution.py:689
  8.9 11.5 %collective-permute-start.2 = (f32[3,72,128]{2,1,0:T(8,128)S(1)}, f32[3,72,128]{2,1,0:T(8,128)S(1)}, u32[]{:S(2)}, u32[]{:S(2)}) collective-permute-start(f32[3,72,128]{2,1,0:T(8,128)S(1)} %get-tuple-element.17.own_y), channel_id=1, source_target_pairs={{0,1},{1,0},{2,3},{3,2},{4,5},{5,4},{6,7},{7,6},{8,9},{9,8},{10,11... | collective-permute-start | bytes 331784 | tf_op jit(solution)/shard_map/ppermute | solution.py:690
  9.4 11.0 %collective-permute-start.1 = (f32[3,16,128]{2,1,0:T(8,128)S(1)}, f32[3,16,128]{2,1,0:T(8,128)S(1)}, u32[]{:S(2)}, u32[]{:S(2)}) collective-permute-start(f32[3,16,128]{2,1,0:T(8,128)S(1)} %get-tuple-element.16), channel_id=1, source_target_pairs={{0,3},{1,2},{2,1},{3,0},{4,7},{5,6},{6,5},{7,4},{8,11},{9,10},{10,... | collective-permute-start | bytes 73736 | tf_op jit(solution)/shard_map/ppermute | solution.py:691
  11.4 0.9 %copy-start.4 = (s32[24576]{0:T(1024)S(1)}, s32[24576]{0:T(1024)}, u32[]{:S(2)}) copy-start(s32[24576]{0:T(1024)} %param.8) | copy-start | bytes 294916
  20.4 1.1 %copy-start.3 = (f32[3,392,128]{2,1,0:T(8,128)S(1)}, f32[3,392,128]{2,1,0:T(8,128)}, u32[]{:S(2)}) copy-start(f32[3,392,128]{2,1,0:T(8,128)} %get-tuple-element.19.own_b) | copy-start | bytes 1806340
  21.4 16.4 %copy-start.5 = (s32[24576]{0:T(1024)S(1)}, s32[24576]{0:T(1024)}, u32[]{:S(2)}) copy-start(s32[24576]{0:T(1024)} %param.8) | copy-start | bytes 294916
  39.9 3.6 %collective-permute-start.5 = (f32[1,128]{1,0:T(1,128)S(1)}, f32[1,128]{1,0:T(1,128)S(1)}, u32[]{:S(2)}, u32[]{:S(2)}) collective-permute-start(f32[1,128]{1,0:T(1,128)S(1)} %get-tuple-element.25), channel_id=1, source_target_pairs={{0,1},{1,0},{2,3},{3,2},{4,5},{5,4},{6,7},{7,6},{8,9},{9,8},{10,11... | collective-permute-start | bytes 1544 | tf_op jit(solution)/shard_map/ppermute | solution.py:704

commit v5 on v4

--- a/solution.py
+++ b/solution.py
@@ -496,7 +496,26 @@
     blocks = cy // SUB
     place = Corner(chunks)
     odd, right, has = place.odd, place.right, place.has
-    sub = subs_of()
+    deep = 4
+    low_b = place.low_side(1) == 1
+    rest, reach = jnp.where(low_b, deep, 0), jnp.where(low_b, 0, cz - deep)
+    edge = pl.multiple_of(jnp.where(right, 0, cy - SUB), SUB)
+    inner_rows = pl.multiple_of(jnp.where(right, SUB, 0), SUB)
+
+    def leaving(ref, z, layers_out, y, rows, i):
+        whole = ref.reshape(chunks, cz, cy, LANES)
+        return [
+            pltpu.make_async_copy(
+                whole.at[c, pl.ds(z, layers_out), pl.ds(y, rows), :],
+                potential.at[pl.ds(z, layers_out), pl.ds(y, rows), pl.ds(c * LANES, LANES)],
+                sem.at[i, c],
+            )
+            for c in range(chunks)
+        ]
+
+    leave = leaving(block, rest, cz - deep, inner_rows, cy - SUB, 0)
+    for c in leave:
+        c.start()
     for z in range(cz):
         store(pot, z * cy, load(block, z * cy, blocks))
 
@@ -540,10 +559,8 @@
 
     respond(cz + 2 * SUB, outer_y, inner_y, mask_y, columns, finish_y)
 
-    leave = [
-        pltpu.make_async_copy(pot.at[c], potential.at[:, pl.ds(c * LANES, LANES)], sem.at[c]) for c in range(chunks)
-    ]
-    for c in leave:
+    last = leaving(pot, reach, deep, 0, cy, 1) + leaving(pot, rest, cz - deep, edge, SUB, 2)
+    for c in last:
         c.start()
 
     wide = picked.shape[0]
@@ -555,13 +572,13 @@
         return carry
 
     lax.fori_loop(0, wide // 16, pick, 0)
-    deep = lax.broadcasted_iota(jnp.int32, (LANES, LANES), 0)
+    number = lax.broadcasted_iota(jnp.int32, (LANES, LANES), 0)
     for q in range(wide // LANES):
         turned = picked[q * LANES:(q + 1) * LANES, :].T
-        chosen = jnp.where(deep == lane_of[q:q + 1, :], turned, 0.0)
+        chosen = jnp.where(number == lane_of[q:q + 1, :], turned, 0.0)
         line = jnp.sum(chosen, axis=0, keepdims=True)
         values[:, :, q * LANES:(q + 1) * LANES] = jnp.broadcast_to(line[None], (values.shape[0], 1, LANES))
-    for c in leave:
+    for c in leave + last:
         c.wait()
 
 
@@ -572,7 +589,7 @@
     nodes = row_of.shape[0]
     return pl.pallas_call(
         join_kernel,
-        out_shape=(f32(cells, chunks * LANES), f32(devices, 1, nodes)),
+        out_shape=(f32(cz, cy, chunks * LANES), f32(devices, 1, nodes)),
         in_specs=[SMEM, VMEM, VMEM] + [VMEM] * 7,
         out_specs=(ANY, VMEM),
         scratch_shapes=[
@@ -580,7 +597,7 @@
             pltpu.VMEM((SLOTS, chunks, cy + 2 * SUB + 2 * PAD, LANES), jnp.float32),
             pltpu.VMEM((SLOTS, chunks, cz + 2 * SUB + 2 * PAD, LANES), jnp.float32),
             pltpu.VMEM((nodes, LANES), jnp.float32),
-            pltpu.SemaphoreType.DMA((chunks,)),
+            pltpu.SemaphoreType.DMA((3, chunks)),
         ],
         compiler_params=pltpu.CompilerParams(vmem_limit_bytes=24 << 20),
         name="join",
@@ -703,7 +720,7 @@
     keep, send = window_product(table, slots, matrix, hot)
     received = lax.ppermute(send, "cols", swap)
     half = layer_matrix.shape[0] // 2
-    return potential.reshape(cz, cy, nx), (keep + received)[0, :half]
+    return potential, (keep + received)[0, :half]
 
 
 def solution(mesh):

time: 44.2 us -> 43.9 us (level)
  transfers between devices with their start and end apart: 6 -> 6, of which waited for: 1 -> 1; matrix products, arithmetic and copies ran while one was open for 0% -> 0% of each run, Pallas kernels for 22% -> 23%
where the time goes in v5:
time: 43.9 us; the launch traced here: 43.7 us
  Pallas kernels  17.9 us (41%)
  blocking collectives  12.9 us (29%)
  starting transfers between devices  7.56 us (17%)
  waiting for transfers between devices  3.17 us (7%)
  local copies, waits for them, and re-layouts  1.46 us (3%)
  between operations  0.77 us (2%)
    all_to_all x1, blocking collectives, local(): table = lax.all_to_all(values, BOTH, 0, 0, tiled=True)  12.9 us
    pallas_call x1, Pallas kernels, alone(): pl.pallas_call(alone_kernel, out_shape=(f32(chunks, cz * cy, LANES), f32(...  8.14 us
    ppermute x1, waiting for transfers between devices, local(): received = lax.ppermute(send, 'cols', swap)  3.16 us
    pallas_call x1, Pallas kernels, join(): pl.pallas_call(join_kernel, out_shape=(f32(cz, cy, chunks * LANES), f32(d...  3.13 us
    ppermute x1, starting transfers between devices, local(): got_b = lax.ppermute(pack_b, BOTH, far)  3 us
    pallas_call x1, Pallas kernels, far_face(): pl.pallas_call(far_face_kernel, out_shape=(f32(chunks, 4 * cy + SUB, LANE...  2.82 us
    pallas_call x1, Pallas kernels, window_product(): pl.pallas_call(window_kernel, out_shape=(out, out), in_specs=[VMEM] * 4,...  2.07 us
    ppermute x1, starting transfers between devices, local(): got_da = lax.ppermute(diag_a, BOTH, near_diag)  1.88 us
  transfers between devices with their start and end apart: 6, of which 1 were waited for; matrix products, arithmetic and copies ran while one was open for 0% of the time, Pallas kernels for 23%

profile of v5, /device:TPU:0, one launch (start us, length us, event | category | flops | bytes accessed | tf_op | source)
XLA Modules:
  0.0 43.7 jit_solution(4144590183662533857)
XLA Ops:
  0.6 2.8 %far_face.1 = (f32[3,392,128]{2,1,0:T(8,128)}, f32[3,16,128]{2,1,0:T(8,128)}) custom-call(f32[16,96,384]{2,1,0:T(8,128)} %phi.5, f32[16,96,384]{2,1,0:T(8,128)} %src.5), custom_call_target="tpu_custom_call" | custom-call | tf_op jit(solution)/shard_map/far_face/pallas_call | solution.py:203
  3.5 3.0 %collective-permute-start.3 = (f32[3,392,128]{2,1,0:T(8,128)}, f32[3,392,128]{2,1,0:T(8,128)S(1)}, u32[]{:S(2)}, u32[]{:S(2)}) collective-permute-start(f32[3,392,128]{2,1,0:T(8,128)} %get-tuple-element.19.own_b), channel_id=1, source_target_pairs={{0,1},{1,0},{2,4},{3,5},{4,2},{5,3},{6,8},{7,9},{8,6},{9,7},{10,12... | collective-permute-start | bytes 1806344 | tf_op jit(solution)/shard_map/ppermute | solution.py:704
  6.5 0.7 %near_face.1 = (f32[3,385,128]{2,1,0:T(8,128)S(1)}, f32[3,72,128]{2,1,0:T(8,128)S(1)}, f32[3,16,128]{2,1,0:T(8,128)S(1)}) custom-call(f32[3,16,128]{2,1,0:T(8,128)} %get-tuple-element.14.after, f32[16,96,384]{2,1,0:T(8,128)S(1)} %copy-done, f32[16,96,384]{2,1,0:T(8,128)S(1)} %copy-done.1), custom_call_target="tpu_custom_call" | custom-call | flops 1 | bytes 1 | tf_op jit(solution)/shard_map/near_face/pallas_call | solution.py:270
  7.2 0.2 collective-permute-start
  7.4 1.5 %collective-permute-start.4 = (f32[3,16,128]{2,1,0:T(8,128)}, f32[3,16,128]{2,1,0:T(8,128)S(1)}, u32[]{:S(2)}, u32[]{:S(2)}) collective-permute-start(f32[3,16,128]{2,1,0:T(8,128)} %get-tuple-element.14.after), channel_id=1, source_target_pairs={{0,1},{1,0},{2,5},{3,4},{4,3},{5,2},{6,9},{7,8},{8,7},{9,6},{10,13... | collective-permute-start | bytes 73736 | tf_op jit(solution)/shard_map/ppermute | solution.py:706
  8.9 0.5 %collective-permute-start.2 = (f32[3,72,128]{2,1,0:T(8,128)S(1)}, f32[3,72,128]{2,1,0:T(8,128)S(1)}, u32[]{:S(2)}, u32[]{:S(2)}) collective-permute-start(f32[3,72,128]{2,1,0:T(8,128)S(1)} %get-tuple-element.17.own_y), channel_id=1, source_target_pairs={{0,1},{1,0},{2,3},{3,2},{4,5},{5,4},{6,7},{7,6},{8,9},{9,8},{10,11... | collective-permute-start | bytes 331784 | tf_op jit(solution)/shard_map/ppermute | solution.py:707
  9.4 1.9 %collective-permute-start.1 = (f32[3,16,128]{2,1,0:T(8,128)S(1)}, f32[3,16,128]{2,1,0:T(8,128)S(1)}, u32[]{:S(2)}, u32[]{:S(2)}) collective-permute-start(f32[3,16,128]{2,1,0:T(8,128)S(1)} %get-tuple-element.16), channel_id=1, source_target_pairs={{0,3},{1,2},{2,1},{3,0},{4,7},{5,6},{6,5},{7,4},{8,11},{9,10},{10,... | collective-permute-start | bytes 73736 | tf_op jit(solution)/shard_map/ppermute | solution.py:708
  11.4 0.0 copy-start.4
  11.4 0.9 %copy-done.4 = s32[24576]{0:T(1024)S(1)} copy-done((s32[24576]{0:T(1024)S(1)}, s32[24576]{0:T(1024)}, u32[]{:S(2)}) %copy-start.4) | copy-done | bytes 98328
  12.3 8.1 %alone.1 = (f32[3,1536,128]{2,1,0:T(8,128)S(1)}, f32[96,12288]{1,0:T(8,128)S(1)}, bf16[192,12288]{1,0:T(8,128)(2,1)S(1)}) custom-call(f32[16,96,384]{2,1,0:T(8,128)S(1)} %copy-done, f32[16,96,384]{2,1,0:T(8,128)S(1)} %copy-done.1, f32[96,12288]{1,0:T(8,128)S(1)} %copy-done.2, s32[192,128]{1,0:T(8,128)S(1)} %bitcast.5), custom_call_target="tpu_custom_call" | custom-call | flops 1 | bytes 1 | tf_op jit(solution)/shard_map/alone/pallas_call | solution.py:339
  20.4 0.0 collective-permute-done.1.got_d.got_da
  20.4 0.0 collective-permute-done.2.got_y
  20.4 0.0 copy-start.3
  20.4 1.0 %near_join.1.block = f32[3,1536,128]{2,1,0:T(8,128)S(1)} custom-call(f32[3,385,128]{2,1,0:T(8,128)S(1)} %get-tuple-element.15.own, f32[3,385,128]{2,1,0:T(8,128)S(1)} %collective-permute-done.got.got_a, f32[3,16,128]{2,1,0:T(8,128)S(1)} %collective-permute-done.1.got_d.got_da, f32[3,72,128]{2,1,0:T(8,128)S(1)} %collective-permute-done.2.got_y, ...), custom_call_target="tpu_custom_call" | custom-call | tf_op jit(solution)/shard_map/near_join/pallas_call | solution.py:478
  21.4 0.0 copy-start.5
  21.5 0.0 collective-permute-done.4.got_db
  21.5 0.0 collective-permute-done.3.got_b
  21.5 0.0 copy-done.3
  21.5 3.1 %join.1 = (f32[16,96,384]{2,1,0:T(8,128)}, f32[32,1,768]{2,1,0:T(1,128)S(1)}) custom-call(s32[768]{0:T(1024)S(1)} %get-tuple-element.27.row_of, s32[6,128]{1,0:T(8,128)S(1)} %get-tuple-element.26.lane_of, f32[3,1536,128]{2,1,0:T(8,128)S(1)} %near_join.1.block, f32[3,392,128]{2,1,0:T(8,128)S(1)} %copy-done.3, f32[3,72,128]{2,1,0:T(8,128)S(1)} %get-tuple-element.17.own_y, ...), custom_call_target="tpu_custom_call" | custom-call | tf_op jit(solution)/shard_map/join/pallas_call | solution.py:590
  24.6 12.9 %all_to_all.5.table_ref = f32[32,1,768]{2,1,0:T(1,128)S(1)} all-to-all(f32[32,1,768]{2,1,0:T(1,128)S(1)} %get-tuple-element.21), channel_id=1, replica_groups=mesh['rows'=16,'cols'=2] {'rows','cols'}, dimensions={0} | all-to-all | bytes 196608 | tf_op jit(solution)/shard_map/all_to_all | solution.py:719
  37.5 2.1 %window.1 = (f32[1,128]{1,0:T(1,128)S(1)}, f32[1,128]{1,0:T(1,128)S(1)}) custom-call(f32[32,1,768]{2,1,0:T(1,128)S(1)} %all_to_all.5.table_ref, s32[192,128]{1,0:T(8,128)S(1)} %bitcast.6, f32[96,12288]{1,0:T(8,128)S(1)} %get-tuple-element.22.matrix_ref, bf16[192,12288]{1,0:T(8,128)(2,1)S(1)} %get-tuple-element.23.hot_ref), custom_call_target="tpu_custom_call" | custom-call | tf_op jit(solution)/shard_map/window/pallas_call | solution.py:668
  39.6 0.4 %collective-permute-start.5 = (f32[1,128]{1,0:T(1,128)S(1)}, f32[1,128]{1,0:T(1,128)S(1)}, u32[]{:S(2)}, u32[]{:S(2)}) collective-permute-start(f32[1,128]{1,0:T(1,128)S(1)} %get-tuple-element.25), channel_id=1, source_target_pairs={{0,1},{1,0},{2,3},{3,2},{4,5},{5,4},{6,7},{7,6},{8,9},{9,8},{10,11... | collective-permute-start | bytes 1544 | tf_op jit(solution)/shard_map/ppermute | solution.py:721
  40.0 3.2 %collective-permute-done.5 = f32[1,128]{1,0:T(1,128)S(1)} collective-permute-done((f32[1,128]{1,0:T(1,128)S(1)}, f32[1,128]{1,0:T(1,128)S(1)}, u32[]{:S(2)}, u32[]{:S(2)}) %collective-permute-start.5) | collective-permute-done | bytes 544 | tf_op jit(solution)/shard_map/ppermute | solution.py:721
  43.2 0.5 %slice_bitcast_fusion = f32[48]{0:T(128)} fusion(f32[1,128]{1,0:T(1,128)S(1)} %add.21), kind=kLoop, calls=%fused_computation.16 | loop fusion | bytes 384 | tf_op jit(solution)/shard_map/squeeze | solution.py:723
  (12 shorter events, 0.0 us)
Async XLA Ops:
  0.6 5.9 %copy-start = (f32[16,96,384]{2,1,0:T(8,128)S(1)}, f32[16,96,384]{2,1,0:T(8,128)}, u32[]{:S(2)}) copy-start(f32[16,96,384]{2,1,0:T(8,128)} %phi.5) | copy-start | bytes 7077892
  0.6 5.8 %copy-start.1 = (f32[16,96,384]{2,1,0:T(8,128)S(1)}, f32[16,96,384]{2,1,0:T(8,128)}, u32[]{:S(2)}) copy-start(f32[16,96,384]{2,1,0:T(8,128)} %src.5) | copy-start | bytes 7077892
  3.5 18.0 %collective-permute-start.3 = (f32[3,392,128]{2,1,0:T(8,128)}, f32[3,392,128]{2,1,0:T(8,128)S(1)}, u32[]{:S(2)}, u32[]{:S(2)}) collective-permute-start(f32[3,392,128]{2,1,0:T(8,128)} %get-tuple-element.19.own_b), channel_id=1, source_target_pairs={{0,1},{1,0},{2,4},{3,5},{4,2},{5,3},{6,8},{7,9},{8,6},{9,7},{10,12... | collective-permute-start | bytes 1806344 | tf_op jit(solution)/shard_map/ppermute | solution.py:704
  6.5 4.8 %copy-start.6 = (s32[768]{0:T(1024)S(1)}, s32[768]{0:T(1024)}, u32[]{:S(2)}) copy-start(s32[768]{0:T(1024)} %param.7) | copy-start | bytes 9220
  6.5 4.9 %copy-start.2 = (f32[96,12288]{1,0:T(8,128)S(1)}, f32[96,12288]{1,0:T(8,128)}, u32[]{:S(2)}) copy-start(f32[96,12288]{1,0:T(8,128)} %matrix.1) | copy-start | bytes 14155780
  7.2 13.2 %collective-permute-start = (f32[3,385,128]{2,1,0:T(8,128)S(1)}, f32[3,385,128]{2,1,0:T(8,128)S(1)}, u32[]{:S(2)}, u32[]{:S(2)}) collective-permute-start(f32[3,385,128]{2,1,0:T(8,128)S(1)} %get-tuple-element.15.own), channel_id=1, source_target_pairs={{0,2},{2,0},{4,6},{6,4},{8,10},{10,8},{12,14},{14,12},{16,18},{18,... | collective-permute-start | bytes 1774088 | tf_op jit(solution)/shard_map/ppermute | solution.py:709
  7.4 14.0 %collective-permute-start.4 = (f32[3,16,128]{2,1,0:T(8,128)}, f32[3,16,128]{2,1,0:T(8,128)S(1)}, u32[]{:S(2)}, u32[]{:S(2)}) collective-permute-start(f32[3,16,128]{2,1,0:T(8,128)} %get-tuple-element.14.after), channel_id=1, source_target_pairs={{0,1},{1,0},{2,5},{3,4},{4,3},{5,2},{6,9},{7,8},{8,7},{9,6},{10,13... | collective-permute-start | bytes 73736 | tf_op jit(solution)/shard_map/ppermute | solution.py:706
  8.9 11.5 %collective-permute-start.2 = (f32[3,72,128]{2,1,0:T(8,128)S(1)}, f32[3,72,128]{2,1,0:T(8,128)S(1)}, u32[]{:S(2)}, u32[]{:S(2)}) collective-permute-start(f32[3,72,128]{2,1,0:T(8,128)S(1)} %get-tuple-element.17.own_y), channel_id=1, source_target_pairs={{0,1},{1,0},{2,3},{3,2},{4,5},{5,4},{6,7},{7,6},{8,9},{9,8},{10,11... | collective-permute-start | bytes 331784 | tf_op jit(solution)/shard_map/ppermute | solution.py:707
  9.4 11.0 %collective-permute-start.1 = (f32[3,16,128]{2,1,0:T(8,128)S(1)}, f32[3,16,128]{2,1,0:T(8,128)S(1)}, u32[]{:S(2)}, u32[]{:S(2)}) collective-permute-start(f32[3,16,128]{2,1,0:T(8,128)S(1)} %get-tuple-element.16), channel_id=1, source_target_pairs={{0,3},{1,2},{2,1},{3,0},{4,7},{5,6},{6,5},{7,4},{8,11},{9,10},{10,... | collective-permute-start | bytes 73736 | tf_op jit(solution)/shard_map/ppermute | solution.py:708
  11.4 0.9 %copy-start.4 = (s32[24576]{0:T(1024)S(1)}, s32[24576]{0:T(1024)}, u32[]{:S(2)}) copy-start(s32[24576]{0:T(1024)} %param.8) | copy-start | bytes 294916
  20.4 1.1 %copy-start.3 = (f32[3,392,128]{2,1,0:T(8,128)S(1)}, f32[3,392,128]{2,1,0:T(8,128)}, u32[]{:S(2)}) copy-start(f32[3,392,128]{2,1,0:T(8,128)} %get-tuple-element.19.own_b) | copy-start | bytes 1806340
  21.4 16.1 %copy-start.5 = (s32[24576]{0:T(1024)S(1)}, s32[24576]{0:T(1024)}, u32[]{:S(2)}) copy-start(s32[24576]{0:T(1024)} %param.8) | copy-start | bytes 294916
  39.6 3.6 %collective-permute-start.5 = (f32[1,128]{1,0:T(1,128)S(1)}, f32[1,128]{1,0:T(1,128)S(1)}, u32[]{:S(2)}, u32[]{:S(2)}) collective-permute-start(f32[1,128]{1,0:T(1,128)S(1)} %get-tuple-element.25), channel_id=1, source_target_pairs={{0,1},{1,0},{2,3},{3,2},{4,5},{5,4},{6,7},{7,6},{8,9},{9,8},{10,11... | collective-permute-start | bytes 1544 | tf_op jit(solution)/shard_map/ppermute | solution.py:721

commit v6 on v5

--- a/solution.py
+++ b/solution.py
@@ -516,11 +516,14 @@
     leave = leaving(block, rest, cz - deep, inner_rows, cy - SUB, 0)
     for c in leave:
         c.start()
-    for z in range(cz):
-        store(pot, z * cy, load(block, z * cy, blocks))
+    for i in range(cz - deep):
+        start = pl.multiple_of((rest + i) * cy, SUB)
+        store(pot, start, load(block, start, blocks))
 
     def finish(j, tiles):
-        place.add_layer(pot, 1, j, cz, cy, tiles)
+        start = pl.multiple_of(jnp.where(low_b, j, cz - 1 - j) * cy, SUB)
+        before = load(block, start, blocks)
+        store(pot, start, [[b + t for b, t in zip(*rows)] for rows in zip(before, tiles)])
 
     place.interface(1, planes((own_b,), cy), planes((got_b,), cy), got_db, got_y, cz, cy, layers, finish)
 
@@ -658,7 +661,7 @@
         out[...] = jnp.sum(tall.T, axis=0, keepdims=True)
 
 
-WINDOW_CHUNKS = 24
+WINDOW_CHUNKS = 48
 
 
 def window_product(table, slots, matrix, hot):

time: 43.9 us -> 43.7 us (level)
  no operation moved by 1% of the time
where the time goes in v6:
time: 43.7 us; the launch traced here: 43.6 us
  Pallas kernels  17.7 us (41%)
  blocking collectives  12.9 us (30%)
  starting transfers between devices  7.56 us (17%)
  waiting for transfers between devices  3.17 us (7%)
  local copies, waits for them, and re-layouts  1.46 us (3%)
  between operations  0.77 us (2%)
    all_to_all x1, blocking collectives, local(): table = lax.all_to_all(values, BOTH, 0, 0, tiled=True)  12.9 us
    pallas_call x1, Pallas kernels, alone(): pl.pallas_call(alone_kernel, out_shape=(f32(chunks, cz * cy, LANES), f32(...  8.14 us
    ppermute x1, waiting for transfers between devices, local(): received = lax.ppermute(send, 'cols', swap)  3.16 us
    ppermute x1, starting transfers between devices, local(): got_b = lax.ppermute(pack_b, BOTH, far)  3 us
    pallas_call x1, Pallas kernels, join(): pl.pallas_call(join_kernel, out_shape=(f32(cz, cy, chunks * LANES), f32(d...  2.98 us
    pallas_call x1, Pallas kernels, far_face(): pl.pallas_call(far_face_kernel, out_shape=(f32(chunks, 4 * cy + SUB, LANE...  2.82 us
    pallas_call x1, Pallas kernels, window_product(): pl.pallas_call(window_kernel, out_shape=(out, out), in_specs=[VMEM] * 4,...  2.07 us
    ppermute x1, starting transfers between devices, local(): got_da = lax.ppermute(diag_a, BOTH, near_diag)  1.88 us
  transfers between devices with their start and end apart: 6, of which 1 were waited for; matrix products, arithmetic and copies ran while one was open for 0% of the time, Pallas kernels for 23%

profile of v6, /device:TPU:0, one launch (start us, length us, event | category | flops | bytes accessed | tf_op | source)
XLA Modules:
  0.0 43.6 jit_solution(8921674987532352402)
XLA Ops:
  0.6 2.8 %far_face.1 = (f32[3,392,128]{2,1,0:T(8,128)}, f32[3,16,128]{2,1,0:T(8,128)}) custom-call(f32[16,96,384]{2,1,0:T(8,128)} %phi.5, f32[16,96,384]{2,1,0:T(8,128)} %src.5), custom_call_target="tpu_custom_call" | custom-call | tf_op jit(solution)/shard_map/far_face/pallas_call | solution.py:203
  3.5 3.0 %collective-permute-start.3 = (f32[3,392,128]{2,1,0:T(8,128)}, f32[3,392,128]{2,1,0:T(8,128)S(1)}, u32[]{:S(2)}, u32[]{:S(2)}) collective-permute-start(f32[3,392,128]{2,1,0:T(8,128)} %get-tuple-element.19.own_b), channel_id=1, source_target_pairs={{0,1},{1,0},{2,4},{3,5},{4,2},{5,3},{6,8},{7,9},{8,6},{9,7},{10,12... | collective-permute-start | bytes 1806344 | tf_op jit(solution)/shard_map/ppermute | solution.py:707
  6.5 0.7 %near_face.1 = (f32[3,385,128]{2,1,0:T(8,128)S(1)}, f32[3,72,128]{2,1,0:T(8,128)S(1)}, f32[3,16,128]{2,1,0:T(8,128)S(1)}) custom-call(f32[3,16,128]{2,1,0:T(8,128)} %get-tuple-element.14.after, f32[16,96,384]{2,1,0:T(8,128)S(1)} %copy-done, f32[16,96,384]{2,1,0:T(8,128)S(1)} %copy-done.1), custom_call_target="tpu_custom_call" | custom-call | flops 1 | bytes 1 | tf_op jit(solution)/shard_map/near_face/pallas_call | solution.py:270
  7.2 0.2 collective-permute-start
  7.4 1.5 %collective-permute-start.4 = (f32[3,16,128]{2,1,0:T(8,128)}, f32[3,16,128]{2,1,0:T(8,128)S(1)}, u32[]{:S(2)}, u32[]{:S(2)}) collective-permute-start(f32[3,16,128]{2,1,0:T(8,128)} %get-tuple-element.14.after), channel_id=1, source_target_pairs={{0,1},{1,0},{2,5},{3,4},{4,3},{5,2},{6,9},{7,8},{8,7},{9,6},{10,13... | collective-permute-start | bytes 73736 | tf_op jit(solution)/shard_map/ppermute | solution.py:709
  8.9 0.5 %collective-permute-start.2 = (f32[3,72,128]{2,1,0:T(8,128)S(1)}, f32[3,72,128]{2,1,0:T(8,128)S(1)}, u32[]{:S(2)}, u32[]{:S(2)}) collective-permute-start(f32[3,72,128]{2,1,0:T(8,128)S(1)} %get-tuple-element.17.own_y), channel_id=1, source_target_pairs={{0,1},{1,0},{2,3},{3,2},{4,5},{5,4},{6,7},{7,6},{8,9},{9,8},{10,11... | collective-permute-start | bytes 331784 | tf_op jit(solution)/shard_map/ppermute | solution.py:710
  9.4 1.9 %collective-permute-start.1 = (f32[3,16,128]{2,1,0:T(8,128)S(1)}, f32[3,16,128]{2,1,0:T(8,128)S(1)}, u32[]{:S(2)}, u32[]{:S(2)}) collective-permute-start(f32[3,16,128]{2,1,0:T(8,128)S(1)} %get-tuple-element.16), channel_id=1, source_target_pairs={{0,3},{1,2},{2,1},{3,0},{4,7},{5,6},{6,5},{7,4},{8,11},{9,10},{10,... | collective-permute-start | bytes 73736 | tf_op jit(solution)/shard_map/ppermute | solution.py:711
  11.4 0.0 copy-start.4
  11.4 0.9 %copy-done.4 = s32[24576]{0:T(1024)S(1)} copy-done((s32[24576]{0:T(1024)S(1)}, s32[24576]{0:T(1024)}, u32[]{:S(2)}) %copy-start.4) | copy-done | bytes 98328
  12.3 8.1 %alone.1 = (f32[3,1536,128]{2,1,0:T(8,128)S(1)}, f32[96,12288]{1,0:T(8,128)S(1)}, bf16[192,12288]{1,0:T(8,128)(2,1)S(1)}) custom-call(f32[16,96,384]{2,1,0:T(8,128)S(1)} %copy-done, f32[16,96,384]{2,1,0:T(8,128)S(1)} %copy-done.1, f32[96,12288]{1,0:T(8,128)S(1)} %copy-done.2, s32[192,128]{1,0:T(8,128)S(1)} %bitcast.5), custom_call_target="tpu_custom_call" | custom-call | flops 1 | bytes 1 | tf_op jit(solution)/shard_map/alone/pallas_call | solution.py:339
  20.4 0.0 collective-permute-done.1.got_d.got_da
  20.4 0.0 collective-permute-done.2.got_y
  20.4 0.0 copy-start.3
  20.4 1.0 %near_join.1.block = f32[3,1536,128]{2,1,0:T(8,128)S(1)} custom-call(f32[3,385,128]{2,1,0:T(8,128)S(1)} %get-tuple-element.15.own, f32[3,385,128]{2,1,0:T(8,128)S(1)} %collective-permute-done.got.got_a, f32[3,16,128]{2,1,0:T(8,128)S(1)} %collective-permute-done.1.got_d.got_da, f32[3,72,128]{2,1,0:T(8,128)S(1)} %collective-permute-done.2.got_y, ...), custom_call_target="tpu_custom_call" | custom-call | tf_op jit(solution)/shard_map/near_join/pallas_call | solution.py:478
  21.4 0.0 copy-start.5
  21.5 0.0 collective-permute-done.4.got_db
  21.5 0.0 collective-permute-done.3.got_b
  21.5 0.0 copy-done.3
  21.5 3.0 %join.1 = (f32[16,96,384]{2,1,0:T(8,128)}, f32[32,1,768]{2,1,0:T(1,128)S(1)}) custom-call(s32[768]{0:T(1024)S(1)} %get-tuple-element.27.row_of, s32[6,128]{1,0:T(8,128)S(1)} %get-tuple-element.26.lane_of, f32[3,1536,128]{2,1,0:T(8,128)S(1)} %near_join.1.block, f32[3,392,128]{2,1,0:T(8,128)S(1)} %copy-done.3, f32[3,72,128]{2,1,0:T(8,128)S(1)} %get-tuple-element.17.own_y, ...), custom_call_target="tpu_custom_call" | custom-call | tf_op jit(solution)/shard_map/join/pallas_call | solution.py:593
  24.5 12.9 %all_to_all.5.table_ref = f32[32,1,768]{2,1,0:T(1,128)S(1)} all-to-all(f32[32,1,768]{2,1,0:T(1,128)S(1)} %get-tuple-element.21), channel_id=1, replica_groups=mesh['rows'=16,'cols'=2] {'rows','cols'}, dimensions={0} | all-to-all | bytes 196608 | tf_op jit(solution)/shard_map/all_to_all | solution.py:722
  37.4 2.1 %window.1 = (f32[1,128]{1,0:T(1,128)S(1)}, f32[1,128]{1,0:T(1,128)S(1)}) custom-call(f32[32,1,768]{2,1,0:T(1,128)S(1)} %all_to_all.5.table_ref, s32[192,128]{1,0:T(8,128)S(1)} %bitcast.6, f32[96,12288]{1,0:T(8,128)S(1)} %get-tuple-element.22.matrix_ref, bf16[192,12288]{1,0:T(8,128)(2,1)S(1)} %get-tuple-element.23.hot_ref), custom_call_target="tpu_custom_call" | custom-call | tf_op jit(solution)/shard_map/window/pallas_call | solution.py:671
  39.4 0.4 %collective-permute-start.5 = (f32[1,128]{1,0:T(1,128)S(1)}, f32[1,128]{1,0:T(1,128)S(1)}, u32[]{:S(2)}, u32[]{:S(2)}) collective-permute-start(f32[1,128]{1,0:T(1,128)S(1)} %get-tuple-element.25), channel_id=1, source_target_pairs={{0,1},{1,0},{2,3},{3,2},{4,5},{5,4},{6,7},{7,6},{8,9},{9,8},{10,11... | collective-permute-start | bytes 1544 | tf_op jit(solution)/shard_map/ppermute | solution.py:724
  39.9 3.2 %collective-permute-done.5 = f32[1,128]{1,0:T(1,128)S(1)} collective-permute-done((f32[1,128]{1,0:T(1,128)S(1)}, f32[1,128]{1,0:T(1,128)S(1)}, u32[]{:S(2)}, u32[]{:S(2)}) %collective-permute-start.5) | collective-permute-done | bytes 544 | tf_op jit(solution)/shard_map/ppermute | solution.py:724
  43.0 0.5 %slice_bitcast_fusion = f32[48]{0:T(128)} fusion(f32[1,128]{1,0:T(1,128)S(1)} %add.21), kind=kLoop, calls=%fused_computation.16 | loop fusion | bytes 384 | tf_op jit(solution)/shard_map/squeeze | solution.py:726
  (12 shorter events, 0.0 us)
Async XLA Ops:
  0.6 5.9 %copy-start = (f32[16,96,384]{2,1,0:T(8,128)S(1)}, f32[16,96,384]{2,1,0:T(8,128)}, u32[]{:S(2)}) copy-start(f32[16,96,384]{2,1,0:T(8,128)} %phi.5) | copy-start | bytes 7077892
  0.6 5.8 %copy-start.1 = (f32[16,96,384]{2,1,0:T(8,128)S(1)}, f32[16,96,384]{2,1,0:T(8,128)}, u32[]{:S(2)}) copy-start(f32[16,96,384]{2,1,0:T(8,128)} %src.5) | copy-start | bytes 7077892
  3.5 18.0 %collective-permute-start.3 = (f32[3,392,128]{2,1,0:T(8,128)}, f32[3,392,128]{2,1,0:T(8,128)S(1)}, u32[]{:S(2)}, u32[]{:S(2)}) collective-permute-start(f32[3,392,128]{2,1,0:T(8,128)} %get-tuple-element.19.own_b), channel_id=1, source_target_pairs={{0,1},{1,0},{2,4},{3,5},{4,2},{5,3},{6,8},{7,9},{8,6},{9,7},{10,12... | collective-permute-start | bytes 1806344 | tf_op jit(solution)/shard_map/ppermute | solution.py:707
  6.5 4.8 %copy-start.6 = (s32[768]{0:T(1024)S(1)}, s32[768]{0:T(1024)}, u32[]{:S(2)}) copy-start(s32[768]{0:T(1024)} %param.7) | copy-start | bytes 9220
  6.5 4.9 %copy-start.2 = (f32[96,12288]{1,0:T(8,128)S(1)}, f32[96,12288]{1,0:T(8,128)}, u32[]{:S(2)}) copy-start(f32[96,12288]{1,0:T(8,128)} %matrix.1) | copy-start | bytes 14155780
  7.2 13.2 %collective-permute-start = (f32[3,385,128]{2,1,0:T(8,128)S(1)}, f32[3,385,128]{2,1,0:T(8,128)S(1)}, u32[]{:S(2)}, u32[]{:S(2)}) collective-permute-start(f32[3,385,128]{2,1,0:T(8,128)S(1)} %get-tuple-element.15.own), channel_id=1, source_target_pairs={{0,2},{2,0},{4,6},{6,4},{8,10},{10,8},{12,14},{14,12},{16,18},{18,... | collective-permute-start | bytes 1774088 | tf_op jit(solution)/shard_map/ppermute | solution.py:712
  7.4 14.0 %collective-permute-start.4 = (f32[3,16,128]{2,1,0:T(8,128)}, f32[3,16,128]{2,1,0:T(8,128)S(1)}, u32[]{:S(2)}, u32[]{:S(2)}) collective-permute-start(f32[3,16,128]{2,1,0:T(8,128)} %get-tuple-element.14.after), channel_id=1, source_target_pairs={{0,1},{1,0},{2,5},{3,4},{4,3},{5,2},{6,9},{7,8},{8,7},{9,6},{10,13... | collective-permute-start | bytes 73736 | tf_op jit(solution)/shard_map/ppermute | solution.py:709
  8.9 11.5 %collective-permute-start.2 = (f32[3,72,128]{2,1,0:T(8,128)S(1)}, f32[3,72,128]{2,1,0:T(8,128)S(1)}, u32[]{:S(2)}, u32[]{:S(2)}) collective-permute-start(f32[3,72,128]{2,1,0:T(8,128)S(1)} %get-tuple-element.17.own_y), channel_id=1, source_target_pairs={{0,1},{1,0},{2,3},{3,2},{4,5},{5,4},{6,7},{7,6},{8,9},{9,8},{10,11... | collective-permute-start | bytes 331784 | tf_op jit(solution)/shard_map/ppermute | solution.py:710
  9.4 11.0 %collective-permute-start.1 = (f32[3,16,128]{2,1,0:T(8,128)S(1)}, f32[3,16,128]{2,1,0:T(8,128)S(1)}, u32[]{:S(2)}, u32[]{:S(2)}) collective-permute-start(f32[3,16,128]{2,1,0:T(8,128)S(1)} %get-tuple-element.16), channel_id=1, source_target_pairs={{0,3},{1,2},{2,1},{3,0},{4,7},{5,6},{6,5},{7,4},{8,11},{9,10},{10,... | collective-permute-start | bytes 73736 | tf_op jit(solution)/shard_map/ppermute | solution.py:711
  11.4 0.9 %copy-start.4 = (s32[24576]{0:T(1024)S(1)}, s32[24576]{0:T(1024)}, u32[]{:S(2)}) copy-start(s32[24576]{0:T(1024)} %param.8) | copy-start | bytes 294916
  20.4 1.1 %copy-start.3 = (f32[3,392,128]{2,1,0:T(8,128)S(1)}, f32[3,392,128]{2,1,0:T(8,128)}, u32[]{:S(2)}) copy-start(f32[3,392,128]{2,1,0:T(8,128)} %get-tuple-element.19.own_b) | copy-start | bytes 1806340
  21.4 15.9 %copy-start.5 = (s32[24576]{0:T(1024)S(1)}, s32[24576]{0:T(1024)}, u32[]{:S(2)}) copy-start(s32[24576]{0:T(1024)} %param.8) | copy-start | bytes 294916
  39.4 3.6 %collective-permute-start.5 = (f32[1,128]{1,0:T(1,128)S(1)}, f32[1,128]{1,0:T(1,128)S(1)}, u32[]{:S(2)}, u32[]{:S(2)}) collective-permute-start(f32[1,128]{1,0:T(1,128)S(1)} %get-tuple-element.25), channel_id=1, source_target_pairs={{0,1},{1,0},{2,3},{3,2},{4,5},{5,4},{6,7},{7,6},{8,9},{9,8},{10,11... | collective-permute-start | bytes 1544 | tf_op jit(solution)/shard_map/ppermute | solution.py:724
